TPU v7x, 768 devices: a whole 4x8x12 slice. The times are simulated.
768 devices in a mesh: dp: 64 (over y, z_hi, core), tensor: 12 (over z_lo, x).
Axes of the slice: x: 4, y: 8, z: 12 (z_hi: 4, z_lo: 3; z = z_hi * 3 + z_lo), core: 2. Of those that a mesh axis runs over, the one named last changes fastest.
Arguments:
- inputs: bfloat16 [12288, 1536], P('dp'), may hold values from -25 to 25
- w_query: bfloat16 [1536, 3072], P('dp', 'tensor'), may hold values from -1 to 1
- w_keyval: bfloat16 [1536, 1536], P('dp', 'tensor'), may hold values from -1 to 1
- sinks: float32 [48], P('tensor'), may hold values from -1 to 3
- segments: int32 [12288], replicated, may hold values from 0 to 63, never falling along the last dimension, each value on 1 to 384 neighbouring positions
- upstream: bfloat16 [12288, 3072], P('dp', 'tensor'), may hold values from -6 to 6
Outputs:
- attended: bfloat16 [12288, 3072], P('dp', 'tensor')
- grad_inputs: float32 [12288, 1536], P('dp', 'tensor')
- grad_query: float32 [1536, 3072], P('dp', 'tensor')
- grad_keyval: float32 [1536, 1536], P('dp', 'tensor')
Inputs may be any that keep to these rules, and one draw needn't show every extreme that they name: `segments`: document numbers never fall along the tokens; each document has at most 384 tokens and one has exactly that many.
All inputs are finite; a program needn't handle non-finite values.
Results may differ from a plain program's by a relative error of at most 0.018.
Values may be sent and summed in bfloat16 or wider, within the bound.
No kernel may reach another device: no remote copies, remote signals or barrier semaphores. Data moves between devices by JAX's collectives and lax.ppermute only.
A program may use at most 32 MiB of HBM per device.

v0:
```python
import jax
import jax.numpy as jnp
from jax import lax
from jax.sharding import PartitionSpec as P

WINDOW = 128


def from_behind(value, axis, steps):
    count = lax.axis_size(axis)
    leading, last = (max(0, -steps), min(count, count - steps))
    return lax.ppermute(value, axis, [(source, source + steps) for source in range(leading, last)])


def attend(query, keys, values, query_seg, key_seg, sinks, upstream):
    count_q = query.shape[0]
    count_k = keys.shape[0]
    head_dim = keys.shape[1]
    scale = head_dim ** (-0.5)
    scores = jnp.einsum("qhe,ke->hqk", query, keys, preferred_element_type=jnp.float32) * scale
    offset = jnp.arange(count_q)[:, None] + WINDOW - jnp.arange(count_k)[None, :]
    allowed = (query_seg[:, None] == key_seg[None, :]) & (offset >= 0) & (offset < WINDOW)
    masked = jnp.where(allowed[None], scores, -1e30)
    top = jnp.maximum(jnp.max(masked, axis=-1), sinks[:, None])
    expo = jnp.where(allowed[None], jnp.exp(masked - top[..., None]), 0.0)
    total = jnp.sum(expo, axis=-1) + jnp.exp(sinks[:, None] - top)
    probs = expo / total[..., None]
    probs_b = probs.astype(jnp.bfloat16)
    attended = jnp.einsum(
        "hqk,ke->qhe", probs_b, values, preferred_element_type=jnp.float32
    ).astype(jnp.bfloat16)
    dprob = jnp.einsum("qhe,ke->hqk", upstream, values, preferred_element_type=jnp.float32)
    delta = jnp.sum(probs * dprob, axis=-1)
    dscore = (probs * (dprob - delta[..., None])).astype(jnp.bfloat16)
    grad_q = (
        jnp.einsum("hqk,ke->qhe", dscore, keys, preferred_element_type=jnp.float32) * scale
    ).astype(jnp.bfloat16)
    grad_k = jnp.einsum("hqk,qhe->ke", dscore, query, preferred_element_type=jnp.float32) * scale
    grad_v = jnp.einsum("hqk,qhe->ke", probs_b, upstream, preferred_element_type=jnp.float32)
    return (attended, grad_q, jnp.concatenate([grad_k, grad_v], axis=1))


def body(inputs, w_query, w_keyval, sinks, segments, upstream):
    tokens = inputs.shape[0]
    head_count = sinks.shape[0]
    head_dim = w_keyval.shape[1] // 2
    device = lax.axis_index("dp")
    full_q, full_kv = (
        lax.all_gather(w_query, "dp", axis=0, tiled=True),
        lax.all_gather(w_keyval, "dp", axis=0, tiled=True),
    )
    query = jnp.dot(inputs, full_q, preferred_element_type=jnp.float32).astype(jnp.bfloat16)
    keyval = jnp.dot(inputs, full_kv, preferred_element_type=jnp.float32).astype(jnp.bfloat16)
    prior = from_behind(keyval[tokens - WINDOW :], "dp", 1)
    key_rows = jnp.concatenate([prior, keyval], axis=0)
    seg_padded = jnp.concatenate([jnp.full((WINDOW,), -1, jnp.int32), segments], axis=0)
    query_seg = lax.dynamic_slice_in_dim(seg_padded, device * tokens + WINDOW, tokens, 0)
    key_seg = lax.dynamic_slice_in_dim(seg_padded, device * tokens, tokens + WINDOW, 0)
    heads_q = query.reshape(tokens, head_count, head_dim)
    heads_up = upstream.reshape(tokens, head_count, head_dim)
    attended, grad_q, grad_kv = attend(
        heads_q, key_rows[:, :head_dim], key_rows[:, head_dim:], query_seg, key_seg, sinks, heads_up
    )
    attended = attended.reshape(tokens, head_count * head_dim)
    grad_q = grad_q.reshape(tokens, head_count * head_dim)
    owed = from_behind(grad_kv[:WINDOW].astype(jnp.bfloat16), "dp", -1).astype(jnp.float32)
    own_kv = grad_kv[WINDOW:].at[tokens - WINDOW :].add(owed).astype(jnp.bfloat16)
    contract_cols = (((1,), (1,)), ((), ()))
    partial_inputs = lax.dot_general(
        grad_q, full_q, contract_cols, preferred_element_type=jnp.float32
    )
    partial_inputs = partial_inputs + lax.dot_general(
        own_kv, full_kv, contract_cols, preferred_element_type=jnp.float32
    )
    grad_inputs = lax.psum_scatter(
        partial_inputs.astype(jnp.bfloat16), "tensor", scatter_dimension=1, tiled=True
    ).astype(jnp.float32)
    combined = jnp.concatenate([grad_q, own_kv], axis=1)
    contract_rows = (((0,), (0,)), ((), ()))
    whole_term = lax.dot_general(
        inputs, combined, contract_rows, preferred_element_type=jnp.float32
    )
    grads = lax.psum_scatter(whole_term, "dp", scatter_dimension=0, tiled=True)
    split_at = head_count * head_dim
    return (attended, grad_inputs, grads[:, :split_at], grads[:, split_at:])


def solution(mesh):
    return jax.shard_map(
        body,
        mesh=mesh,
        in_specs=(
            P("dp", None),
            P("dp", "tensor"),
            P("dp", "tensor"),
            P("tensor"),
            P(),
            P("dp", "tensor"),
        ),
        out_specs=(P("dp", "tensor"), P("dp", "tensor"), P("dp", "tensor"), P("dp", "tensor")),
        check_vma=False,
    )
```

profile of v0, /device:TPU:38, one launch (start us, length us, event | category | flops | bytes accessed | tf_op | source)
XLA Modules:
  0.0 845.5 jit_solution(9546882175217601250)
XLA Ops:
  8.0 0.0 copy-start
  8.0 0.0 copy-start.3
  8.0 0.0 reduce-scatter.5.cloned.1.call-start
  8.1 97.3 %all_gather.6 = bf16[1536,128]{1,0:T(8,128)(2,1)S(1)} all-gather(bf16[24,128]{1,0:T(8,128)(2,1)} %param.10), channel_id=1, replica_groups=mesh['dp'=64,'tensor'=12] {'dp'}, dimensions={0}, use_global_device_ids=true | all-gather | bytes 399360 | tf_op jit(solution)/shard_map/all_gather | solution.py:50
  105.4 0.0 copy-done
  105.4 0.3 convolution_convert_fusion.2
  105.7 0.0 copy-start.1
  105.7 2.3 collective-permute-start
  108.0 0.0 copy-done.3
  108.0 0.0 copy-start.2
  108.0 85.6 %all_gather.7 = bf16[1536,256]{1,0:T(8,128)(2,1)S(1)} all-gather(bf16[24,256]{1,0:T(8,128)(2,1)S(1)} %copy-done.3), channel_id=1, replica_groups=mesh['dp'=64,'tensor'=12] {'dp'}, dimensions={0}, use_global_device_ids=true | all-gather | bytes 798720 | tf_op jit(solution)/shard_map/all_gather | solution.py:49
  193.6 0.3 convolution_convert_fusion.1
  193.9 0.0 copy-start.4
  193.9 0.0 copy-done.1
  193.9 0.1 pad_dynamic-slice_fusion.1
  194.0 0.1 pad_dynamic-slice_fusion
  194.1 0.2 fusion.12
  194.3 0.1 copy.30
  194.4 0.0 copy-done.2
  194.4 0.1 copy.33
  194.5 0.0 collective-permute-done
  194.5 0.6 fusion.30
  195.1 0.0 copy-done.4
  195.1 0.1 broadcast_maximum_fusion
  195.2 0.5 fusion.6
  195.7 0.1 exponential_add_fusion
  195.8 0.5 convolution_bitcast_fusion.2
  196.3 0.7 multiply_reduce_fusion
  197.0 0.4 multiply_convert_fusion
  197.4 0.3 fusion.4
  197.7 0.4 fusion.3
  198.1 1.4 fusion.31
  199.6 6.7 collective-permute-start.1
  206.3 1.6 collective-permute-done.1
  207.9 0.1 fusion.19
  208.0 0.4 scatter-add.4
  208.4 1.6 fusion
  210.0 1.2 copy.47
  211.2 0.0 reduce-scatter.5.cloned.1.call-update
  211.2 0.0 all-reduce.4.cloned.1.call-start
  211.3 1.9 convolution_bitcast_fusion
  213.1 0.0 all-reduce.4.cloned.1.call-update
  213.2 1.3 dynamic-slice.8
  215.1 0.7 convolution_convert_fusion
  215.8 0.7 copy.36
  216.5 54.6 %reduce-scatter.5.cloned.1.call-done = bf16[128,192]{1,0:T(8,128)(2,1)} async-done(((bf16[1536,192]{1,0:T(8,128)(2,1)}), bf16[128,192]{1,0:T(8,128)(2,1)}) %reduce-scatter.5.cloned.1.call-update) | async-done | bytes 49168
  271.1 0.9 copy.48
  272.1 0.7 convert_element_type.48
  272.7 561.9 %all-reduce.4.cloned.1.call-done = f32[1536,384]{0,1:T(8,128)} async-done(((f32[1536,384]{0,1:T(8,128)}), f32[1536,384]{0,1:T(8,128)}) %all-reduce.4.cloned.1.call-update) | async-done | bytes 2359312
  834.6 1.0 constant_dynamic-slice_fusion
  835.7 0.7 copy.37
  836.4 1.0 dynamic-slice.11
  837.3 0.7 copy.38
  (3 shorter events, 0.0 us)
Async XLA Ops:
  8.0 97.4 %copy-start = (bf16[192,1536]{1,0:T(8,128)(2,1)S(1)}, bf16[192,1536]{1,0:T(8,128)(2,1)}, u32[]{:S(2)}) copy-start(bf16[192,1536]{1,0:T(8,128)(2,1)} %param.8) | copy-start | bytes 1769476
  8.0 99.9 %copy-start.3 = (bf16[24,256]{1,0:T(8,128)(2,1)S(1)}, bf16[24,256]{1,0:T(8,128)(2,1)}, u32[]{:S(2)}) copy-start(bf16[24,256]{1,0:T(8,128)(2,1)} %param.9) | copy-start | bytes 36868
  8.0 263.1 %reduce-scatter.5.cloned.1.call-start = ((), (), s32[]{:S(2)}) async-start(), calls=%async_computation.1 | async-start | bytes 851968
  105.7 88.3 %copy-start.1 = (s32[12288]{0:T(1024)S(1)}, s32[12288]{0:T(1024)}, u32[]{:S(2)}) copy-start(s32[12288]{0:T(1024)} %param.12) | copy-start | bytes 147460
  105.7 88.8 %collective-permute-start = (bf16[128,128]{1,0:T(8,128)(2,1)S(1)}, bf16[128,128]{1,0:T(8,128)(2,1)S(1)}, u32[]{:S(2)}, u32[]{:S(2)}) collective-permute-start(bf16[128,128]{1,0:T(8,128)(2,1)S(1)} %slice.50), channel_id=1, source_target_pairs={{0,12},{12,24},{24,36},{36,48},{48,60},{60,72},{72,84},{84,96},{96... | collective-permute-start | bytes 98312 | tf_op jit(solution)/shard_map/ppermute | solution.py:12
  108.0 86.4 %copy-start.2 = (bf16[192,256]{1,0:T(8,128)(2,1)S(1)}, bf16[192,256]{1,0:T(8,128)(2,1)}, u32[]{:S(2)}) copy-start(bf16[192,256]{1,0:T(8,128)(2,1)} %param.13) | copy-start | bytes 294916
  193.9 1.2 copy-start.4
  199.6 8.3 collective-permute-start.1
  211.2 623.4 %all-reduce.4.cloned.1.call-start = ((), (), s32[]{:S(2)}) async-start(), calls=%async_computation.2 | async-start | bytes 4718592
Sparse Core Ops, SparseCore 0:
  211.3 59.7 reduce-scatter.4
Sparse Core Ops, SparseCore 1:
  214.9 619.7 all-reduce.3
where the time goes:
time: 846 us; the launch traced here: 845 us
  waiting for transfers between devices  618 us (73%)
  blocking collectives  183 us (22%)
  between operations  16.3 us (2%)
  starting transfers between devices  9.05 us (1%)
  matrix products  8.76 us (1%)
    unnamed x4, waiting for transfers between devices  617 us
    all_gather x1, blocking collectives, body(): lax.all_gather(w_keyval, 'dp', axis=0, tiled=True)  97.3 us
    all_gather x1, blocking collectives, body(): lax.all_gather(w_query, 'dp', axis=0, tiled=True)  85.6 us
  transfers between devices with their start and end apart: 4, of which 3 were waited for; matrix products, arithmetic and copies ran while one was open for 1% of the time, Pallas kernels for 0%

commit v1 on v0

v1 whole, which is shorter than its diff:
```python
import jax
import jax.numpy as jnp
from jax import lax
from jax.sharding import Mesh, PartitionSpec as P

WINDOW = 128
DP = ("y", "zh", "core")
TENSOR = ("zl", "x")
FAR = ("y", "zh")
SWAP = [(0, 1), (1, 0)]


def from_behind(value, axis, steps):
    count = lax.axis_size(axis)
    leading, last = (max(0, -steps), min(count, count - steps))
    return lax.ppermute(value, axis, [(source, source + steps) for source in range(leading, last)])


def exchange(value, axes):
    return lax.all_to_all(value, axes, split_axis=0, concat_axis=0, tiled=True)


def attend(query, keys, values, query_seg, key_seg, sinks, upstream):
    count_q = query.shape[0]
    count_k = keys.shape[0]
    head_dim = keys.shape[1]
    scale = head_dim ** (-0.5)
    scores = jnp.einsum("qhe,ke->hqk", query, keys, preferred_element_type=jnp.float32) * scale
    offset = jnp.arange(count_q)[:, None] + WINDOW - jnp.arange(count_k)[None, :]
    allowed = (query_seg[:, None] == key_seg[None, :]) & (offset >= 0) & (offset < WINDOW)
    masked = jnp.where(allowed[None], scores, -1e30)
    top = jnp.maximum(jnp.max(masked, axis=-1), sinks[:, None])
    expo = jnp.where(allowed[None], jnp.exp(masked - top[..., None]), 0.0)
    total = jnp.sum(expo, axis=-1) + jnp.exp(sinks[:, None] - top)
    probs = expo / total[..., None]
    probs_b = probs.astype(jnp.bfloat16)
    attended = jnp.einsum(
        "hqk,ke->qhe", probs_b, values, preferred_element_type=jnp.float32
    ).astype(jnp.bfloat16)
    dprob = jnp.einsum("qhe,ke->hqk", upstream, values, preferred_element_type=jnp.float32)
    delta = jnp.sum(probs * dprob, axis=-1)
    dscore = (probs * (dprob - delta[..., None])).astype(jnp.bfloat16)
    grad_q = (
        jnp.einsum("hqk,ke->qhe", dscore, keys, preferred_element_type=jnp.float32) * scale
    ).astype(jnp.bfloat16)
    grad_k = jnp.einsum("hqk,qhe->ke", dscore, query, preferred_element_type=jnp.float32) * scale
    grad_v = jnp.einsum("hqk,qhe->ke", probs_b, upstream, preferred_element_type=jnp.float32)
    return (attended, grad_q, jnp.concatenate([grad_k, grad_v], axis=1))


def body(inputs, w_query, w_keyval, sinks, segments, upstream):
    tokens, width = inputs.shape
    head_count = sinks.shape[0]
    head_dim = w_keyval.shape[1] // 2
    split_at = head_count * head_dim
    rows = w_query.shape[0]
    device = lax.axis_index(DP)
    core = lax.axis_index("core")
    far = lax.axis_size(FAR)
    parts = lax.axis_size(TENSOR)

    shard = jnp.concatenate([w_query, w_keyval], axis=1)
    columns = shard.shape[1]
    copies = lax.optimization_barrier(jnp.broadcast_to(shard[None], (far, rows, columns)))
    mine = exchange(copies, FAR)
    other = lax.ppermute(mine, "core", SWAP)
    weights = jnp.stack(
        [jnp.where(core == 0, mine, other), jnp.where(core == 0, other, mine)], axis=1
    ).reshape(width, columns)

    projected = jnp.dot(inputs, weights, preferred_element_type=jnp.float32).astype(jnp.bfloat16)
    query, keyval = projected[:, :split_at], projected[:, split_at:]
    prior = from_behind(keyval[tokens - WINDOW :], DP, 1)
    key_rows = jnp.concatenate([prior, keyval], axis=0)
    seg_padded = jnp.concatenate([jnp.full((WINDOW,), -1, jnp.int32), segments], axis=0)
    query_seg = lax.dynamic_slice_in_dim(seg_padded, device * tokens + WINDOW, tokens, 0)
    key_seg = lax.dynamic_slice_in_dim(seg_padded, device * tokens, tokens + WINDOW, 0)
    heads_q = query.reshape(tokens, head_count, head_dim)
    heads_up = upstream.reshape(tokens, head_count, head_dim)
    attended, grad_q, grad_kv = attend(
        heads_q, key_rows[:, :head_dim], key_rows[:, head_dim:], query_seg, key_seg, sinks, heads_up
    )
    attended = attended.reshape(tokens, split_at)
    grad_q = grad_q.reshape(tokens, split_at)
    owed = from_behind(grad_kv[:WINDOW].astype(jnp.bfloat16), DP, -1).astype(jnp.float32)
    own_kv = grad_kv[WINDOW:] + jnp.concatenate(
        [jnp.zeros((tokens - WINDOW, 2 * head_dim), jnp.float32), owed], axis=0
    )
    combined = jnp.concatenate([grad_q, own_kv.astype(jnp.bfloat16)], axis=1)

    whole_term = lax.dot_general(
        inputs, combined, (((0,), (0,)), ((), ())), preferred_element_type=jnp.float32
    ).astype(jnp.bfloat16).reshape(far, 2, rows, columns)
    theirs = lax.dynamic_index_in_dim(whole_term, 1 - core, 1, keepdims=False)
    ours = lax.dynamic_index_in_dim(whole_term, core, 1, keepdims=False)
    theirs = lax.ppermute(theirs, "core", SWAP)
    pair = (ours.astype(jnp.float32) + theirs.astype(jnp.float32)).astype(jnp.bfloat16)
    grads = jnp.sum(exchange(pair, FAR).astype(jnp.float32), axis=0)

    terms = jnp.einsum(
        "tk,pnk->ptn",
        combined,
        weights.reshape(parts, width // parts, columns),
        preferred_element_type=jnp.float32,
    ).astype(jnp.bfloat16)
    grad_inputs = jnp.sum(exchange(terms, TENSOR).astype(jnp.float32), axis=0)
    return (attended, grad_inputs, grads[:, :split_at], grads[:, split_at:])


def solution(mesh):
    fine = Mesh(mesh.devices.reshape(8, 4, 2, 3, 4), (*DP, *TENSOR))
    return jax.shard_map(
        body,
        mesh=fine,
        in_specs=(
            P(DP, None),
            P(DP, TENSOR),
            P(DP, TENSOR),
            P(TENSOR),
            P(),
            P(DP, TENSOR),
        ),
        out_specs=(P(DP, TENSOR), P(DP, TENSOR), P(DP, TENSOR), P(DP, TENSOR)),
        check_vma=False,
    )
```

time: 846 us -> 129 us (0.15)
  the two profiles are of different devices: /device:TPU:38 before, /device:TPU:138 now
where the time goes in v1:
time: 129 us; the launch traced here: 128 us
  blocking collectives  47.2 us (37%)
  waiting for transfers between devices  39.8 us (31%)
  starting transfers between devices  22.9 us (18%)
  matrix products  6.57 us (5%)
  local copies, waits for them, and re-layouts  5.82 us (5%)
  other arithmetic  5.31 us (4%)
    all_to_all x1, blocking collectives, exchange(): return lax.all_to_all(value, axes, split_axis=0, concat_axis=0, tiled=True)  47.2 us
    all_to_all x2, waiting for transfers between devices, exchange(): return lax.all_to_all(value, axes, split_axis=0, concat_axis=0, tiled=True)  28.6 us
    all_to_all x2, starting transfers between devices, exchange(): return lax.all_to_all(value, axes, split_axis=0, concat_axis=0, tiled=True)  15.2 us
    ppermute x2, waiting for transfers between devices, from_behind(): lax.ppermute(value, axis, [(source, source + steps) for source in range(l...  7.04 us
    ppermute x2, starting transfers between devices, from_behind(): lax.ppermute(value, axis, [(source, source + steps) for source in range(l...  3.96 us
  transfers between devices with their start and end apart: 6, of which 6 were waited for; matrix products, arithmetic and copies ran while one was open for 8% of the time, Pallas kernels for 0%

profile of v1, /device:TPU:138, one launch (start us, length us, event | category | flops | bytes accessed | tf_op | source)
XLA Modules:
  0.0 128.5 jit_solution(9846753298046502425)
XLA Ops:
  0.6 0.0 copy-start
  0.6 0.0 copy-start.5
  0.7 0.8 pad_maximum_fusion.6
  1.5 0.1 broadcast_in_dim.20
  1.5 47.2 %all_to_all.15 = bf16[32,24,384]{2,1,0:T(8,128)(2,1)S(1)} all-to-all(bf16[32,24,384]{2,1,0:T(8,128)(2,1)S(1)} %broadcast_in_dim.20), channel_id=1, replica_groups=mesh['y'=8,'zh'=4,'core'=2,'zl'=3,'x'=4] {'y','zh'}, dimensions={0} | all-to-all | bytes 1179648 | tf_op jit(solution)/shard_map/all_to_all | solution.py:20
  48.7 1.9 %collective-permute-start = (bf16[32,24,384]{2,1,0:T(8,128)(2,1)S(1)}, bf16[32,24,384]{2,1,0:T(8,128)(2,1)S(1)}, u32[]{:S(2)}, u32[]{:S(2)}) collective-permute-start(bf16[32,24,384]{2,1,0:T(8,128)(2,1)S(1)} %all_to_all.15), channel_id=1, source_target_pairs={{0,12},{12,0},{1,13},{13,1},{2,14},{14,2},{3,15},{15,3},{4,16},{16... | collective-permute-start | bytes 1769480 | tf_op jit(solution)/shard_map/ppermute | solution.py:66
  50.6 0.0 copy-done.5
  50.6 0.1 pad_dynamic-slice_fusion
  50.7 0.1 pad_dynamic-slice_fusion.1
  50.8 1.8 %collective-permute-done = bf16[32,24,384]{2,1,0:T(8,128)(2,1)S(1)} collective-permute-done((bf16[32,24,384]{2,1,0:T(8,128)(2,1)S(1)}, bf16[32,24,384]{2,1,0:T(8,128)(2,1)S(1)}, u32[]{:S(2)}, u32[]{:S(2)}) %collective-permute-start) | collective-permute-done | bytes 589856 | tf_op jit(solution)/shard_map/ppermute | solution.py:66
  52.6 0.1 select_bitcast_fusion.1
  52.7 0.1 pad_maximum_fusion
  52.8 0.0 copy-start.10
  52.9 0.0 copy-done
  52.9 0.5 fusion.6
  53.3 0.0 copy-start.11
  53.4 2.0 %collective-permute-start.1 = (bf16[128,128]{1,0:T(8,128)(2,1)S(1)}, bf16[128,128]{1,0:T(8,128)(2,1)S(1)}, u32[]{:S(2)}, u32[]{:S(2)}) collective-permute-start(bf16[128,128]{1,0:T(8,128)(2,1)S(1)} %slice.38), channel_id=1, source_target_pairs={{0,12},{12,24},{24,36},{36,48},{48,60},{60,72},{72,84},{84,96},{96... | collective-permute-start | bytes 98312 | tf_op jit(solution)/shard_map/ppermute | solution.py:16
  55.4 0.2 fusion.15
  55.6 0.0 copy-done.10
  55.6 0.0 copy-start.1
  55.6 0.8 copy.26
  56.4 0.1 copy.23
  56.5 6.0 %collective-permute-done.1 = bf16[128,128]{1,0:T(8,128)(2,1)S(1)} collective-permute-done((bf16[128,128]{1,0:T(8,128)(2,1)S(1)}, bf16[128,128]{1,0:T(8,128)(2,1)S(1)}, u32[]{:S(2)}, u32[]{:S(2)}) %collective-permute-start.1) | collective-permute-done | bytes 32800 | tf_op jit(solution)/shard_map/ppermute | solution.py:16
  62.5 0.6 fusion.32
  63.1 0.0 copy-done.11
  63.1 0.1 broadcast_maximum_fusion
  63.2 0.5 fusion.9
  63.7 0.1 exponential_add_fusion
  63.7 0.0 copy-done.9
  63.7 0.5 convolution_bitcast_fusion.1
  64.3 0.0 copy-done.6
  64.3 0.7 multiply_reduce_fusion
  65.0 0.0 copy-done.1
  65.0 0.0 copy-start.7
  65.0 0.4 multiply_convert_fusion
  65.4 0.3 fusion.7
  65.7 1.9 %collective-permute-start.2 = (bf16[128,128]{0,1:T(8,128)(2,1)S(1)}, bf16[128,128]{0,1:T(8,128)(2,1)S(1)}, u32[]{:S(2)}, u32[]{:S(2)}) collective-permute-start(bf16[128,128]{0,1:T(8,128)(2,1)S(1)} %fusion.21), channel_id=1, source_target_pairs={{12,0},{24,12},{36,24},{48,36},{60,48},{72,60},{84,72},{96,84},{10... | collective-permute-start | bytes 98312 | tf_op jit(solution)/shard_map/ppermute | solution.py:16
  67.6 0.0 copy-done.3
  67.6 0.0 copy-done.7
  67.6 0.4 fusion.5
  68.0 0.1 copy.29
  68.2 1.0 collective-permute-done.2
  69.2 0.1 fusion.19
  69.3 0.1 copy.30
  69.4 1.4 %fusion.3 = bf16[12,192,128]{2,1,0:T(8,128)(2,1)} fusion(bf16[12,128,384]{2,1,0:T(8,128)(2,1)S(1)} %bitcast.68, bf16[192,128]{1,0:T(8,128)(2,1)S(1)} %copy.30, bf16[192,256]{1,0:T(8,128)(2,1)S(1)} %copy.29), kind=kOutput, calls=%fused_computation.7 | convolution fusion | flops 227082240 | bytes 1916928 | tf_op jit(solution)/shard_map/tk,pnk->ptn/dot_general | solution.py:100
  70.8 6.6 %all-to-all-start.1 = ((bf16[12,192,128]{2,1,0:T(8,128)(2,1)}), bf16[12,192,128]{2,1,0:T(8,128)(2,1)S(1)}, u32[]{:S(2)}, u32[]{:S(2)}) async-start(bf16[12,192,128]{2,1,0:T(8,128)(2,1)} %fusion.3), calls=%async_computation.1 | async-start | bytes 1179648 | tf_op jit(solution)/shard_map/all_to_all | solution.py:20
  77.5 1.5 %fusion = bf16[1536,384]{0,1:T(8,128)(2,1)} fusion(bf16[192,1536]{1,0:T(8,128)(2,1)S(1)} %copy-done, bf16[192,128]{1,0:T(8,128)(2,1)S(1)} %copy.30, bf16[192,256]{1,0:T(8,128)(2,1)S(1)} %copy.29), kind=kOutput, calls=%fused_computation.1 | convolution fusion | flops 227377152 | bytes 1916928 | tf_op jit(solution)/shard_map/dot_general | solution.py:91
  79.0 1.7 %copy.31 = bf16[1536,384]{1,0:T(8,128)(2,1)S(1)} copy(bf16[1536,384]{0,1:T(8,128)(2,1)} %fusion) | data formatting | bytes 2359296 | tf_op jit(solution)/shard_map/convert_element_type | solution.py:93
  80.7 0.9 dynamic-slice_bitcast_fusion
  81.6 1.9 %collective-permute-start.3 = (bf16[32,24,384]{2,1,0:T(8,128)(2,1)}, bf16[32,24,384]{2,1,0:T(8,128)(2,1)}, u32[]{:S(2)}, u32[]{:S(2)}) collective-permute-start(bf16[32,24,384]{2,1,0:T(8,128)(2,1)} %dynamic-slice_bitcast_fusion), channel_id=1, source_target_pairs={{0,12},{12,0},{1,13},{13,1},{2,14},{14,2},{3,15},{15,3},{4,16},{16... | collective-permute-start | bytes 1769480 | tf_op jit(solution)/shard_map/ppermute | solution.py:96
  83.5 2.3 %collective-permute-done.3 = bf16[32,24,384]{2,1,0:T(8,128)(2,1)} collective-permute-done((bf16[32,24,384]{2,1,0:T(8,128)(2,1)}, bf16[32,24,384]{2,1,0:T(8,128)(2,1)}, u32[]{:S(2)}, u32[]{:S(2)}) %collective-permute-start.3) | collective-permute-done | bytes 589856 | tf_op jit(solution)/shard_map/ppermute | solution.py:96
  85.8 2.0 %fusion.4 = bf16[32,24,384]{2,1,0:T(8,128)(2,1)} fusion(bf16[32,24,384]{2,1,0:T(8,128)(2,1)} %collective-permute-done.3, bf16[32,2,24,384]{3,2,1,0:T(8,128)(2,1)S(1)} %bitcast.70, s32[]{:T(128)S(6)} %select_n.39), kind=kLoop, calls=%fused_computation.10 | loop fusion | flops 1179648 | bytes 1769476 | tf_op jit(solution)/shard_map/convert_element_type | solution.py:97
  87.8 0.4 all-to-all-done.1
  88.2 8.5 %all-to-all-start.2 = ((bf16[32,24,384]{2,1,0:T(8,128)(2,1)}), bf16[32,24,384]{2,1,0:T(8,128)(2,1)S(1)}, u32[]{:S(2)}, u32[]{:S(2)}) async-start(bf16[32,24,384]{2,1,0:T(8,128)(2,1)} %fusion.4), calls=%async_computation.2 | async-start | bytes 1179648 | tf_op jit(solution)/shard_map/all_to_all | solution.py:20
  96.7 0.0 copy-done.2
  96.7 0.0 copy-done.4
  96.8 0.0 copy-done.8
  96.8 0.7 convolution_convert_fusion.3
  97.5 0.8 copy.32
  98.2 0.7 convert_reduce_fusion.1
  98.9 28.3 %all-to-all-done.2 = bf16[32,24,384]{2,1,0:T(8,128)(2,1)S(1)} async-done(((bf16[32,24,384]{2,1,0:T(8,128)(2,1)}), bf16[32,24,384]{2,1,0:T(8,128)(2,1)S(1)}, u32[]{:S(2)}, u32[]{:S(2)}) %all-to-all-start.2) | async-done | bytes 589856 | tf_op jit(solution)/shard_map/all_to_all | solution.py:20
  127.2 0.1 convert_reduce_fusion
  127.3 0.6 slice.46
  127.9 0.6 slice.45
  (10 shorter events, 0.0 us)
Async XLA Ops:
  0.6 52.2 %copy-start = (bf16[192,1536]{1,0:T(8,128)(2,1)S(1)}, bf16[192,1536]{1,0:T(8,128)(2,1)}, u32[]{:S(2)}) copy-start(bf16[192,1536]{1,0:T(8,128)(2,1)} %param.6) | copy-start | bytes 1769476
  0.6 50.0 %copy-start.5 = (s32[12288]{0:T(1024)S(1)}, s32[12288]{0:T(1024)}, u32[]{:S(2)}) copy-start(s32[12288]{0:T(1024)} %param.10) | copy-start | bytes 147460
  48.7 3.9 %collective-permute-start = (bf16[32,24,384]{2,1,0:T(8,128)(2,1)S(1)}, bf16[32,24,384]{2,1,0:T(8,128)(2,1)S(1)}, u32[]{:S(2)}, u32[]{:S(2)}) collective-permute-start(bf16[32,24,384]{2,1,0:T(8,128)(2,1)S(1)} %all_to_all.15), channel_id=1, source_target_pairs={{0,12},{12,0},{1,13},{13,1},{2,14},{14,2},{3,15},{15,3},{4,16},{16... | collective-permute-start | bytes 1769480 | tf_op jit(solution)/shard_map/ppermute | solution.py:66
  52.8 2.8 %copy-start.10 = (bf16[192,256]{1,0:T(8,128)(2,1)S(1)}, bf16[192,256]{1,0:T(8,128)(2,1)}, u32[]{:S(2)}) copy-start(bf16[192,256]{1,0:T(8,128)(2,1)} %param.11) | copy-start | bytes 294916
  53.3 9.8 %copy-start.11 = (f32[4]{0:T(128)S(1)}, f32[4]{0:T(128)}, u32[]{:S(2)}) copy-start(f32[4]{0:T(128)} %param.9) | copy-start | bytes 52
  53.4 9.1 %collective-permute-start.1 = (bf16[128,128]{1,0:T(8,128)(2,1)S(1)}, bf16[128,128]{1,0:T(8,128)(2,1)S(1)}, u32[]{:S(2)}, u32[]{:S(2)}) collective-permute-start(bf16[128,128]{1,0:T(8,128)(2,1)S(1)} %slice.38), channel_id=1, source_target_pairs={{0,12},{12,24},{24,36},{36,48},{48,60},{60,72},{72,84},{84,96},{96... | collective-permute-start | bytes 98312 | tf_op jit(solution)/shard_map/ppermute | solution.py:16
  55.6 9.4 %copy-start.1 = (pred[192,320]{1,0:T(8,128)(4,1)}, pred[192,320]{1,0:T(8,128)(4,1)S(1)}, u32[]{:S(2)}) copy-start(pred[192,320]{1,0:T(8,128)(4,1)S(1)} %fusion.15) | copy-start | bytes 184324
  56.4 11.2 %copy-start.3 = (bf16[192,128]{1,0:T(8,128)(2,1)}, bf16[192,128]{1,0:T(8,128)(2,1)S(1)}, u32[]{:S(2)}) copy-start(bf16[192,128]{1,0:T(8,128)(2,1)S(1)} %slice.39) | copy-start | bytes 147460
  62.5 1.8 %copy-start.6 = (bf16[128,128]{1,0:T(8,128)(2,1)}, bf16[128,128]{1,0:T(8,128)(2,1)S(1)}, u32[]{:S(2)}) copy-start(bf16[128,128]{1,0:T(8,128)(2,1)S(1)} %collective-permute-done.1) | copy-start | bytes 98308
  62.5 1.2 copy-start.9
  65.0 2.7 %copy-start.7 = (bf16[128,128]{1,0:T(8,128)(2,1)S(1)}, bf16[128,128]{1,0:T(8,128)(2,1)}, u32[]{:S(2)}) copy-start(bf16[128,128]{1,0:T(8,128)(2,1)} %copy-done.6) | copy-start | bytes 98308
  65.7 3.5 %collective-permute-start.2 = (bf16[128,128]{0,1:T(8,128)(2,1)S(1)}, bf16[128,128]{0,1:T(8,128)(2,1)S(1)}, u32[]{:S(2)}, u32[]{:S(2)}) collective-permute-start(bf16[128,128]{0,1:T(8,128)(2,1)S(1)} %fusion.21), channel_id=1, source_target_pairs={{12,0},{24,12},{36,24},{48,36},{60,48},{72,60},{84,72},{96,84},{10... | collective-permute-start | bytes 98312 | tf_op jit(solution)/shard_map/ppermute | solution.py:16
  70.8 17.4 %all-to-all-start.1 = ((bf16[12,192,128]{2,1,0:T(8,128)(2,1)}), bf16[12,192,128]{2,1,0:T(8,128)(2,1)S(1)}, u32[]{:S(2)}, u32[]{:S(2)}) async-start(bf16[12,192,128]{2,1,0:T(8,128)(2,1)} %fusion.3), calls=%async_computation.1 | async-start | bytes 1179648 | tf_op jit(solution)/shard_map/all_to_all | solution.py:20
  81.6 4.2 %collective-permute-start.3 = (bf16[32,24,384]{2,1,0:T(8,128)(2,1)}, bf16[32,24,384]{2,1,0:T(8,128)(2,1)}, u32[]{:S(2)}, u32[]{:S(2)}) collective-permute-start(bf16[32,24,384]{2,1,0:T(8,128)(2,1)} %dynamic-slice_bitcast_fusion), channel_id=1, source_target_pairs={{0,12},{12,0},{1,13},{13,1},{2,14},{14,2},{3,15},{15,3},{4,16},{16... | collective-permute-start | bytes 1769480 | tf_op jit(solution)/shard_map/ppermute | solution.py:96
  87.8 8.9 %copy-start.2 = (pred[192,320]{1,0:T(8,128)(4,1)S(1)}, pred[192,320]{1,0:T(8,128)(4,1)}, u32[]{:S(2)}) copy-start(pred[192,320]{1,0:T(8,128)(4,1)} %copy-done.1) | copy-start | bytes 184324
  87.8 8.9 %copy-start.4 = (bf16[192,128]{1,0:T(8,128)(2,1)S(1)}, bf16[192,128]{1,0:T(8,128)(2,1)}, u32[]{:S(2)}) copy-start(bf16[192,128]{1,0:T(8,128)(2,1)} %copy-done.3) | copy-start | bytes 147460
  87.8 8.9 %copy-start.8 = (bf16[128,128]{1,0:T(8,128)(2,1)S(1)}, bf16[128,128]{1,0:T(8,128)(2,1)}, u32[]{:S(2)}) copy-start(bf16[128,128]{1,0:T(8,128)(2,1)} %copy-done.6) | copy-start | bytes 98308
  88.2 39.0 %all-to-all-start.2 = ((bf16[32,24,384]{2,1,0:T(8,128)(2,1)}), bf16[32,24,384]{2,1,0:T(8,128)(2,1)S(1)}, u32[]{:S(2)}, u32[]{:S(2)}) async-start(bf16[32,24,384]{2,1,0:T(8,128)(2,1)} %fusion.4), calls=%async_computation.2 | async-start | bytes 1179648 | tf_op jit(solution)/shard_map/all_to_all | solution.py:20

commit v2 on v1

v2 whole, which is shorter than its diff:
```python
import functools

import jax
import jax.numpy as jnp
from jax import lax
from jax.experimental import pallas as pl
from jax.experimental.pallas import tpu as pltpu
from jax.sharding import Mesh, PartitionSpec as P

WINDOW = 128
TILE = 64
DP = ("y", "zh", "core")
TENSOR = ("zl", "x")
FAR = ("y", "zh")
SWAP = [(0, 1), (1, 0)]
F32 = jnp.float32
BF16 = jnp.bfloat16
VMEM = pl.BlockSpec(memory_space=pltpu.VMEM)
SMEM = pl.BlockSpec(memory_space=pltpu.SMEM)


def exchange(value, axes):
    return lax.all_to_all(value, axes, split_axis=0, concat_axis=0, tiled=True)


def project_kernel(core_ref, mine_ref, theirs_ref, w_ref, own_ref, halo_ref, send_ref):
    tokens, columns = own_ref.shape
    kv = columns - 128
    first = core_ref[0] == 0
    mine = jnp.dot(mine_ref[...], w_ref[...], preferred_element_type=F32)
    theirs = jnp.dot(theirs_ref[...], w_ref[...], preferred_element_type=F32)
    own_ref[...] = mine[WINDOW:]
    halo_ref[...] = jnp.where(first, mine[:WINDOW, kv:], theirs[tokens:, kv:])
    send_ref[:, :columns] = theirs[WINDOW:]
    send_ref[: tokens - WINDOW, columns:] = jnp.zeros((tokens - WINDOW, 128), F32)
    send_ref[tokens - WINDOW :, columns:] = jnp.where(first, mine[tokens:, kv:], theirs[:WINDOW, kv:])


def attend_kernel(own_ref, halo_ref, got_ref, up_ref, bias_ref, sinks_ref, att_ref, pack_ref, acc_ref):
    tokens, columns = own_ref.shape
    wide = up_ref.shape[1]
    heads = wide // 64
    proj = own_ref[...] + got_ref[:, :columns]
    halo = halo_ref[...] + got_ref[tokens - WINDOW :, columns:]
    query = (proj[:, :wide].astype(BF16).astype(F32) * 0.125).astype(BF16)
    keyval = jnp.concatenate([halo, proj[:, wide:]], axis=0)
    flipped = jnp.transpose(keyval).astype(BF16)
    keyval = keyval.astype(BF16)
    upstream = up_ref[...]
    sinks = sinks_ref[...]
    acc_ref[...] = jnp.zeros_like(acc_ref)

    def stack(value, start):
        return jnp.concatenate(
            [value[start : start + TILE, 64 * h : 64 * h + 64] for h in range(heads)], axis=0
        )

    for tile in range(tokens // TILE):
        start = tile * TILE
        span = TILE + WINDOW
        qs, us = stack(query, start), stack(upstream, start)
        block = keyval[start : start + span]
        keys, values = block[:, :64], block[:, 64:]
        contract = (((1,), (1,)), ((), ()))
        score = lax.dot_general(keys, qs, contract, preferred_element_type=F32) + bias_ref[tile]
        top = jnp.maximum(jnp.max(score, axis=0, keepdims=True), sinks)
        expo = jnp.exp(score - top)
        total = jnp.sum(expo, axis=0, keepdims=True) + jnp.exp(sinks - top)
        probs = expo * (1.0 / total)
        probs_b = probs.astype(BF16)
        dprob = lax.dot_general(values, us, contract, preferred_element_type=F32)
        delta = jnp.sum(probs * dprob, axis=0, keepdims=True)
        dscore = (probs * (dprob - delta)).astype(BF16)
        part = flipped[:, start : start + span]
        att_t = jnp.dot(part[64:], probs_b, preferred_element_type=F32)
        dq_t = jnp.dot(part[:64], dscore, preferred_element_type=F32) * 0.125
        both = jnp.transpose(jnp.concatenate([att_t, dq_t], axis=0)).astype(BF16)
        for h in range(heads):
            rows = both[h * TILE : (h + 1) * TILE]
            att_ref[start : start + TILE, 64 * h : 64 * h + 64] = rows[:, :64]
            pack_ref[start : start + TILE, 64 * h : 64 * h + 64] = rows[:, 64:]
        grad_k = jnp.dot(dscore, qs, preferred_element_type=F32)
        grad_v = jnp.dot(probs_b, us, preferred_element_type=F32)
        acc_ref[start : start + span] += jnp.concatenate([grad_k, grad_v], axis=1)
    pack_ref[:, wide:columns] = acc_ref[WINDOW:].astype(BF16)
    pack_ref[: tokens - WINDOW, columns:] = jnp.zeros((tokens - WINDOW, 128), BF16)
    pack_ref[tokens - WINDOW :, columns:] = acc_ref[:WINDOW].astype(BF16)


def weight_grad_kernel(core_ref, mine_ref, theirs_ref, pack_ref, got_ref, out_ref, own_ref):
    columns = out_ref.shape[1]
    tokens = pack_ref.shape[0]
    wide = columns - 128
    first = core_ref[0] == 0
    mine_owed = pack_ref[:, columns:]
    theirs_owed = got_ref[:, columns:]
    none = jnp.zeros(mine_owed.shape, F32)
    mine_kv = pack_ref[:, wide:columns].astype(F32) + jnp.where(first, theirs_owed.astype(F32), none)
    theirs_kv = got_ref[:, wide:columns].astype(F32) + jnp.where(first, none, mine_owed.astype(F32))
    mine_kv = mine_kv.astype(BF16)
    own_ref[...] = mine_kv
    zero = jnp.zeros((WINDOW, wide), BF16)
    grads = jnp.concatenate(
        [
            jnp.concatenate([zero, mine_owed[tokens - WINDOW :]], axis=1),
            jnp.concatenate([pack_ref[:, :wide], mine_kv], axis=1),
            jnp.concatenate([zero, theirs_owed[tokens - WINDOW :]], axis=1),
            jnp.concatenate([got_ref[:, :wide], theirs_kv.astype(BF16)], axis=1),
        ],
        axis=0,
    )
    half = WINDOW + tokens
    out_ref[...] = (
        jnp.dot(mine_ref[...], grads[:half], preferred_element_type=F32)
        + jnp.dot(theirs_ref[...], grads[half:], preferred_element_type=F32)
    ).astype(BF16)


def call(kernel, specs, shapes, *args, scratch=()):
    return pl.pallas_call(
        kernel,
        in_specs=specs,
        out_specs=[VMEM] * len(shapes),
        out_shape=[jax.ShapeDtypeStruct(*s) for s in shapes],
        scratch_shapes=scratch,
    )(*args)


def body(inputs, w_query, w_keyval, sinks, segments, upstream):
    tokens, width = inputs.shape
    heads = sinks.shape[0]
    split_at = w_query.shape[1]
    rows = w_query.shape[0]
    columns = split_at + w_keyval.shape[1]
    device = lax.axis_index(DP)
    core = lax.axis_index("core")
    flag = core.reshape(1).astype(jnp.int32)
    count = lax.axis_size(DP)
    far = lax.axis_size(FAR)
    parts = lax.axis_size(TENSOR)
    half = width // 2

    halo = lax.ppermute(inputs[tokens - WINDOW :], DP, [(i - 1, i) for i in range(2, count, 2)])

    shard = jnp.concatenate([w_query, w_keyval], axis=1)
    copies = lax.optimization_barrier(jnp.broadcast_to(shard[None], (far, rows, columns)))
    weights = exchange(copies, FAR).reshape(half, columns)

    source = lax.broadcasted_iota(jnp.int32, (half, 2, half // 2), 0)
    part = lax.broadcasted_iota(jnp.int32, (half, 2, half // 2), 1)
    target = lax.broadcasted_iota(jnp.int32, (half, 2, half // 2), 2)
    chosen = (source == (target // rows) * (2 * rows) + part * rows + target % rows).astype(BF16)
    extended = jnp.concatenate([halo, inputs], axis=0).reshape(WINDOW + tokens, 2, half)
    sorted_x = jnp.einsum("tkd,dhn->htkn", extended, chosen, preferred_element_type=F32).astype(BF16)
    sorted_x = sorted_x.reshape(2, WINDOW + tokens, half)
    mine_x = lax.dynamic_index_in_dim(sorted_x, core, 0, keepdims=False)
    theirs_x = lax.ppermute(
        lax.dynamic_index_in_dim(sorted_x, 1 - core, 0, keepdims=False), "core", SWAP
    )
    mine_xt, theirs_xt = mine_x.T, theirs_x.T

    seg_padded = jnp.concatenate([jnp.full((WINDOW,), -1, jnp.int32), segments], axis=0)
    query_seg = lax.dynamic_slice_in_dim(seg_padded, device * tokens + WINDOW, tokens, 0)
    key_seg = lax.dynamic_slice_in_dim(seg_padded, device * tokens, tokens + WINDOW, 0)
    offset = jnp.arange(TILE)[None, :] + WINDOW - jnp.arange(TILE + WINDOW)[:, None]
    near = (offset >= 0) & (offset < WINDOW)
    bias = jnp.stack(
        [
            jnp.where(
                near
                & (
                    query_seg[None, s : s + TILE] == key_seg[s : s + TILE + WINDOW, None]
                ),
                0.0,
                -1e30,
            )
            for s in range(0, tokens, TILE)
        ]
    ).astype(F32)
    bias = jnp.tile(bias, (1, 1, heads))
    sink_row = jnp.repeat(sinks, TILE)[None, :]

    own, halo_kv, send = call(
        project_kernel,
        [SMEM, VMEM, VMEM, VMEM],
        [((tokens, columns), F32), ((WINDOW, 128), F32), ((tokens, columns + 128), F32)],
        flag,
        mine_x,
        theirs_x,
        weights,
    )
    got = lax.ppermute(send, "core", SWAP)
    attended, pack = call(
        attend_kernel,
        [VMEM] * 6,
        [((tokens, split_at), BF16), ((tokens, columns + 128), BF16)],
        own,
        halo_kv,
        got,
        upstream,
        bias,
        sink_row,
        scratch=[pltpu.VMEM((WINDOW + tokens, 128), F32)],
    )
    got_pack = lax.ppermute(pack, "core", SWAP)
    term, own_kv = call(
        weight_grad_kernel,
        [SMEM] + [VMEM] * 4,
        [((half, columns), BF16), ((tokens, 128), BF16)],
        flag,
        mine_xt,
        theirs_xt,
        pack,
        got_pack,
    )
    received = exchange(term.reshape(far, rows, columns), FAR)
    grad_query = jnp.sum(received[:, :, :split_at].astype(F32), axis=0)
    grad_keyval = jnp.sum(received[:, :, split_at:].astype(F32), axis=0)

    weights, owed, _ = lax.optimization_barrier((weights, pack[tokens - WINDOW :, columns:], term))
    other = lax.ppermute(weights, "core", SWAP)
    owed = lax.ppermute(owed, DP, [(i, i - 1) for i in range(2, count, 2)])
    tail = (own_kv[tokens - WINDOW :].astype(F32) + owed.astype(F32)).astype(BF16)
    own_kv = jnp.concatenate([own_kv[: tokens - WINDOW], tail], axis=0)
    combined = jnp.concatenate([pack[:, :split_at], own_kv], axis=1)
    pair = (weights.reshape(far, rows, columns), other.reshape(far, rows, columns))
    whole = jnp.stack(
        [jnp.where(core == 0, pair[0], pair[1]), jnp.where(core == 0, pair[1], pair[0])], axis=1
    ).reshape(parts, width // parts, columns)
    terms = jnp.einsum("tk,pnk->ptn", combined, whole, preferred_element_type=F32).astype(BF16)
    grad_inputs = jnp.sum(exchange(terms, TENSOR).astype(F32), axis=0)
    return (attended, grad_inputs, grad_query, grad_keyval)


def solution(mesh):
    fine = Mesh(mesh.devices.reshape(8, 4, 2, 3, 4), (*DP, *TENSOR))
    return jax.shard_map(
        body,
        mesh=fine,
        in_specs=(
            P(DP, None),
            P(DP, TENSOR),
            P(DP, TENSOR),
            P(TENSOR),
            P(),
            P(DP, TENSOR),
        ),
        out_specs=(P(DP, TENSOR), P(DP, TENSOR), P(DP, TENSOR), P(DP, TENSOR)),
        check_vma=False,
    )
```

time: 129 us -> 146 us (1.13)
  the two profiles are of different devices: /device:TPU:138 before, /device:TPU:14 now
where the time goes in v2:
time: 146 us; the launch traced here: 145 us
  starting transfers between devices  82.2 us (56%)
  waiting for transfers between devices  37.9 us (26%)
  Pallas kernels  9.42 us (6%)
  local copies, waits for them, and re-layouts  8.77 us (6%)
  other arithmetic  3.38 us (2%)
  matrix products  2.54 us (2%)
    all_to_all x3, starting transfers between devices, exchange(): return lax.all_to_all(value, axes, split_axis=0, concat_axis=0, tiled=True)  66.3 us
    ppermute x1, waiting for transfers between devices, body(): lax.ppermute(inputs[tokens - WINDOW:], DP, [(i - 1, i) for i in range(2,...  17.8 us
    all_to_all x3, waiting for transfers between devices, exchange(): return lax.all_to_all(value, axes, split_axis=0, concat_axis=0, tiled=True)  14.8 us
    pallas_call x3, Pallas kernels, call(): pl.pallas_call(kernel, in_specs=specs, out_specs=[VMEM] * len(shapes), ou...  9.42 us
    ppermute x1, starting transfers between devices, body(): owed = lax.ppermute(owed, DP, [(i, i - 1) for i in range(2, count, 2)])  6.48 us
    ppermute x1, waiting for transfers between devices, body(): owed = lax.ppermute(owed, DP, [(i, i - 1) for i in range(2, count, 2)])  3.78 us
  transfers between devices with their start and end apart: 9, of which 5 were waited for; matrix products, arithmetic and copies ran while one was open for 7% of the time, Pallas kernels for 0%

profile of v2, /device:TPU:14, one launch (start us, length us, event | category | flops | bytes accessed | tf_op | source)
XLA Modules:
  0.0 145.2 jit_solution(10927271258895063127)
XLA Ops:
  0.6 0.0 copy-start.5
  0.6 0.8 pad_maximum_fusion.3
  1.4 0.9 broadcast_in_dim.16
  2.3 20.4 %all-to-all-start = ((bf16[32,24,384]{2,1,0:T(8,128)(2,1)}), bf16[32,24,384]{2,1,0:T(8,128)(2,1)S(1)}, u32[]{:S(2)}, u32[]{:S(2)}) async-start(bf16[32,24,384]{2,1,0:T(8,128)(2,1)} %broadcast_in_dim.16), calls=%async_computation | async-start | bytes 1179648 | tf_op jit(solution)/shard_map/all_to_all | solution.py:23
  22.7 0.0 copy-done.5
  22.8 1.3 collective-permute-start
  24.1 17.8 %collective-permute-done = bf16[128,1536]{1,0:T(8,128)(2,1)S(1)} collective-permute-done((bf16[128,1536]{1,0:T(8,128)(2,1)S(1)}, bf16[128,1536]{1,0:T(8,128)(2,1)S(1)}, u32[]{:S(2)}, u32[]{:S(2)}) %collective-permute-start) | collective-permute-done | bytes 393248 | tf_op jit(solution)/shard_map/ppermute | solution.py:143
  41.9 0.1 pad_maximum_fusion.1
  42.0 1.1 fusion.6
  43.1 0.1 copy.31
  43.2 0.0 copy-start.8
  43.2 0.9 dynamic-slice_bitcast_fusion
  44.1 1.9 %collective-permute-start.1 = (bf16[320,768]{1,0:T(8,128)(2,1)S(1)}, bf16[320,768]{1,0:T(8,128)(2,1)S(1)}, u32[]{:S(2)}, u32[]{:S(2)}) collective-permute-start(bf16[320,768]{1,0:T(8,128)(2,1)S(1)} %get-tuple-element.24), channel_id=1, source_target_pairs={{0,12},{12,0},{1,13},{13,1},{2,14},{14,2},{3,15},{15,3},{4,16},{16... | collective-permute-start | bytes 1474568 | tf_op jit(solution)/shard_map/ppermute | solution.py:157
  46.0 0.0 copy-done.8
  46.0 0.1 pad_dynamic-slice_fusion.1
  46.1 0.1 pad_dynamic-slice_fusion
  46.2 0.1 fusion.34
  46.3 1.6 %collective-permute-done.1.theirs_ref = bf16[320,768]{1,0:T(8,128)(2,1)S(1)} collective-permute-done((bf16[320,768]{1,0:T(8,128)(2,1)S(1)}, bf16[320,768]{1,0:T(8,128)(2,1)S(1)}, u32[]{:S(2)}, u32[]{:S(2)}) %collective-permute-start.1) | collective-permute-done | bytes 491552 | tf_op jit(solution)/shard_map/ppermute | solution.py:157
  47.8 0.0 copy-start.3
  47.8 0.0 all-to-all-done
  47.8 0.0 copy-start
  47.8 0.8 copy-done.3
  48.6 0.2 copy-done
  48.9 2.8 %shard_map.93 = (f32[192,384]{1,0:T(8,128)}, f32[128,128]{1,0:T(8,128)}, f32[192,512]{1,0:T(8,128)}) custom-call(s32[1]{0:T(128)} %bitcast.core_ref, bf16[320,768]{1,0:T(8,128)(2,1)} %bitcast.44, bf16[320,768]{1,0:T(8,128)(2,1)} %copy-done.3, bf16[768,384]{1,0:T(8,128)(2,1)} %bitcast.40), custom_call_target="tpu_custom_call" | custom-call | tf_op jit(solution)/shard_map/pallas_call | solution.py:120
  51.7 2.0 %collective-permute-start.2 = (f32[192,512]{1,0:T(8,128)}, f32[192,512]{1,0:T(8,128)S(1)}, u32[]{:S(2)}, u32[]{:S(2)}) collective-permute-start(f32[192,512]{1,0:T(8,128)} %get-tuple-element.15), channel_id=1, source_target_pairs={{0,12},{12,0},{1,13},{13,1},{2,14},{14,2},{3,15},{15,3},{4,16},{16... | collective-permute-start | bytes 1179656 | tf_op jit(solution)/shard_map/ppermute | solution.py:192
  53.7 0.1 fusion.35
  53.8 0.1 and_select_fusion.2
  53.9 0.0 copy-start.11
  54.0 0.1 tile.4
  54.0 0.0 copy-start.2
  54.0 1.1 copy.25.bias_ref
  55.1 0.0 copy-done.11
  55.1 0.1 broadcast_in_dim.33
  55.2 0.6 broadcast_in_dim_reshape.3.sinks_ref
  55.8 0.0 collective-permute-done.2.got_ref
  55.8 0.0 copy-start.7
  55.8 0.8 copy-done.7
  56.6 3.5 %shard_map.94 = (bf16[192,256]{1,0:T(8,128)(2,1)}, bf16[192,512]{1,0:T(8,128)(2,1)}) custom-call(f32[192,384]{1,0:T(8,128)} %get-tuple-element.13.own_ref, f32[128,128]{1,0:T(8,128)} %get-tuple-element.14.halo_ref, f32[192,512]{1,0:T(8,128)} %copy-done.7, bf16[192,256]{1,0:T(8,128)(2,1)} %up_ref.1, f32[3,192,256]{2,1,0:T(8,128)} %copy.25.bias_ref, ...), custom_call_target="tpu_custom_call" | custom-call | tf_op jit(solution)/shard_map/pallas_call | solution.py:120
  60.1 2.3 %collective-permute-start.3 = (bf16[192,512]{1,0:T(8,128)(2,1)}, bf16[192,512]{1,0:T(8,128)(2,1)S(1)}, u32[]{:S(2)}, u32[]{:S(2)}) collective-permute-start(bf16[192,512]{1,0:T(8,128)(2,1)} %get-tuple-element.17.pack_ref), channel_id=1, source_target_pairs={{0,12},{12,0},{1,13},{13,1},{2,14},{14,2},{3,15},{15,3},{4,16},{16... | collective-permute-start | bytes 589832 | tf_op jit(solution)/shard_map/ppermute | solution.py:205
  62.4 0.0 copy-done.2
  62.4 1.1 copy.23
  63.4 0.0 copy-done.4
  63.4 1.1 copy.26
  64.5 0.0 collective-permute-done.3.got_ref
  64.5 0.7 copy-done.9
  65.2 3.1 %shard_map.95 = (bf16[768,384]{1,0:T(8,128)(2,1)}, bf16[192,128]{1,0:T(8,128)(2,1)}) custom-call(s32[1]{0:T(128)} %bitcast.core_ref, bf16[768,320]{1,0:T(8,128)(2,1)} %bitcast.47, bf16[768,320]{1,0:T(8,128)(2,1)} %bitcast.48, bf16[192,512]{1,0:T(8,128)(2,1)} %get-tuple-element.17.pack_ref, bf16[192,512]{1,0:T(8,128)(2,1)} %copy-done.9), custom_call_target="tpu_custom_call" | custom-call | tf_op jit(solution)/shard_map/pallas_call | solution.py:120
  68.3 27.5 %all-to-all-start.2 = ((bf16[32,24,384]{2,1,0:T(8,128)(2,1)}), bf16[32,24,384]{2,1,0:T(8,128)(2,1)S(1)}, u32[]{:S(2)}, u32[]{:S(2)}) async-start(bf16[32,24,384]{2,1,0:T(8,128)(2,1)} %bitcast.52), calls=%async_computation.2 | async-start | bytes 1179648 | tf_op jit(solution)/shard_map/all_to_all | solution.py:23
  95.8 0.0 copy-done.6
  95.8 0.0 copy-done.1
  95.8 1.9 %collective-permute-start.4 = (bf16[768,384]{1,0:T(8,128)(2,1)S(1)}, bf16[768,384]{1,0:T(8,128)(2,1)S(1)}, u32[]{:S(2)}, u32[]{:S(2)}) collective-permute-start(bf16[768,384]{1,0:T(8,128)(2,1)S(1)} %bitcast.41), channel_id=1, source_target_pairs={{0,12},{12,0},{1,13},{13,1},{2,14},{14,2},{3,15},{15,3},{4,16},{16... | collective-permute-start | bytes 1769480 | tf_op jit(solution)/shard_map/ppermute | solution.py:221
  97.8 6.5 %collective-permute-start.5 = (bf16[128,128]{1,0:T(8,128)(2,1)S(1)}, bf16[128,128]{1,0:T(8,128)(2,1)S(1)}, u32[]{:S(2)}, u32[]{:S(2)}) collective-permute-start(bf16[128,128]{1,0:T(8,128)(2,1)S(1)} %slice.46), channel_id=1, source_target_pairs={{24,12},{48,36},{72,60},{96,84},{120,108},{144,132},{168,156},{192... | collective-permute-start | bytes 98312 | tf_op jit(solution)/shard_map/ppermute | solution.py:222
  104.3 0.0 copy-done.10
  104.3 3.8 %collective-permute-done.5 = bf16[128,128]{1,0:T(8,128)(2,1)S(1)} collective-permute-done((bf16[128,128]{1,0:T(8,128)(2,1)S(1)}, bf16[128,128]{1,0:T(8,128)(2,1)S(1)}, u32[]{:S(2)}, u32[]{:S(2)}) %collective-permute-start.5) | collective-permute-done | bytes 32800 | tf_op jit(solution)/shard_map/ppermute | solution.py:222
  108.1 0.0 collective-permute-done.4
  108.1 0.1 broadcast_select_fusion.1
  108.2 0.1 pad_maximum_fusion
  108.4 0.1 copy.27
  108.5 1.4 fusion.9
  109.9 4.4 %all-to-all-done.2 = bf16[32,24,384]{2,1,0:T(8,128)(2,1)S(1)} async-done(((bf16[32,24,384]{2,1,0:T(8,128)(2,1)}), bf16[32,24,384]{2,1,0:T(8,128)(2,1)S(1)}, u32[]{:S(2)}, u32[]{:S(2)}) %all-to-all-start.2) | async-done | bytes 589856 | tf_op jit(solution)/shard_map/all_to_all | solution.py:23
  114.3 18.4 %all-to-all-start.1 = ((bf16[12,192,128]{2,1,0:T(8,128)(2,1)}), bf16[12,192,128]{2,1,0:T(8,128)(2,1)S(1)}, u32[]{:S(2)}, u32[]{:S(2)}) async-start(bf16[12,192,128]{2,1,0:T(8,128)(2,1)} %fusion.9), calls=%async_computation.1 | async-start | bytes 1179648 | tf_op jit(solution)/shard_map/all_to_all | solution.py:23
  132.7 0.6 convert_reduce_fusion.2
  133.4 0.7 convert_reduce_fusion.1
  134.1 10.4 %all-to-all-done.1 = bf16[12,192,128]{2,1,0:T(8,128)(2,1)S(1)} async-done(((bf16[12,192,128]{2,1,0:T(8,128)(2,1)}), bf16[12,192,128]{2,1,0:T(8,128)(2,1)S(1)}, u32[]{:S(2)}, u32[]{:S(2)}) %all-to-all-start.1) | async-done | bytes 589856 | tf_op jit(solution)/shard_map/all_to_all | solution.py:23
  144.4 0.7 convert_reduce_fusion
  (15 shorter events, 0.1 us)
Async XLA Ops:
  0.6 22.1 %copy-start.5 = (bf16[192,1536]{1,0:T(8,128)(2,1)S(1)}, bf16[192,1536]{1,0:T(8,128)(2,1)}, u32[]{:S(2)}) copy-start(bf16[192,1536]{1,0:T(8,128)(2,1)} %param.6) | copy-start | bytes 1769476
  2.3 45.5 %all-to-all-start = ((bf16[32,24,384]{2,1,0:T(8,128)(2,1)}), bf16[32,24,384]{2,1,0:T(8,128)(2,1)S(1)}, u32[]{:S(2)}, u32[]{:S(2)}) async-start(bf16[32,24,384]{2,1,0:T(8,128)(2,1)} %broadcast_in_dim.16), calls=%async_computation | async-start | bytes 1179648 | tf_op jit(solution)/shard_map/all_to_all | solution.py:23
  22.8 19.1 %collective-permute-start = (bf16[128,1536]{1,0:T(8,128)(2,1)S(1)}, bf16[128,1536]{1,0:T(8,128)(2,1)S(1)}, u32[]{:S(2)}, u32[]{:S(2)}) collective-permute-start(bf16[128,1536]{1,0:T(8,128)(2,1)S(1)} %slice.39), channel_id=1, source_target_pairs={{12,24},{36,48},{60,72},{84,96},{108,120},{132,144},{156,168},{180... | collective-permute-start | bytes 1179656 | tf_op jit(solution)/shard_map/ppermute | solution.py:143
  43.2 2.8 %copy-start.8 = (s32[12288]{0:T(1024)S(1)}, s32[12288]{0:T(1024)}, u32[]{:S(2)}) copy-start(s32[12288]{0:T(1024)} %param.10) | copy-start | bytes 147460
  44.1 3.7 %collective-permute-start.1 = (bf16[320,768]{1,0:T(8,128)(2,1)S(1)}, bf16[320,768]{1,0:T(8,128)(2,1)S(1)}, u32[]{:S(2)}, u32[]{:S(2)}) collective-permute-start(bf16[320,768]{1,0:T(8,128)(2,1)S(1)} %get-tuple-element.24), channel_id=1, source_target_pairs={{0,12},{12,0},{1,13},{13,1},{2,14},{14,2},{3,15},{15,3},{4,16},{16... | collective-permute-start | bytes 1474568 | tf_op jit(solution)/shard_map/ppermute | solution.py:157
  47.8 0.8 copy-start.3
  47.8 1.0 copy-start
  51.7 4.2 %collective-permute-start.2 = (f32[192,512]{1,0:T(8,128)}, f32[192,512]{1,0:T(8,128)S(1)}, u32[]{:S(2)}, u32[]{:S(2)}) collective-permute-start(f32[192,512]{1,0:T(8,128)} %get-tuple-element.15), channel_id=1, source_target_pairs={{0,12},{12,0},{1,13},{13,1},{2,14},{14,2},{3,15},{15,3},{4,16},{16... | collective-permute-start | bytes 1179656 | tf_op jit(solution)/shard_map/ppermute | solution.py:192
  53.9 1.2 copy-start.11
  54.0 8.3 %copy-start.2 = (bf16[1,320,768]{2,1,0:T(8,128)(2,1)S(1)}, bf16[1,320,768]{2,1,0:T(8,128)(2,1)}, u32[]{:S(2)}) copy-start(bf16[1,320,768]{2,1,0:T(8,128)(2,1)} %get-tuple-element.25) | copy-start | bytes 1474564
  55.8 0.8 copy-start.7
  56.6 6.9 %copy-start.4 = (bf16[320,768]{1,0:T(8,128)(2,1)S(1)}, bf16[320,768]{1,0:T(8,128)(2,1)}, u32[]{:S(2)}) copy-start(bf16[320,768]{1,0:T(8,128)(2,1)} %copy-done.3) | copy-start | bytes 1474564
  60.1 4.4 %collective-permute-start.3 = (bf16[192,512]{1,0:T(8,128)(2,1)}, bf16[192,512]{1,0:T(8,128)(2,1)S(1)}, u32[]{:S(2)}, u32[]{:S(2)}) collective-permute-start(bf16[192,512]{1,0:T(8,128)(2,1)} %get-tuple-element.17.pack_ref), channel_id=1, source_target_pairs={{0,12},{12,0},{1,13},{13,1},{2,14},{14,2},{3,15},{15,3},{4,16},{16... | collective-permute-start | bytes 589832 | tf_op jit(solution)/shard_map/ppermute | solution.py:205
  64.5 0.7 copy-start.9
  65.2 30.6 %copy-start.6 = (bf16[192,512]{1,0:T(8,128)(2,1)S(1)}, bf16[192,512]{1,0:T(8,128)(2,1)}, u32[]{:S(2)}) copy-start(bf16[192,512]{1,0:T(8,128)(2,1)} %get-tuple-element.17.pack_ref) | copy-start | bytes 589828
  65.2 30.6 %copy-start.1 = (bf16[32,24,384]{2,1,0:T(8,128)(2,1)S(1)}, bf16[32,24,384]{2,1,0:T(8,128)(2,1)}, u32[]{:S(2)}) copy-start(bf16[32,24,384]{2,1,0:T(8,128)(2,1)} %copy-done) | copy-start | bytes 1769476
  68.3 36.0 %copy-start.10 = (bf16[192,128]{1,0:T(8,128)(2,1)S(1)}, bf16[192,128]{1,0:T(8,128)(2,1)}, u32[]{:S(2)}) copy-start(bf16[192,128]{1,0:T(8,128)(2,1)} %get-tuple-element.20) | copy-start | bytes 147460
  68.3 46.0 %all-to-all-start.2 = ((bf16[32,24,384]{2,1,0:T(8,128)(2,1)}), bf16[32,24,384]{2,1,0:T(8,128)(2,1)S(1)}, u32[]{:S(2)}, u32[]{:S(2)}) async-start(bf16[32,24,384]{2,1,0:T(8,128)(2,1)} %bitcast.52), calls=%async_computation.2 | async-start | bytes 1179648 | tf_op jit(solution)/shard_map/all_to_all | solution.py:23
  95.8 12.3 %collective-permute-start.4 = (bf16[768,384]{1,0:T(8,128)(2,1)S(1)}, bf16[768,384]{1,0:T(8,128)(2,1)S(1)}, u32[]{:S(2)}, u32[]{:S(2)}) collective-permute-start(bf16[768,384]{1,0:T(8,128)(2,1)S(1)} %bitcast.41), channel_id=1, source_target_pairs={{0,12},{12,0},{1,13},{13,1},{2,14},{14,2},{3,15},{15,3},{4,16},{16... | collective-permute-start | bytes 1769480 | tf_op jit(solution)/shard_map/ppermute | solution.py:221
  97.8 10.3 %collective-permute-start.5 = (bf16[128,128]{1,0:T(8,128)(2,1)S(1)}, bf16[128,128]{1,0:T(8,128)(2,1)S(1)}, u32[]{:S(2)}, u32[]{:S(2)}) collective-permute-start(bf16[128,128]{1,0:T(8,128)(2,1)S(1)} %slice.46), channel_id=1, source_target_pairs={{24,12},{48,36},{72,60},{96,84},{120,108},{144,132},{168,156},{192... | collective-permute-start | bytes 98312 | tf_op jit(solution)/shard_map/ppermute | solution.py:222
  114.3 30.1 %all-to-all-start.1 = ((bf16[12,192,128]{2,1,0:T(8,128)(2,1)}), bf16[12,192,128]{2,1,0:T(8,128)(2,1)S(1)}, u32[]{:S(2)}, u32[]{:S(2)}) async-start(bf16[12,192,128]{2,1,0:T(8,128)(2,1)} %fusion.9), calls=%async_computation.1 | async-start | bytes 1179648 | tf_op jit(solution)/shard_map/all_to_all | solution.py:23

commit v3 on v2

--- a/solution.py
+++ b/solution.py
@@ -1,5 +1,3 @@
-import functools
-
 import jax
 import jax.numpy as jnp
 from jax import lax
@@ -7,11 +5,12 @@
 from jax.experimental.pallas import tpu as pltpu
 from jax.sharding import Mesh, PartitionSpec as P
 
+
 WINDOW = 128
 TILE = 64
 DP = ("y", "zh", "core")
 TENSOR = ("zl", "x")
-FAR = ("y", "zh")
+FAR = ("zh", "y")
 SWAP = [(0, 1), (1, 0)]
 F32 = jnp.float32
 BF16 = jnp.bfloat16
@@ -21,6 +20,15 @@
 
 def exchange(value, axes):
     return lax.all_to_all(value, axes, split_axis=0, concat_axis=0, tiled=True)
+
+
+def spread(blocks, axis):
+    size, here = blocks.shape[0], lax.axis_index(axis)
+    got = [lax.dynamic_index_in_dim(blocks, here, 0, keepdims=False)]
+    for step in range(1, size):
+        block = lax.dynamic_index_in_dim(blocks, (here + step) % size, 0, keepdims=False)
+        got.append(lax.ppermute(block, axis, [(i, (i + step) % size) for i in range(size)]))
+    return sum(block.astype(F32) for block in got)
 
 
 def project_kernel(core_ref, mine_ref, theirs_ref, w_ref, own_ref, halo_ref, send_ref):
@@ -117,13 +125,17 @@
 
 
 def call(kernel, specs, shapes, *args, scratch=()):
+    placed = [
+        a if s is SMEM else pltpu.with_memory_space_constraint(a, pltpu.VMEM)
+        for a, s in zip(args, specs)
+    ]
     return pl.pallas_call(
         kernel,
         in_specs=specs,
         out_specs=[VMEM] * len(shapes),
-        out_shape=[jax.ShapeDtypeStruct(*s) for s in shapes],
+        out_shape=[pltpu.VMEM(*s) for s in shapes],
         scratch_shapes=scratch,
-    )(*args)
+    )(*placed)
 
 
 def body(inputs, w_query, w_keyval, sinks, segments, upstream):
@@ -140,34 +152,35 @@
     parts = lax.axis_size(TENSOR)
     half = width // 2
 
-    halo = lax.ppermute(inputs[tokens - WINDOW :], DP, [(i - 1, i) for i in range(2, count, 2)])
+    halo = lax.ppermute(
+        inputs[tokens - WINDOW :], DP, [(i - 1, i) for i in range(2, count, 2)]
+    )
 
     shard = jnp.concatenate([w_query, w_keyval], axis=1)
     copies = lax.optimization_barrier(jnp.broadcast_to(shard[None], (far, rows, columns)))
     weights = exchange(copies, FAR).reshape(half, columns)
 
-    source = lax.broadcasted_iota(jnp.int32, (half, 2, half // 2), 0)
-    part = lax.broadcasted_iota(jnp.int32, (half, 2, half // 2), 1)
-    target = lax.broadcasted_iota(jnp.int32, (half, 2, half // 2), 2)
-    chosen = (source == (target // rows) * (2 * rows) + part * rows + target % rows).astype(BF16)
-    extended = jnp.concatenate([halo, inputs], axis=0).reshape(WINDOW + tokens, 2, half)
-    sorted_x = jnp.einsum("tkd,dhn->htkn", extended, chosen, preferred_element_type=F32).astype(BF16)
-    sorted_x = sorted_x.reshape(2, WINDOW + tokens, half)
-    mine_x = lax.dynamic_index_in_dim(sorted_x, core, 0, keepdims=False)
-    theirs_x = lax.ppermute(
-        lax.dynamic_index_in_dim(sorted_x, 1 - core, 0, keepdims=False), "core", SWAP
-    )
+    near, outer = lax.axis_size(FAR[1]), lax.axis_size(FAR[0])
+    target = jnp.arange(width, dtype=jnp.int32)
+    block = target % half // rows
+    wanted = ((block % near * outer + block // near) * 2 + target // half) * rows + target % rows
+    chosen = (jnp.arange(width, dtype=jnp.int32)[:, None] == wanted[None, :]).astype(BF16)
+    extended = jnp.concatenate([halo, inputs], axis=0)
+    sorted_x = jnp.dot(extended, chosen, preferred_element_type=F32).astype(BF16)
+    mine_x = jnp.where(core == 0, sorted_x[:, :half], sorted_x[:, half:])
+    theirs_x = jnp.where(core == 0, sorted_x[:, half:], sorted_x[:, :half])
+    theirs_x = lax.ppermute(theirs_x, "core", SWAP)
     mine_xt, theirs_xt = mine_x.T, theirs_x.T
 
     seg_padded = jnp.concatenate([jnp.full((WINDOW,), -1, jnp.int32), segments], axis=0)
     query_seg = lax.dynamic_slice_in_dim(seg_padded, device * tokens + WINDOW, tokens, 0)
     key_seg = lax.dynamic_slice_in_dim(seg_padded, device * tokens, tokens + WINDOW, 0)
     offset = jnp.arange(TILE)[None, :] + WINDOW - jnp.arange(TILE + WINDOW)[:, None]
-    near = (offset >= 0) & (offset < WINDOW)
+    reach = (offset >= 0) & (offset < WINDOW)
     bias = jnp.stack(
         [
             jnp.where(
-                near
+                reach
                 & (
                     query_seg[None, s : s + TILE] == key_seg[s : s + TILE + WINDOW, None]
                 ),
@@ -180,6 +193,9 @@
     bias = jnp.tile(bias, (1, 1, heads))
     sink_row = jnp.repeat(sinks, TILE)[None, :]
 
+    weights, mine_xt, theirs_xt, bias, sink_row = lax.optimization_barrier(
+        (weights, mine_xt, theirs_xt, bias, sink_row)
+    )
     own, halo_kv, send = call(
         project_kernel,
         [SMEM, VMEM, VMEM, VMEM],
@@ -190,6 +206,7 @@
         weights,
     )
     got = lax.ppermute(send, "core", SWAP)
+    other = lax.ppermute(weights, "core", SWAP)
     attended, pack = call(
         attend_kernel,
         [VMEM] * 6,
@@ -203,6 +220,9 @@
         scratch=[pltpu.VMEM((WINDOW + tokens, 128), F32)],
     )
     got_pack = lax.ppermute(pack, "core", SWAP)
+    owed = lax.ppermute(
+        pack[tokens - WINDOW :, columns:], DP, [(i, i - 1) for i in range(2, count, 2)]
+    )
     term, own_kv = call(
         weight_grad_kernel,
         [SMEM] + [VMEM] * 4,
@@ -217,23 +237,27 @@
     grad_query = jnp.sum(received[:, :, :split_at].astype(F32), axis=0)
     grad_keyval = jnp.sum(received[:, :, split_at:].astype(F32), axis=0)
 
-    weights, owed, _ = lax.optimization_barrier((weights, pack[tokens - WINDOW :, columns:], term))
-    other = lax.ppermute(weights, "core", SWAP)
-    owed = lax.ppermute(owed, DP, [(i, i - 1) for i in range(2, count, 2)])
     tail = (own_kv[tokens - WINDOW :].astype(F32) + owed.astype(F32)).astype(BF16)
     own_kv = jnp.concatenate([own_kv[: tokens - WINDOW], tail], axis=0)
     combined = jnp.concatenate([pack[:, :split_at], own_kv], axis=1)
+    weights, other, combined, _ = lax.optimization_barrier((weights, other, combined, term))
     pair = (weights.reshape(far, rows, columns), other.reshape(far, rows, columns))
     whole = jnp.stack(
         [jnp.where(core == 0, pair[0], pair[1]), jnp.where(core == 0, pair[1], pair[0])], axis=1
-    ).reshape(parts, width // parts, columns)
-    terms = jnp.einsum("tk,pnk->ptn", combined, whole, preferred_element_type=F32).astype(BF16)
-    grad_inputs = jnp.sum(exchange(terms, TENSOR).astype(F32), axis=0)
+    ).reshape(outer, near, 2 * rows, columns)
+    deep, across = (lax.axis_size(axis) for axis in TENSOR)
+    whole = jnp.swapaxes(whole, 0, 1).reshape(deep, across, width // parts, columns)
+    terms = jnp.einsum("tk,zxck->xtzc", combined, whole, preferred_element_type=F32).astype(BF16)
+    terms = terms.reshape(across, tokens, width // across)
+    near_sum = spread(terms, "x")
+    near_sum = jnp.swapaxes(near_sum.astype(BF16).reshape(tokens, deep, width // parts), 0, 1)
+    grad_inputs = spread(near_sum, "zl")
     return (attended, grad_inputs, grad_query, grad_keyval)
 
 
 def solution(mesh):
     fine = Mesh(mesh.devices.reshape(8, 4, 2, 3, 4), (*DP, *TENSOR))
+
     return jax.shard_map(
         body,
         mesh=fine,

time: 146 us -> 113 us (0.77)
  the two profiles are of different devices: /device:TPU:14 before, /device:TPU:8 now
where the time goes in v3:
time: 113 us; the launch traced here: 112 us
  starting transfers between devices  65.5 us (58%)
  waiting for transfers between devices  23.2 us (21%)
  local copies, waits for them, and re-layouts  9.99 us (9%)
  other arithmetic  4.76 us (4%)
  Pallas kernels  4.56 us (4%)
  matrix products  3.26 us (3%)
    all_to_all x2, starting transfers between devices, exchange(): return lax.all_to_all(value, axes, split_axis=0, concat_axis=0, tiled=True)  29.5 us
    ppermute x5, starting transfers between devices, spread(): lax.ppermute(block, axis, [(i, (i + step) % size) for i in range(size)])  17.4 us
    all_to_all x2, waiting for transfers between devices, exchange(): return lax.all_to_all(value, axes, split_axis=0, concat_axis=0, tiled=True)  14.3 us
    ppermute x5, waiting for transfers between devices, spread(): lax.ppermute(block, axis, [(i, (i + step) % size) for i in range(size)])  7.94 us
    ppermute x1, starting transfers between devices, body(): theirs_x = lax.ppermute(theirs_x, 'core', SWAP)  6 us
    ppermute x1, starting transfers between devices, body(): got = lax.ppermute(send, 'core', SWAP)  5.59 us
    pallas_call x3, Pallas kernels, call(): pl.pallas_call(kernel, in_specs=specs, out_specs=[VMEM] * len(shapes), ou...  4.56 us
    unnamed x21, local copies, waits for them, and re-layouts  3.39 us
  transfers between devices with their start and end apart: 13, of which 5 were waited for; matrix products, arithmetic and copies ran while one was open for 11% of the time, Pallas kernels for 3%

profile of v3, /device:TPU:8, one launch (start us, length us, event | category | flops | bytes accessed | tf_op | source)
XLA Modules:
  0.0 112.5 jit_solution(17536496075913404686)
XLA Ops:
  0.6 0.0 copy-start.7
  0.6 0.0 copy-start.8
  0.7 1.0 slice.47
  1.7 0.0 copy-start.6
  1.7 1.4 %collective-permute-start = (bf16[128,1536]{1,0:T(8,128)(2,1)S(1)}, bf16[128,1536]{1,0:T(8,128)(2,1)S(1)}, u32[]{:S(2)}, u32[]{:S(2)}) collective-permute-start(bf16[128,1536]{1,0:T(8,128)(2,1)S(1)} %slice.47), channel_id=1, source_target_pairs={{12,24},{36,48},{60,72},{84,96},{108,120},{132,144},{156,168},{180... | collective-permute-start | bytes 1179656 | tf_op jit(solution)/shard_map/ppermute | solution.py:155
  3.1 0.7 pad_maximum_fusion.2
  3.9 0.9 broadcast_in_dim.16
  4.8 20.4 %all-to-all-start = ((bf16[32,24,384]{2,1,0:T(8,128)(2,1)}), bf16[32,24,384]{2,1,0:T(8,128)(2,1)S(1)}, u32[]{:S(2)}, u32[]{:S(2)}) async-start(bf16[32,24,384]{2,1,0:T(8,128)(2,1)} %broadcast_in_dim.16), calls=%async_computation | async-start | bytes 1179648 | tf_op jit(solution)/shard_map/all_to_all | solution.py:22
  25.2 0.1 pad_dynamic-slice_fusion
  25.3 0.1 broadcast_in_dim.19
  25.3 0.1 broadcast_in_dim_reshape.3.sinks_ref
  25.4 0.1 pad_dynamic-slice_fusion.1
  25.5 0.1 fusion.43
  25.6 0.0 collective-permute-done
  25.6 2.7 %fusion.2 = bf16[320,1536]{0,1:T(8,128)(2,1)S(1)} fusion(s32[1536]{0:T(1024)S(1)} %fusion.26, bf16[192,1536]{1,0:T(8,128)(2,1)S(1)} %copy-done.6, bf16[128,1536]{1,0:T(8,128)(2,1)S(1)} %collective-permute-done), kind=kOutput, calls=%fused_computation.3 | convolution fusion | flops 1514766336 | bytes 1972224 | tf_op jit(solution)/shard_map/dot_general | solution.py:169
  28.3 0.1 broadcast_select_fusion.2
  28.4 0.2 copy.30
  28.7 6.0 %collective-permute-start.1 = (bf16[320,768]{1,0:T(8,128)(2,1)S(1)}, bf16[320,768]{1,0:T(8,128)(2,1)S(1)}, u32[]{:S(2)}, u32[]{:S(2)}) collective-permute-start(bf16[320,768]{1,0:T(8,128)(2,1)S(1)} %copy.30), channel_id=1, source_target_pairs={{0,12},{12,0},{1,13},{13,1},{2,14},{14,2},{3,15},{15,3},{4,16},{16... | collective-permute-start | bytes 1474568 | tf_op jit(solution)/shard_map/ppermute | solution.py:172
  34.7 0.1 fusion.44
  34.8 0.1 and_select_fusion.2
  34.9 0.2 copy.32.mine_ref
  35.1 1.0 collective-permute-done.1.theirs_ref
  36.2 1.1 copy.31
  37.2 14.3 %all-to-all-done = bf16[32,24,384]{2,1,0:T(8,128)(2,1)S(1)} async-done(((bf16[32,24,384]{2,1,0:T(8,128)(2,1)}), bf16[32,24,384]{2,1,0:T(8,128)(2,1)S(1)}, u32[]{:S(2)}, u32[]{:S(2)}) %all-to-all-start) | async-done | bytes 589856 | tf_op jit(solution)/shard_map/all_to_all | solution.py:22
  51.5 1.0 tile.4
  52.5 1.5 %shard_map.93 = (f32[192,384]{1,0:T(8,128)S(1)}, f32[128,128]{1,0:T(8,128)S(1)}, f32[192,512]{1,0:T(8,128)}) custom-call(s32[1]{0:T(128)} %bitcast.core_ref, bf16[320,768]{1,0:T(8,128)(2,1)S(1)} %copy.32.mine_ref, bf16[320,768]{1,0:T(8,128)(2,1)S(1)} %collective-permute-done.1.theirs_ref, bf16[768,384]{1,0:T(8,128)(2,1)S(1)} %bitcast.44), custom_call_target="tpu_custom_call" | custom-call | tf_op jit(solution)/shard_map/pallas_call | solution.py:132
  53.9 0.7 copy-done.3
  54.7 5.6 %collective-permute-start.2 = (f32[192,512]{1,0:T(8,128)}, f32[192,512]{1,0:T(8,128)S(1)}, u32[]{:S(2)}, u32[]{:S(2)}) collective-permute-start(f32[192,512]{1,0:T(8,128)} %get-tuple-element.22), channel_id=1, source_target_pairs={{0,12},{12,0},{1,13},{13,1},{2,14},{14,2},{3,15},{15,3},{4,16},{16... | collective-permute-start | bytes 1179656 | tf_op jit(solution)/shard_map/ppermute | solution.py:208
  60.3 1.9 %collective-permute-start.3 = (bf16[768,384]{1,0:T(8,128)(2,1)S(1)}, bf16[768,384]{1,0:T(8,128)(2,1)}, u32[]{:S(2)}, u32[]{:S(2)}) collective-permute-start(bf16[768,384]{1,0:T(8,128)(2,1)S(1)} %bitcast.45), channel_id=1, source_target_pairs={{0,12},{12,0},{1,13},{13,1},{2,14},{14,2},{3,15},{15,3},{4,16},{16... | collective-permute-start | bytes 1769480 | tf_op jit(solution)/shard_map/ppermute | solution.py:209
  62.2 1.4 %copy.33.bias_ref = f32[3,192,256]{2,1,0:T(8,128)S(1)} copy(f32[3,192,256]{1,2,0:T(8,128)} %bitcast.51) | data formatting | bytes 1179648 | tf_op jit(solution)/shard_map/optimization_barrier | solution.py:196
  63.6 0.0 collective-permute-done.2.got_ref
  63.6 1.4 %shard_map.94 = (bf16[192,256]{1,0:T(8,128)(2,1)S(1)}, bf16[192,512]{1,0:T(8,128)(2,1)S(1)}) custom-call(f32[192,384]{1,0:T(8,128)S(1)} %copy-done.4, f32[128,128]{1,0:T(8,128)S(1)} %get-tuple-element.21.halo_ref, f32[192,512]{1,0:T(8,128)S(1)} %collective-permute-done.2.got_ref, bf16[192,256]{1,0:T(8,128)(2,1)S(1)} %copy-done.5, ...), custom_call_target="tpu_custom_call" | custom-call | tf_op jit(solution)/shard_map/pallas_call | solution.py:132
  65.0 2.4 %collective-permute-start.4 = (bf16[192,512]{1,0:T(8,128)(2,1)S(1)}, bf16[192,512]{1,0:T(8,128)(2,1)S(1)}, u32[]{:S(2)}, u32[]{:S(2)}) collective-permute-start(bf16[192,512]{1,0:T(8,128)(2,1)S(1)} %get-tuple-element.26.pack_ref), channel_id=1, source_target_pairs={{0,12},{12,0},{1,13},{13,1},{2,14},{14,2},{3,15},{15,3},{4,16},{16... | collective-permute-start | bytes 589832 | tf_op jit(solution)/shard_map/ppermute | solution.py:222
  67.4 1.3 %collective-permute-start.5 = (bf16[128,128]{1,0:T(8,128)(2,1)S(1)}, bf16[128,128]{1,0:T(8,128)(2,1)S(1)}, u32[]{:S(2)}, u32[]{:S(2)}) collective-permute-start(bf16[128,128]{1,0:T(8,128)(2,1)S(1)} %slice.59), channel_id=1, source_target_pairs={{24,12},{48,36},{72,60},{96,84},{120,108},{144,132},{168,156},{192... | collective-permute-start | bytes 98312 | tf_op jit(solution)/shard_map/ppermute | solution.py:223
  68.8 0.0 collective-permute-done.4.got_ref
  68.8 1.1 copy-done
  69.9 0.9 copy-done.2
  70.8 1.7 %shard_map.95 = (bf16[768,384]{1,0:T(8,128)(2,1)}, bf16[192,128]{1,0:T(8,128)(2,1)S(1)}) custom-call(s32[1]{0:T(128)} %bitcast.core_ref, bf16[768,320]{1,0:T(8,128)(2,1)S(1)} %bitcast.47, bf16[768,320]{1,0:T(8,128)(2,1)S(1)} %bitcast.48, bf16[192,512]{1,0:T(8,128)(2,1)S(1)} %copy-done.2, bf16[192,512]{1,0:T(8,128)(2,1)S(1)} %collective-permute-done.4.got_ref), custom_call_target="tpu_custom_call" | custom-call | tf_op jit(solution)/shard_map/pallas_call | solution.py:132
  72.5 9.1 %all-to-all-start.1 = ((bf16[32,24,384]{2,1,0:T(8,128)(2,1)}), bf16[32,24,384]{2,1,0:T(8,128)(2,1)S(1)}, u32[]{:S(2)}, u32[]{:S(2)}) async-start(bf16[32,24,384]{2,1,0:T(8,128)(2,1)} %bitcast.20), calls=%async_computation.1 | async-start | bytes 1179648 | tf_op jit(solution)/shard_map/all_to_all | solution.py:22
  81.7 0.0 collective-permute-done.5
  81.7 0.0 collective-permute-done.3
  81.7 1.2 %broadcast_select_fusion.1 = (bf16[768,384]{1,0:T(8,128)(2,1)S(1)}, bf16[768,384]{1,0:T(8,128)(2,1)S(1)}) fusion(bf16[768,384]{1,0:T(8,128)(2,1)S(1)} %bitcast.46, bf16[768,384]{1,0:T(8,128)(2,1)} %collective-permute-done.3, pred[]{:T(512)S(6)} %eq.89), kind=kLoop, calls=%fused_computation.13 | loop fusion | flops 589824 | bytes 2359297 | tf_op jit(solution)/shard_map/jit(_where)/select_n | solution.py:246
  82.9 0.1 pad_maximum_fusion
  83.1 0.1 copy.36
  83.2 0.6 fusion.3
  83.8 0.1 copy.46
  83.9 0.1 dynamic-slice_bitcast_fusion.2
  84.0 3.4 %collective-permute-start.6 = (bf16[192,384]{1,0:T(8,128)(2,1)S(1)}, bf16[192,384]{1,0:T(8,128)(2,1)S(1)}, u32[]{:S(2)}, u32[]{:S(2)}) collective-permute-start(bf16[192,384]{1,0:T(8,128)(2,1)S(1)} %get-tuple-element.38), channel_id=1, source_target_pairs={{0,1},{1,2},{2,3},{3,0},{4,5},{5,6},{6,7},{7,4},{8,9},{9,10},{10,1... | collective-permute-start | bytes 442376 | tf_op jit(solution)/shard_map/ppermute | solution.py:30
  87.4 4.6 %collective-permute-start.7 = (bf16[192,384]{1,0:T(8,128)(2,1)S(1)}, bf16[192,384]{1,0:T(8,128)(2,1)S(1)}, u32[]{:S(2)}, u32[]{:S(2)}) collective-permute-start(bf16[192,384]{1,0:T(8,128)(2,1)S(1)} %get-tuple-element.40), channel_id=1, source_target_pairs={{0,2},{1,3},{2,0},{3,1},{4,6},{5,7},{6,4},{7,5},{8,10},{9,11},{10,... | collective-permute-start | bytes 442376 | tf_op jit(solution)/shard_map/ppermute | solution.py:30
  92.0 3.3 %collective-permute-start.8 = (bf16[192,384]{1,0:T(8,128)(2,1)S(1)}, bf16[192,384]{1,0:T(8,128)(2,1)S(1)}, u32[]{:S(2)}, u32[]{:S(2)}) collective-permute-start(bf16[192,384]{1,0:T(8,128)(2,1)S(1)} %get-tuple-element.39), channel_id=1, source_target_pairs={{0,3},{1,0},{2,1},{3,2},{4,7},{5,4},{6,5},{7,6},{8,11},{9,8},{10,9... | collective-permute-start | bytes 442376 | tf_op jit(solution)/shard_map/ppermute | solution.py:30
  95.4 0.0 collective-permute-done.6
  95.4 0.5 collective-permute-done.7
  95.9 3.1 %collective-permute-done.8 = bf16[192,384]{1,0:T(8,128)(2,1)S(1)} collective-permute-done((bf16[192,384]{1,0:T(8,128)(2,1)S(1)}, bf16[192,384]{1,0:T(8,128)(2,1)S(1)}, u32[]{:S(2)}, u32[]{:S(2)}) %collective-permute-start.8) | collective-permute-done | bytes 147488 | tf_op jit(solution)/shard_map/ppermute | solution.py:30
  99.0 0.1 fusion.9
  99.2 0.3 constant_dynamic-slice_fusion.1
  99.5 4.1 %collective-permute-start.10 = (bf16[192,128]{1,0:T(8,128)(2,1)S(1)}, bf16[192,128]{1,0:T(8,128)(2,1)S(1)}, u32[]{:S(2)}, u32[]{:S(2)}) collective-permute-start(bf16[192,128]{1,0:T(8,128)(2,1)S(1)} %bitcast.57), channel_id=1, source_target_pairs={{0,8},{4,0},{8,4},{1,9},{5,1},{9,5},{2,10},{6,2},{10,6},{3,11},{7,... | collective-permute-start | bytes 147464 | tf_op jit(solution)/shard_map/ppermute | solution.py:30
  103.6 1.9 %collective-permute-start.9 = (bf16[192,128]{1,0:T(8,128)(2,1)S(1)}, bf16[192,128]{1,0:T(8,128)(2,1)S(1)}, u32[]{:S(2)}, u32[]{:S(2)}) collective-permute-start(bf16[192,128]{1,0:T(8,128)(2,1)S(1)} %bitcast.58), channel_id=1, source_target_pairs={{0,4},{4,8},{8,0},{1,5},{5,9},{9,1},{2,6},{6,10},{10,2},{3,7},{7,1... | collective-permute-start | bytes 147464 | tf_op jit(solution)/shard_map/ppermute | solution.py:30
  105.5 0.6 copy.49
  106.2 0.0 collective-permute-done.10
  106.2 4.3 %collective-permute-done.9 = bf16[192,128]{1,0:T(8,128)(2,1)S(1)} collective-permute-done((bf16[192,128]{1,0:T(8,128)(2,1)S(1)}, bf16[192,128]{1,0:T(8,128)(2,1)S(1)}, u32[]{:S(2)}, u32[]{:S(2)}) %collective-permute-start.9) | collective-permute-done | bytes 49184 | tf_op jit(solution)/shard_map/ppermute | solution.py:30
  110.5 0.7 convert_add_fusion.1
  111.2 0.0 all-to-all-done.1
  111.2 0.7 convert_reduce_fusion
  111.8 0.6 convert_reduce_fusion.1
  (22 shorter events, 0.2 us)
Async XLA Ops:
  0.6 24.5 %copy-start.7 = (s32[12288]{0:T(1024)S(1)}, s32[12288]{0:T(1024)}, u32[]{:S(2)}) copy-start(s32[12288]{0:T(1024)} %param.10) | copy-start | bytes 147460
  0.6 24.6 %copy-start.8 = (f32[4]{0:T(128)S(1)}, f32[4]{0:T(128)}, u32[]{:S(2)}) copy-start(f32[4]{0:T(128)} %param.9) | copy-start | bytes 52
  1.7 23.9 %copy-start.6 = (bf16[192,1536]{1,0:T(8,128)(2,1)S(1)}, bf16[192,1536]{1,0:T(8,128)(2,1)}, u32[]{:S(2)}) copy-start(bf16[192,1536]{1,0:T(8,128)(2,1)} %param.6) | copy-start | bytes 1769476
  1.7 23.9 %collective-permute-start = (bf16[128,1536]{1,0:T(8,128)(2,1)S(1)}, bf16[128,1536]{1,0:T(8,128)(2,1)S(1)}, u32[]{:S(2)}, u32[]{:S(2)}) collective-permute-start(bf16[128,1536]{1,0:T(8,128)(2,1)S(1)} %slice.47), channel_id=1, source_target_pairs={{12,24},{36,48},{60,72},{84,96},{108,120},{132,144},{156,168},{180... | collective-permute-start | bytes 1179656 | tf_op jit(solution)/shard_map/ppermute | solution.py:155
  4.8 46.7 %all-to-all-start = ((bf16[32,24,384]{2,1,0:T(8,128)(2,1)}), bf16[32,24,384]{2,1,0:T(8,128)(2,1)S(1)}, u32[]{:S(2)}, u32[]{:S(2)}) async-start(bf16[32,24,384]{2,1,0:T(8,128)(2,1)} %broadcast_in_dim.16), calls=%async_computation | async-start | bytes 1179648 | tf_op jit(solution)/shard_map/all_to_all | solution.py:22
  28.7 7.5 %collective-permute-start.1 = (bf16[320,768]{1,0:T(8,128)(2,1)S(1)}, bf16[320,768]{1,0:T(8,128)(2,1)S(1)}, u32[]{:S(2)}, u32[]{:S(2)}) collective-permute-start(bf16[320,768]{1,0:T(8,128)(2,1)S(1)} %copy.30), channel_id=1, source_target_pairs={{0,12},{12,0},{1,13},{13,1},{2,14},{14,2},{3,15},{15,3},{4,16},{16... | collective-permute-start | bytes 1474568 | tf_op jit(solution)/shard_map/ppermute | solution.py:172
  52.5 11.1 %copy-start.5 = (bf16[192,256]{1,0:T(8,128)(2,1)S(1)}, bf16[192,256]{1,0:T(8,128)(2,1)}, u32[]{:S(2)}) copy-start(bf16[192,256]{1,0:T(8,128)(2,1)} %up_ref.1) | copy-start | bytes 294916
  53.9 0.7 copy-start.3
  54.7 8.9 %copy-start.4 = (f32[192,384]{1,0:T(8,128)S(1)}, f32[192,384]{1,0:T(8,128)}, u32[]{:S(2)}) copy-start(f32[192,384]{1,0:T(8,128)} %copy-done.3) | copy-start | bytes 884740
  54.7 8.9 %collective-permute-start.2 = (f32[192,512]{1,0:T(8,128)}, f32[192,512]{1,0:T(8,128)S(1)}, u32[]{:S(2)}, u32[]{:S(2)}) collective-permute-start(f32[192,512]{1,0:T(8,128)} %get-tuple-element.22), channel_id=1, source_target_pairs={{0,12},{12,0},{1,13},{13,1},{2,14},{14,2},{3,15},{15,3},{4,16},{16... | collective-permute-start | bytes 1179656 | tf_op jit(solution)/shard_map/ppermute | solution.py:208
  60.3 21.5 %collective-permute-start.3 = (bf16[768,384]{1,0:T(8,128)(2,1)S(1)}, bf16[768,384]{1,0:T(8,128)(2,1)}, u32[]{:S(2)}, u32[]{:S(2)}) collective-permute-start(bf16[768,384]{1,0:T(8,128)(2,1)S(1)} %bitcast.45), channel_id=1, source_target_pairs={{0,12},{12,0},{1,13},{13,1},{2,14},{14,2},{3,15},{15,3},{4,16},{16... | collective-permute-start | bytes 1769480 | tf_op jit(solution)/shard_map/ppermute | solution.py:209
  65.0 3.8 %copy-start.1 = (bf16[192,512]{1,0:T(8,128)(2,1)}, bf16[192,512]{1,0:T(8,128)(2,1)S(1)}, u32[]{:S(2)}) copy-start(bf16[192,512]{1,0:T(8,128)(2,1)S(1)} %get-tuple-element.26.pack_ref) | copy-start | bytes 589828
  65.0 3.8 %collective-permute-start.4 = (bf16[192,512]{1,0:T(8,128)(2,1)S(1)}, bf16[192,512]{1,0:T(8,128)(2,1)S(1)}, u32[]{:S(2)}, u32[]{:S(2)}) collective-permute-start(bf16[192,512]{1,0:T(8,128)(2,1)S(1)} %get-tuple-element.26.pack_ref), channel_id=1, source_target_pairs={{0,12},{12,0},{1,13},{13,1},{2,14},{14,2},{3,15},{15,3},{4,16},{16... | collective-permute-start | bytes 589832 | tf_op jit(solution)/shard_map/ppermute | solution.py:222
  67.4 14.2 %collective-permute-start.5 = (bf16[128,128]{1,0:T(8,128)(2,1)S(1)}, bf16[128,128]{1,0:T(8,128)(2,1)S(1)}, u32[]{:S(2)}, u32[]{:S(2)}) collective-permute-start(bf16[128,128]{1,0:T(8,128)(2,1)S(1)} %slice.59), channel_id=1, source_target_pairs={{24,12},{48,36},{72,60},{96,84},{120,108},{144,132},{168,156},{192... | collective-permute-start | bytes 98312 | tf_op jit(solution)/shard_map/ppermute | solution.py:223
  68.8 1.1 copy-start
  69.9 0.9 copy-start.2
  72.5 38.6 %all-to-all-start.1 = ((bf16[32,24,384]{2,1,0:T(8,128)(2,1)}), bf16[32,24,384]{2,1,0:T(8,128)(2,1)S(1)}, u32[]{:S(2)}, u32[]{:S(2)}) async-start(bf16[32,24,384]{2,1,0:T(8,128)(2,1)} %bitcast.20), calls=%async_computation.1 | async-start | bytes 1179648 | tf_op jit(solution)/shard_map/all_to_all | solution.py:22
  84.0 11.5 %collective-permute-start.6 = (bf16[192,384]{1,0:T(8,128)(2,1)S(1)}, bf16[192,384]{1,0:T(8,128)(2,1)S(1)}, u32[]{:S(2)}, u32[]{:S(2)}) collective-permute-start(bf16[192,384]{1,0:T(8,128)(2,1)S(1)} %get-tuple-element.38), channel_id=1, source_target_pairs={{0,1},{1,2},{2,3},{3,0},{4,5},{5,6},{6,7},{7,4},{8,9},{9,10},{10,1... | collective-permute-start | bytes 442376 | tf_op jit(solution)/shard_map/ppermute | solution.py:30
  87.4 8.5 %collective-permute-start.7 = (bf16[192,384]{1,0:T(8,128)(2,1)S(1)}, bf16[192,384]{1,0:T(8,128)(2,1)S(1)}, u32[]{:S(2)}, u32[]{:S(2)}) collective-permute-start(bf16[192,384]{1,0:T(8,128)(2,1)S(1)} %get-tuple-element.40), channel_id=1, source_target_pairs={{0,2},{1,3},{2,0},{3,1},{4,6},{5,7},{6,4},{7,5},{8,10},{9,11},{10,... | collective-permute-start | bytes 442376 | tf_op jit(solution)/shard_map/ppermute | solution.py:30
  92.0 7.0 %collective-permute-start.8 = (bf16[192,384]{1,0:T(8,128)(2,1)S(1)}, bf16[192,384]{1,0:T(8,128)(2,1)S(1)}, u32[]{:S(2)}, u32[]{:S(2)}) collective-permute-start(bf16[192,384]{1,0:T(8,128)(2,1)S(1)} %get-tuple-element.39), channel_id=1, source_target_pairs={{0,3},{1,0},{2,1},{3,2},{4,7},{5,4},{6,5},{7,6},{8,11},{9,8},{10,9... | collective-permute-start | bytes 442376 | tf_op jit(solution)/shard_map/ppermute | solution.py:30
  99.5 6.7 %collective-permute-start.10 = (bf16[192,128]{1,0:T(8,128)(2,1)S(1)}, bf16[192,128]{1,0:T(8,128)(2,1)S(1)}, u32[]{:S(2)}, u32[]{:S(2)}) collective-permute-start(bf16[192,128]{1,0:T(8,128)(2,1)S(1)} %bitcast.57), channel_id=1, source_target_pairs={{0,8},{4,0},{8,4},{1,9},{5,1},{9,5},{2,10},{6,2},{10,6},{3,11},{7,... | collective-permute-start | bytes 147464 | tf_op jit(solution)/shard_map/ppermute | solution.py:30
  103.6 6.9 %collective-permute-start.9 = (bf16[192,128]{1,0:T(8,128)(2,1)S(1)}, bf16[192,128]{1,0:T(8,128)(2,1)S(1)}, u32[]{:S(2)}, u32[]{:S(2)}) collective-permute-start(bf16[192,128]{1,0:T(8,128)(2,1)S(1)} %bitcast.58), channel_id=1, source_target_pairs={{0,4},{4,8},{8,0},{1,5},{5,9},{9,1},{2,6},{6,10},{10,2},{3,7},{7,1... | collective-permute-start | bytes 147464 | tf_op jit(solution)/shard_map/ppermute | solution.py:30

commit v4 on v3

v4 whole, which is shorter than its diff:
```python
import jax
import jax.numpy as jnp
from jax import lax
from jax.experimental import pallas as pl
from jax.experimental.pallas import tpu as pltpu
from jax.sharding import Mesh, PartitionSpec as P


WINDOW = 128
TILE = 64
DP = ("y", "zh", "core")
TENSOR = ("zl", "x")
FAR = ("zh", "y")
SWAP = [(0, 1), (1, 0)]
F32 = jnp.float32
BF16 = jnp.bfloat16
VMEM = pl.BlockSpec(memory_space=pltpu.VMEM)
SMEM = pl.BlockSpec(memory_space=pltpu.SMEM)


def exchange(value, axes):
    return lax.all_to_all(value, axes, split_axis=0, concat_axis=0, tiled=True)


def dot(a, b):
    return jnp.dot(a, b, preferred_element_type=F32)


def mask_kernel(query_ref, key_ref, bias_ref):
    tiles, span, lanes = bias_ref.shape
    key = lax.broadcasted_iota(jnp.int32, (span, TILE), 0)
    offset = lax.broadcasted_iota(jnp.int32, (span, TILE), 1) + WINDOW - key
    reach = (offset >= 0) & (offset < WINDOW)
    for tile in range(tiles):
        start = tile * TILE
        same = query_ref[:, start : start + TILE] == key_ref[start : start + span, :]
        bias = jnp.where(reach & same, 0.0, -1e30).astype(F32)
        bias_ref[tile] = jnp.concatenate([bias] * (lanes // TILE), axis=1)


def project_kernel(core_ref, mine_ref, theirs_ref, w_ref, edge_ref, keep_ref, send_ref):
    tokens, wide = send_ref.shape
    columns = wide - 128
    first = core_ref[0] == 0
    theirs = dot(theirs_ref[...], w_ref[...])
    mine_kv = dot(mine_ref[...], w_ref[:, columns - 128 :])
    send_ref[:, :columns] = theirs
    send_ref[:, columns:] = mine_kv
    theirs_last = theirs[tokens - WINDOW :, columns - 128 :]
    edge_ref[...] = jnp.where(first, theirs_last, mine_kv[tokens - WINDOW :])
    keep_ref[...] = theirs_last


def attend_kernel(
    core_ref, mine_ref, w_ref, got_ref, keep_ref, even_ref, odd_ref, up_ref, bias_ref, sinks_ref,
    att_ref, pack_ref, acc_ref,
):
    tokens, wide = up_ref.shape
    columns = w_ref.shape[1]
    heads = wide // 64
    proj = dot(mine_ref[...], w_ref[...]) + got_ref[:, :columns]
    halo = jnp.where(
        core_ref[0] == 0,
        even_ref[...] + odd_ref[...],
        keep_ref[...] + got_ref[tokens - WINDOW :, columns:],
    )
    query = (proj[:, :wide].astype(BF16).astype(F32) * 0.125).astype(BF16)
    keyval = jnp.concatenate([halo, proj[:, wide:]], axis=0)
    flipped = jnp.transpose(keyval).astype(BF16)
    keyval = keyval.astype(BF16)
    upstream = up_ref[...]
    sinks = sinks_ref[...]
    acc_ref[...] = jnp.zeros_like(acc_ref)

    def stack(value, start):
        return jnp.concatenate(
            [value[start : start + TILE, 64 * h : 64 * h + 64] for h in range(heads)], axis=0
        )

    for tile in range(tokens // TILE):
        start = tile * TILE
        span = TILE + WINDOW
        qs, us = stack(query, start), stack(upstream, start)
        block = keyval[start : start + span]
        keys, values = block[:, :64], block[:, 64:]
        contract = (((1,), (1,)), ((), ()))
        score = lax.dot_general(keys, qs, contract, preferred_element_type=F32) + bias_ref[tile]
        top = jnp.maximum(jnp.max(score, axis=0, keepdims=True), sinks)
        expo = jnp.exp(score - top)
        total = jnp.sum(expo, axis=0, keepdims=True) + jnp.exp(sinks - top)
        probs = expo * (1.0 / total)
        probs_b = probs.astype(BF16)
        dprob = lax.dot_general(values, us, contract, preferred_element_type=F32)
        delta = jnp.sum(probs * dprob, axis=0, keepdims=True)
        dscore = (probs * (dprob - delta)).astype(BF16)
        part = flipped[:, start : start + span]
        att_t = dot(part[64:], probs_b)
        dq_t = dot(part[:64], dscore) * 0.125
        both = jnp.transpose(jnp.concatenate([att_t, dq_t], axis=0)).astype(BF16)
        for h in range(heads):
            rows = both[h * TILE : (h + 1) * TILE]
            att_ref[start : start + TILE, 64 * h : 64 * h + 64] = rows[:, :64]
            pack_ref[start : start + TILE, 64 * h : 64 * h + 64] = rows[:, 64:]
        grads = jnp.concatenate([dot(dscore, qs), dot(probs_b, us)], axis=1)
        acc_ref[start : start + span] += grads
    pack_ref[:, wide:columns] = acc_ref[WINDOW:].astype(BF16)
    pack_ref[: tokens - WINDOW, columns:] = jnp.zeros((tokens - WINDOW, 128), BF16)
    pack_ref[tokens - WINDOW :, columns:] = acc_ref[:WINDOW].astype(BF16)


def weight_grad_kernel(
    place_ref, mine_ref, theirs_ref, pack_ref, got_ref, even_ref, odd_ref, whole_ref,
    out_ref, term_ref,
):
    columns = out_ref.shape[1]
    tokens = pack_ref.shape[0]
    wide = columns - 128
    across, deep = term_ref.shape[0], term_ref.shape[2] // 128
    first = place_ref[0] == 0
    here = place_ref[1]
    none = jnp.zeros((tokens, 128), F32)
    late = even_ref[...].astype(F32) + odd_ref[...].astype(F32)
    late = jnp.concatenate([none[: tokens - WINDOW], late], axis=0)
    mine_kv = pack_ref[:, wide:columns].astype(F32) + jnp.where(
        first, got_ref[:, columns:].astype(F32), late
    )
    theirs_kv = got_ref[:, wide:columns].astype(F32) + jnp.where(
        first, late, pack_ref[:, columns:].astype(F32)
    )
    mine = jnp.concatenate([pack_ref[:, :wide], mine_kv.astype(BF16)], axis=1)
    theirs = jnp.concatenate([got_ref[:, :wide], theirs_kv.astype(BF16)], axis=1)
    for x in range(across):
        slot = (x + across - here) % across
        for z in range(deep):
            rows = whole_ref[128 * (z * across + x) : 128 * (z * across + x + 1), :]
            block = lax.dot_general(
                mine, rows, (((1,), (1,)), ((), ())), preferred_element_type=F32
            )
            term_ref[slot, :, 128 * z : 128 * z + 128] = block.astype(BF16)
    out_ref[...] = (dot(mine_ref[...], mine) + dot(theirs_ref[...], theirs)).astype(BF16)


def call(kernel, specs, shapes, *args, scratch=()):
    placed = [
        a if s is SMEM else pltpu.with_memory_space_constraint(a, pltpu.VMEM)
        for a, s in zip(args, specs)
    ]
    return pl.pallas_call(
        kernel,
        in_specs=specs,
        out_specs=[VMEM] * len(shapes),
        out_shape=[pltpu.VMEM(*s) for s in shapes],
        scratch_shapes=scratch,
        compiler_params=pltpu.CompilerParams(vmem_limit_bytes=16 << 20),
    )(*placed)


def body(inputs, w_query, w_keyval, sinks, segments, upstream):
    tokens, width = inputs.shape
    heads = sinks.shape[0]
    split_at = w_query.shape[1]
    rows = w_query.shape[0]
    columns = split_at + w_keyval.shape[1]
    device = lax.axis_index(DP)
    core = lax.axis_index("core")
    place = jnp.stack([core, lax.axis_index("x")]).astype(jnp.int32)
    count = lax.axis_size(DP)
    far = lax.axis_size(FAR)
    outer, near = (lax.axis_size(axis) for axis in FAR)
    deep, across = (lax.axis_size(axis) for axis in TENSOR)
    half = width // 2
    span = TILE + WINDOW

    shard = jnp.concatenate([w_query, w_keyval], axis=1)
    copies = lax.optimization_barrier(jnp.broadcast_to(shard[None], (far, rows, columns)))
    weights = exchange(copies, FAR).reshape(half, columns)

    target = jnp.arange(width, dtype=jnp.int32)
    block = target % half // rows
    wanted = ((block % near * outer + block // near) * 2 + target // half) * rows + target % rows
    chosen = (jnp.arange(width, dtype=jnp.int32)[:, None] == wanted[None, :]).astype(BF16)
    sorted_x = dot(inputs, chosen).astype(BF16)
    mine_x = jnp.where(core == 0, sorted_x[:, :half], sorted_x[:, half:])
    theirs_x = jnp.where(core == 0, sorted_x[:, half:], sorted_x[:, :half])
    theirs_x = lax.ppermute(theirs_x, "core", SWAP)
    mine_xt, theirs_xt = mine_x.T, theirs_x.T

    seg_padded = jnp.concatenate([jnp.full((WINDOW,), -1, jnp.int32), segments], axis=0)
    query_seg = lax.dynamic_slice_in_dim(seg_padded, device * tokens + WINDOW, tokens, 0)
    key_seg = lax.dynamic_slice_in_dim(seg_padded, device * tokens, tokens + WINDOW, 0)
    (bias,) = call(
        mask_kernel,
        [VMEM] * 2,
        [((tokens // TILE, span, heads * TILE), F32)],
        query_seg[None, :],
        key_seg[:, None],
    )
    sink_row = jnp.repeat(sinks, TILE)[None, :]

    weights, mine_xt, theirs_xt, bias, sink_row, upstream = lax.optimization_barrier(
        (weights, mine_xt, theirs_xt, bias, sink_row, upstream)
    )
    edge, keep, send = call(
        project_kernel,
        [SMEM] + [VMEM] * 3,
        [((WINDOW, 128), F32), ((WINDOW, 128), F32), ((tokens, columns + 128), F32)],
        place,
        mine_x,
        theirs_x,
        weights,
    )
    even = lax.ppermute(edge, DP, [(i, i + 2) for i in range(0, count - 2, 2)])
    odd = lax.ppermute(edge, DP, [(i, i + 1) for i in range(1, count - 2, 2)])
    got = lax.ppermute(send, "core", SWAP)
    other = lax.ppermute(weights, "core", SWAP)
    attended, pack = call(
        attend_kernel,
        [SMEM] + [VMEM] * 9,
        [((tokens, split_at), BF16), ((tokens, columns + 128), BF16)],
        place,
        mine_x,
        weights,
        got,
        keep,
        even,
        odd,
        upstream,
        bias,
        sink_row,
        scratch=[pltpu.VMEM((WINDOW + tokens, 128), F32)],
    )
    owed = pack[tokens - WINDOW :, columns:]
    even = lax.ppermute(owed, DP, [(i, i - 2) for i in range(2, count, 2)])
    odd = lax.ppermute(owed, DP, [(i, i - 1) for i in range(2, count, 2)])
    got_pack = lax.ppermute(pack, "core", SWAP)

    pair = (weights.reshape(far, rows, columns), other.reshape(far, rows, columns))
    whole = jnp.stack(
        [jnp.where(core == 0, pair[0], pair[1]), jnp.where(core == 0, pair[1], pair[0])], axis=1
    ).reshape(outer, near, 2 * rows, columns)
    whole = jnp.swapaxes(whole, 0, 1).reshape(width, columns)

    term, blocks = call(
        weight_grad_kernel,
        [SMEM] + [VMEM] * 7,
        [((half, columns), BF16), ((across, tokens, width // across), BF16)],
        place,
        mine_xt,
        theirs_xt,
        pack,
        got_pack,
        even,
        odd,
        whole,
    )
    got_x = [
        lax.ppermute(blocks[s], "x", [(i, (i + s) % across) for i in range(across)])
        for s in range(1, across)
    ]
    received = exchange(term.reshape(far, rows, columns), FAR)
    sums = sum((g.astype(F32) for g in got_x), blocks[0].astype(F32)).astype(BF16)
    sums = [sums[:, 128 * z : 128 * z + 128] for z in range(deep)]
    depth = lax.axis_index("zl")

    def pick(step):
        return lax.select_n((depth + step) % deep, *sums)

    got_z = [
        lax.ppermute(pick(s), "zl", [(i, (i + s) % deep) for i in range(deep)])
        for s in range(1, deep)
    ]
    grad_inputs = sum((g.astype(F32) for g in got_z), pick(0).astype(F32))
    grad_query = jnp.sum(received[:, :, :split_at].astype(F32), axis=0)
    grad_keyval = jnp.sum(received[:, :, split_at:].astype(F32), axis=0)
    return (attended, grad_inputs, grad_query, grad_keyval)


def solution(mesh):
    fine = Mesh(mesh.devices.reshape(8, 4, 2, 3, 4), (*DP, *TENSOR))

    return jax.shard_map(
        body,
        mesh=fine,
        in_specs=(
            P(DP, None),
            P(DP, TENSOR),
            P(DP, TENSOR),
            P(TENSOR),
            P(),
            P(DP, TENSOR),
        ),
        out_specs=(P(DP, TENSOR), P(DP, TENSOR), P(DP, TENSOR), P(DP, TENSOR)),
        check_vma=False,
    )
```

time: 113 us -> 124 us (1.097)
  the two profiles are of different devices: /device:TPU:8 before, /device:TPU:70 now
where the time goes in v4:
time: 124 us
  starting transfers between devices  66 us (53%)
  waiting for transfers between devices  41.8 us (34%)
  Pallas kernels  5.96 us (5%)
  other arithmetic  4.35 us (4%)
  local copies, waits for them, and re-layouts  2.72 us (2%)
  matrix products  1.91 us (2%)
    all_to_all x2, starting transfers between devices, exchange(): return lax.all_to_all(value, axes, split_axis=0, concat_axis=0, tiled=True)  33.2 us
    all_to_all x2, waiting for transfers between devices, exchange(): return lax.all_to_all(value, axes, split_axis=0, concat_axis=0, tiled=True)  24.5 us
    ppermute x3, starting transfers between devices, body(): lax.ppermute(blocks[s], 'x', [(i, (i + s) % across) for i in range(across)])  9.77 us
    pallas_call x4, Pallas kernels, call(): pl.pallas_call(kernel, in_specs=specs, out_specs=[VMEM] * len(shapes), ou...  5.96 us
    ppermute x2, starting transfers between devices, body(): lax.ppermute(pick(s), 'zl', [(i, (i + s) % deep) for i in range(deep)])  5.84 us
    ppermute x1, waiting for transfers between devices, body(): even = lax.ppermute(owed, DP, [(i, i - 2) for i in range(2, count, 2)])  5.65 us
    ppermute x1, starting transfers between devices, body(): got_pack = lax.ppermute(pack, 'core', SWAP)  5.38 us
    ppermute x3, waiting for transfers between devices, body(): lax.ppermute(blocks[s], 'x', [(i, (i + s) % across) for i in range(across)])  5.17 us
  transfers between devices with their start and end apart: 15, of which 9 were waited for; matrix products, arithmetic and copies ran while one was open for 5% of the time, Pallas kernels for 3%

profile of v4, /device:TPU:70, one launch (start us, length us, event | category | flops | bytes accessed | tf_op | source)
XLA Modules:
  0.0 123.8 jit_solution(10590208531047240158)
XLA Ops:
  0.6 0.0 copy-start
  0.6 0.8 pad_maximum_fusion.1
  1.4 0.9 broadcast_in_dim.8
  2.3 19.3 %all-to-all-start = ((bf16[32,24,384]{2,1,0:T(8,128)(2,1)}), bf16[32,24,384]{2,1,0:T(8,128)(2,1)S(1)}, u32[]{:S(2)}, u32[]{:S(2)}) async-start(bf16[32,24,384]{2,1,0:T(8,128)(2,1)} %broadcast_in_dim.8), calls=%async_computation | async-start | bytes 1179648 | tf_op jit(solution)/shard_map/all_to_all | solution.py:22
  21.6 0.0 copy-done
  21.6 1.9 %fusion.2 = bf16[1536,192]{0,1:T(8,128)(2,1)S(1)} fusion(bf16[192,1536]{1,0:T(8,128)(2,1)S(1)} %copy-done, s32[1536]{0:T(1024)S(1)} %fusion.18), kind=kOutput, calls=%fused_computation.3 | convolution fusion | flops 908623872 | bytes 1185792 | tf_op jit(solution)/shard_map/dot_general | solution.py:26
  23.5 0.0 copy-start.2
  23.6 0.3 copy.22
  23.8 0.0 copy-start.3
  23.8 0.1 broadcast_select_fusion.2
  23.9 1.9 %collective-permute-start = (bf16[192,768]{0,1:T(8,128)(2,1)S(1)}, bf16[192,768]{0,1:T(8,128)(2,1)S(1)}, u32[]{:S(2)}, u32[]{:S(2)}) collective-permute-start(bf16[192,768]{0,1:T(8,128)(2,1)S(1)} %get-tuple-element.32), channel_id=1, source_target_pairs={{0,12},{12,0},{1,13},{13,1},{2,14},{14,2},{3,15},{15,3},{4,16},{16... | collective-permute-start | bytes 884744 | tf_op jit(solution)/shard_map/ppermute | solution.py:185
  25.9 0.0 copy-done.2
  25.9 0.1 pad_dynamic-slice_fusion
  26.0 0.1 broadcast_in_dim.22.key_ref
  26.1 0.0 copy-done.3
  26.1 0.1 broadcast_in_dim.21
  26.1 0.1 broadcast_in_dim_reshape.3.sinks_ref
  26.2 0.1 pad_dynamic-slice_fusion.1
  26.3 0.4 shard_map.93.bias_ref
  26.7 0.8 collective-permute-done
  27.5 22.4 %all-to-all-done = bf16[32,24,384]{2,1,0:T(8,128)(2,1)S(1)} async-done(((bf16[32,24,384]{2,1,0:T(8,128)(2,1)}), bf16[32,24,384]{2,1,0:T(8,128)(2,1)S(1)}, u32[]{:S(2)}, u32[]{:S(2)}) %all-to-all-start) | async-done | bytes 589856 | tf_op jit(solution)/shard_map/all_to_all | solution.py:22
  49.9 1.9 %collective-permute-start.7 = (bf16[768,384]{1,0:T(8,128)(2,1)S(1)}, bf16[768,384]{1,0:T(8,128)(2,1)}, u32[]{:S(2)}, u32[]{:S(2)}) collective-permute-start(bf16[768,384]{1,0:T(8,128)(2,1)S(1)} %bitcast.28), channel_id=1, source_target_pairs={{0,12},{12,0},{1,13},{13,1},{2,14},{14,2},{3,15},{15,3},{4,16},{16... | collective-permute-start | bytes 1769480 | tf_op jit(solution)/shard_map/ppermute | solution.py:215
  51.8 0.0 copy-start.1
  51.8 0.2 copy.26.mine_ref
  52.0 0.1 pad_add_fusion.core_ref.place_ref
  52.1 0.2 copy.25.theirs_ref
  52.2 0.9 shard_map.94
  53.2 2.4 %collective-permute-start.1 = (f32[192,512]{1,0:T(8,128)S(1)}, f32[192,512]{1,0:T(8,128)S(1)}, u32[]{:S(2)}, u32[]{:S(2)}) collective-permute-start(f32[192,512]{1,0:T(8,128)S(1)} %get-tuple-element.18), channel_id=1, source_target_pairs={{0,12},{12,0},{1,13},{13,1},{2,14},{14,2},{3,15},{15,3},{4,16},{16... | collective-permute-start | bytes 1179656 | tf_op jit(solution)/shard_map/ppermute | solution.py:214
  55.6 3.0 %collective-permute-start.2 = (f32[128,128]{1,0:T(8,128)S(1)}, f32[128,128]{1,0:T(8,128)S(1)}, u32[]{:S(2)}, u32[]{:S(2)}) collective-permute-start(f32[128,128]{1,0:T(8,128)S(1)} %get-tuple-element.20), channel_id=1, source_target_pairs={{0,24},{24,48},{48,72},{72,96},{96,120},{120,144},{144,168},{168,1... | collective-permute-start | bytes 196616 | tf_op jit(solution)/shard_map/ppermute | solution.py:212
  58.6 0.7 collective-permute-start.3
  59.3 1.2 collective-permute-done.2.even_ref
  60.5 0.0 collective-permute-done.3.odd_ref
  60.5 0.0 collective-permute-done.1.got_ref
  60.5 0.0 copy-done.1
  60.5 2.2 %shard_map.95 = (bf16[192,256]{1,0:T(8,128)(2,1)S(1)}, bf16[192,512]{1,0:T(8,128)(2,1)S(1)}) custom-call(s32[2]{0:T(128)S(1)} %pad_add_fusion.core_ref.place_ref, bf16[192,768]{1,0:T(8,128)(2,1)S(1)} %copy.26.mine_ref, bf16[768,384]{1,0:T(8,128)(2,1)S(1)} %bitcast.30, f32[192,512]{1,0:T(8,128)S(1)} %collective-permute-done.1.got_ref, ...), custom_call_target="tpu_custom_call" | custom-call | tf_op jit(solution)/shard_map/pallas_call | solution.py:148
  62.7 5.4 %collective-permute-start.4 = (bf16[192,512]{1,0:T(8,128)(2,1)S(1)}, bf16[192,512]{1,0:T(8,128)(2,1)S(1)}, u32[]{:S(2)}, u32[]{:S(2)}) collective-permute-start(bf16[192,512]{1,0:T(8,128)(2,1)S(1)} %get-tuple-element.27.pack_ref), channel_id=1, source_target_pairs={{0,12},{12,0},{1,13},{13,1},{2,14},{14,2},{3,15},{15,3},{4,16},{16... | collective-permute-start | bytes 589832 | tf_op jit(solution)/shard_map/ppermute | solution.py:235
  68.1 1.3 %collective-permute-start.5 = (bf16[128,128]{1,0:T(8,128)(2,1)S(1)}, bf16[128,128]{1,0:T(8,128)(2,1)S(1)}, u32[]{:S(2)}, u32[]{:S(2)}) collective-permute-start(bf16[128,128]{1,0:T(8,128)(2,1)S(1)} %slice.40), channel_id=1, source_target_pairs={{24,0},{48,24},{72,48},{96,72},{120,96},{144,120},{168,144},{192,1... | collective-permute-start | bytes 98312 | tf_op jit(solution)/shard_map/ppermute | solution.py:233
  69.4 0.7 collective-permute-start.6
  70.1 0.0 collective-permute-done.7
  70.1 1.2 broadcast_select_fusion.1
  71.3 0.1 pad_maximum_fusion
  71.4 0.1 copy.29
  71.6 5.6 %collective-permute-done.5.even_ref = bf16[128,128]{1,0:T(8,128)(2,1)S(1)} collective-permute-done((bf16[128,128]{1,0:T(8,128)(2,1)S(1)}, bf16[128,128]{1,0:T(8,128)(2,1)S(1)}, u32[]{:S(2)}, u32[]{:S(2)}) %collective-permute-start.5) | collective-permute-done | bytes 32800 | tf_op jit(solution)/shard_map/ppermute | solution.py:233
  77.2 0.0 collective-permute-done.6.odd_ref
  77.2 0.0 collective-permute-done.4.got_ref
  77.2 2.5 %shard_map.96 = (bf16[768,384]{1,0:T(8,128)(2,1)}, bf16[4,192,384]{2,1,0:T(8,128)(2,1)S(1)}) custom-call(s32[2]{0:T(128)S(1)} %pad_add_fusion.core_ref.place_ref, bf16[768,192]{1,0:T(8,128)(2,1)S(1)} %bitcast.33, bf16[768,192]{1,0:T(8,128)(2,1)S(1)} %bitcast.34, bf16[192,512]{1,0:T(8,128)(2,1)S(1)} %get-tuple-element.27.pack_ref, ...), custom_call_target="tpu_custom_call" | custom-call | tf_op jit(solution)/shard_map/pallas_call | solution.py:148
  79.7 13.9 %all-to-all-start.1 = ((bf16[32,24,384]{2,1,0:T(8,128)(2,1)}), bf16[32,24,384]{2,1,0:T(8,128)(2,1)S(1)}, u32[]{:S(2)}, u32[]{:S(2)}) async-start(bf16[32,24,384]{2,1,0:T(8,128)(2,1)} %bitcast.18), calls=%async_computation.1 | async-start | bytes 1179648 | tf_op jit(solution)/shard_map/all_to_all | solution.py:22
  93.6 2.7 %collective-permute-start.10 = (bf16[192,384]{1,0:T(8,128)(2,1)S(1)}, bf16[192,384]{1,0:T(8,128)(2,1)S(1)}, u32[]{:S(2)}, u32[]{:S(2)}) collective-permute-start(bf16[192,384]{1,0:T(8,128)(2,1)S(1)} %get-tuple-element.35), channel_id=1, source_target_pairs={{0,3},{1,0},{2,1},{3,2},{4,7},{5,4},{6,5},{7,6},{8,11},{9,8},{10,9... | collective-permute-start | bytes 442376 | tf_op jit(solution)/shard_map/ppermute | solution.py:257
  96.4 3.0 %collective-permute-start.9 = (bf16[192,384]{1,0:T(8,128)(2,1)S(1)}, bf16[192,384]{1,0:T(8,128)(2,1)S(1)}, u32[]{:S(2)}, u32[]{:S(2)}) collective-permute-start(bf16[192,384]{1,0:T(8,128)(2,1)S(1)} %get-tuple-element.36), channel_id=1, source_target_pairs={{0,2},{1,3},{2,0},{3,1},{4,6},{5,7},{6,4},{7,5},{8,10},{9,11},{10,... | collective-permute-start | bytes 442376 | tf_op jit(solution)/shard_map/ppermute | solution.py:257
  99.4 4.0 %collective-permute-start.8 = (bf16[192,384]{1,0:T(8,128)(2,1)S(1)}, bf16[192,384]{1,0:T(8,128)(2,1)S(1)}, u32[]{:S(2)}, u32[]{:S(2)}) collective-permute-start(bf16[192,384]{1,0:T(8,128)(2,1)S(1)} %get-tuple-element.34), channel_id=1, source_target_pairs={{0,1},{1,2},{2,3},{3,0},{4,5},{5,6},{6,7},{7,4},{8,9},{9,10},{10,1... | collective-permute-start | bytes 442376 | tf_op jit(solution)/shard_map/ppermute | solution.py:257
  103.5 2.7 %collective-permute-done.10 = bf16[192,384]{1,0:T(8,128)(2,1)S(1)} collective-permute-done((bf16[192,384]{1,0:T(8,128)(2,1)S(1)}, bf16[192,384]{1,0:T(8,128)(2,1)S(1)}, u32[]{:S(2)}, u32[]{:S(2)}) %collective-permute-start.10) | collective-permute-done | bytes 147488 | tf_op jit(solution)/shard_map/ppermute | solution.py:257
  106.2 0.0 collective-permute-done.9
  106.2 2.5 %collective-permute-done.8 = bf16[192,384]{1,0:T(8,128)(2,1)S(1)} collective-permute-done((bf16[192,384]{1,0:T(8,128)(2,1)S(1)}, bf16[192,384]{1,0:T(8,128)(2,1)S(1)}, u32[]{:S(2)}, u32[]{:S(2)}) %collective-permute-start.8) | collective-permute-done | bytes 147488 | tf_op jit(solution)/shard_map/ppermute | solution.py:257
  108.7 0.1 fusion.5
  108.8 2.3 %collective-permute-start.12 = (bf16[192,128]{1,0:T(8,128)(2,1)S(1)}, bf16[192,128]{1,0:T(8,128)(2,1)S(1)}, u32[]{:S(2)}, u32[]{:S(2)}) collective-permute-start(bf16[192,128]{1,0:T(8,128)(2,1)S(1)} %get-tuple-element.38), channel_id=1, source_target_pairs={{0,8},{4,0},{8,4},{1,9},{5,1},{9,5},{2,10},{6,2},{10,6},{3,11},{7,... | collective-permute-start | bytes 147464 | tf_op jit(solution)/shard_map/ppermute | solution.py:269
  111.0 3.6 %collective-permute-start.11 = (bf16[192,128]{1,0:T(8,128)(2,1)S(1)}, bf16[192,128]{1,0:T(8,128)(2,1)S(1)}, u32[]{:S(2)}, u32[]{:S(2)}) collective-permute-start(bf16[192,128]{1,0:T(8,128)(2,1)S(1)} %get-tuple-element.37), channel_id=1, source_target_pairs={{0,4},{4,8},{8,0},{1,5},{5,9},{9,1},{2,6},{6,10},{10,2},{3,7},{7,1... | collective-permute-start | bytes 147464 | tf_op jit(solution)/shard_map/ppermute | solution.py:269
  114.6 0.6 copy.30
  115.3 1.2 collective-permute-done.12
  116.5 3.2 %collective-permute-done.11 = bf16[192,128]{1,0:T(8,128)(2,1)S(1)} collective-permute-done((bf16[192,128]{1,0:T(8,128)(2,1)S(1)}, bf16[192,128]{1,0:T(8,128)(2,1)S(1)}, u32[]{:S(2)}, u32[]{:S(2)}) %collective-permute-start.11) | collective-permute-done | bytes 49184 | tf_op jit(solution)/shard_map/ppermute | solution.py:269
  119.7 0.7 convert_add_fusion.1
  120.3 2.1 %all-to-all-done.1 = bf16[32,24,384]{2,1,0:T(8,128)(2,1)S(1)} async-done(((bf16[32,24,384]{2,1,0:T(8,128)(2,1)}), bf16[32,24,384]{2,1,0:T(8,128)(2,1)S(1)}, u32[]{:S(2)}, u32[]{:S(2)}) %all-to-all-start.1) | async-done | bytes 589856 | tf_op jit(solution)/shard_map/all_to_all | solution.py:22
  122.5 0.7 convert_reduce_fusion
  123.1 0.6 convert_reduce_fusion.1
  (4 shorter events, 0.1 us)
Async XLA Ops:
  0.6 21.0 %copy-start = (bf16[192,1536]{1,0:T(8,128)(2,1)S(1)}, bf16[192,1536]{1,0:T(8,128)(2,1)}, u32[]{:S(2)}) copy-start(bf16[192,1536]{1,0:T(8,128)(2,1)} %param.6) | copy-start | bytes 1769476
  2.3 47.6 %all-to-all-start = ((bf16[32,24,384]{2,1,0:T(8,128)(2,1)}), bf16[32,24,384]{2,1,0:T(8,128)(2,1)S(1)}, u32[]{:S(2)}, u32[]{:S(2)}) async-start(bf16[32,24,384]{2,1,0:T(8,128)(2,1)} %broadcast_in_dim.8), calls=%async_computation | async-start | bytes 1179648 | tf_op jit(solution)/shard_map/all_to_all | solution.py:22
  23.5 2.3 %copy-start.2 = (s32[12288]{0:T(1024)S(1)}, s32[12288]{0:T(1024)}, u32[]{:S(2)}) copy-start(s32[12288]{0:T(1024)} %param.10) | copy-start | bytes 147460
  23.8 2.2 %copy-start.3 = (f32[4]{0:T(128)S(1)}, f32[4]{0:T(128)}, u32[]{:S(2)}) copy-start(f32[4]{0:T(128)} %param.9) | copy-start | bytes 52
  23.9 3.6 %collective-permute-start = (bf16[192,768]{0,1:T(8,128)(2,1)S(1)}, bf16[192,768]{0,1:T(8,128)(2,1)S(1)}, u32[]{:S(2)}, u32[]{:S(2)}) collective-permute-start(bf16[192,768]{0,1:T(8,128)(2,1)S(1)} %get-tuple-element.32), channel_id=1, source_target_pairs={{0,12},{12,0},{1,13},{13,1},{2,14},{14,2},{3,15},{15,3},{4,16},{16... | collective-permute-start | bytes 884744 | tf_op jit(solution)/shard_map/ppermute | solution.py:185
  49.9 20.2 %collective-permute-start.7 = (bf16[768,384]{1,0:T(8,128)(2,1)S(1)}, bf16[768,384]{1,0:T(8,128)(2,1)}, u32[]{:S(2)}, u32[]{:S(2)}) collective-permute-start(bf16[768,384]{1,0:T(8,128)(2,1)S(1)} %bitcast.28), channel_id=1, source_target_pairs={{0,12},{12,0},{1,13},{13,1},{2,14},{14,2},{3,15},{15,3},{4,16},{16... | collective-permute-start | bytes 1769480 | tf_op jit(solution)/shard_map/ppermute | solution.py:215
  51.8 8.7 %copy-start.1 = (bf16[192,256]{1,0:T(8,128)(2,1)S(1)}, bf16[192,256]{1,0:T(8,128)(2,1)}, u32[]{:S(2)}) copy-start(bf16[192,256]{1,0:T(8,128)(2,1)} %up_ref) | copy-start | bytes 294916
  53.2 7.3 %collective-permute-start.1 = (f32[192,512]{1,0:T(8,128)S(1)}, f32[192,512]{1,0:T(8,128)S(1)}, u32[]{:S(2)}, u32[]{:S(2)}) collective-permute-start(f32[192,512]{1,0:T(8,128)S(1)} %get-tuple-element.18), channel_id=1, source_target_pairs={{0,12},{12,0},{1,13},{13,1},{2,14},{14,2},{3,15},{15,3},{4,16},{16... | collective-permute-start | bytes 1179656 | tf_op jit(solution)/shard_map/ppermute | solution.py:214
  55.6 4.9 %collective-permute-start.2 = (f32[128,128]{1,0:T(8,128)S(1)}, f32[128,128]{1,0:T(8,128)S(1)}, u32[]{:S(2)}, u32[]{:S(2)}) collective-permute-start(f32[128,128]{1,0:T(8,128)S(1)} %get-tuple-element.20), channel_id=1, source_target_pairs={{0,24},{24,48},{48,72},{72,96},{96,120},{120,144},{144,168},{168,1... | collective-permute-start | bytes 196616 | tf_op jit(solution)/shard_map/ppermute | solution.py:212
  58.6 1.9 %collective-permute-start.3 = (f32[128,128]{1,0:T(8,128)S(1)}, f32[128,128]{1,0:T(8,128)S(1)}, u32[]{:S(2)}, u32[]{:S(2)}) collective-permute-start(f32[128,128]{1,0:T(8,128)S(1)} %get-tuple-element.20), channel_id=1, source_target_pairs={{12,24},{36,48},{60,72},{84,96},{108,120},{132,144},{156,168},{180... | collective-permute-start | bytes 196616 | tf_op jit(solution)/shard_map/ppermute | solution.py:213
  62.7 14.5 %collective-permute-start.4 = (bf16[192,512]{1,0:T(8,128)(2,1)S(1)}, bf16[192,512]{1,0:T(8,128)(2,1)S(1)}, u32[]{:S(2)}, u32[]{:S(2)}) collective-permute-start(bf16[192,512]{1,0:T(8,128)(2,1)S(1)} %get-tuple-element.27.pack_ref), channel_id=1, source_target_pairs={{0,12},{12,0},{1,13},{13,1},{2,14},{14,2},{3,15},{15,3},{4,16},{16... | collective-permute-start | bytes 589832 | tf_op jit(solution)/shard_map/ppermute | solution.py:235
  68.1 9.1 %collective-permute-start.5 = (bf16[128,128]{1,0:T(8,128)(2,1)S(1)}, bf16[128,128]{1,0:T(8,128)(2,1)S(1)}, u32[]{:S(2)}, u32[]{:S(2)}) collective-permute-start(bf16[128,128]{1,0:T(8,128)(2,1)S(1)} %slice.40), channel_id=1, source_target_pairs={{24,0},{48,24},{72,48},{96,72},{120,96},{144,120},{168,144},{192,1... | collective-permute-start | bytes 98312 | tf_op jit(solution)/shard_map/ppermute | solution.py:233
  69.4 7.8 %collective-permute-start.6 = (bf16[128,128]{1,0:T(8,128)(2,1)S(1)}, bf16[128,128]{1,0:T(8,128)(2,1)S(1)}, u32[]{:S(2)}, u32[]{:S(2)}) collective-permute-start(bf16[128,128]{1,0:T(8,128)(2,1)S(1)} %slice.40), channel_id=1, source_target_pairs={{24,12},{48,36},{72,60},{96,84},{120,108},{144,132},{168,156},{192... | collective-permute-start | bytes 98312 | tf_op jit(solution)/shard_map/ppermute | solution.py:234
  79.7 42.8 %all-to-all-start.1 = ((bf16[32,24,384]{2,1,0:T(8,128)(2,1)}), bf16[32,24,384]{2,1,0:T(8,128)(2,1)S(1)}, u32[]{:S(2)}, u32[]{:S(2)}) async-start(bf16[32,24,384]{2,1,0:T(8,128)(2,1)} %bitcast.18), calls=%async_computation.1 | async-start | bytes 1179648 | tf_op jit(solution)/shard_map/all_to_all | solution.py:22
  93.6 12.5 %collective-permute-start.10 = (bf16[192,384]{1,0:T(8,128)(2,1)S(1)}, bf16[192,384]{1,0:T(8,128)(2,1)S(1)}, u32[]{:S(2)}, u32[]{:S(2)}) collective-permute-start(bf16[192,384]{1,0:T(8,128)(2,1)S(1)} %get-tuple-element.35), channel_id=1, source_target_pairs={{0,3},{1,0},{2,1},{3,2},{4,7},{5,4},{6,5},{7,6},{8,11},{9,8},{10,9... | collective-permute-start | bytes 442376 | tf_op jit(solution)/shard_map/ppermute | solution.py:257
  96.4 9.8 %collective-permute-start.9 = (bf16[192,384]{1,0:T(8,128)(2,1)S(1)}, bf16[192,384]{1,0:T(8,128)(2,1)S(1)}, u32[]{:S(2)}, u32[]{:S(2)}) collective-permute-start(bf16[192,384]{1,0:T(8,128)(2,1)S(1)} %get-tuple-element.36), channel_id=1, source_target_pairs={{0,2},{1,3},{2,0},{3,1},{4,6},{5,7},{6,4},{7,5},{8,10},{9,11},{10,... | collective-permute-start | bytes 442376 | tf_op jit(solution)/shard_map/ppermute | solution.py:257
  99.4 9.2 %collective-permute-start.8 = (bf16[192,384]{1,0:T(8,128)(2,1)S(1)}, bf16[192,384]{1,0:T(8,128)(2,1)S(1)}, u32[]{:S(2)}, u32[]{:S(2)}) collective-permute-start(bf16[192,384]{1,0:T(8,128)(2,1)S(1)} %get-tuple-element.34), channel_id=1, source_target_pairs={{0,1},{1,2},{2,3},{3,0},{4,5},{5,6},{6,7},{7,4},{8,9},{9,10},{10,1... | collective-permute-start | bytes 442376 | tf_op jit(solution)/shard_map/ppermute | solution.py:257
  108.8 7.7 %collective-permute-start.12 = (bf16[192,128]{1,0:T(8,128)(2,1)S(1)}, bf16[192,128]{1,0:T(8,128)(2,1)S(1)}, u32[]{:S(2)}, u32[]{:S(2)}) collective-permute-start(bf16[192,128]{1,0:T(8,128)(2,1)S(1)} %get-tuple-element.38), channel_id=1, source_target_pairs={{0,8},{4,0},{8,4},{1,9},{5,1},{9,5},{2,10},{6,2},{10,6},{3,11},{7,... | collective-permute-start | bytes 147464 | tf_op jit(solution)/shard_map/ppermute | solution.py:269
  111.0 8.6 %collective-permute-start.11 = (bf16[192,128]{1,0:T(8,128)(2,1)S(1)}, bf16[192,128]{1,0:T(8,128)(2,1)S(1)}, u32[]{:S(2)}, u32[]{:S(2)}) collective-permute-start(bf16[192,128]{1,0:T(8,128)(2,1)S(1)} %get-tuple-element.37), channel_id=1, source_target_pairs={{0,4},{4,8},{8,0},{1,5},{5,9},{9,1},{2,6},{6,10},{10,2},{3,7},{7,1... | collective-permute-start | bytes 147464 | tf_op jit(solution)/shard_map/ppermute | solution.py:269

commit v5 on v4

v5 whole, which is shorter than its diff:
```python
import jax
import jax.numpy as jnp
from jax import lax
from jax.experimental import pallas as pl
from jax.experimental.pallas import tpu as pltpu
from jax.sharding import Mesh, PartitionSpec as P


WINDOW = 128
TILE = 64
DP = ("y", "zh", "core")
TENSOR = ("zl", "x")
SWAP = [(0, 1), (1, 0)]
F32 = jnp.float32
BF16 = jnp.bfloat16
VMEM = pl.BlockSpec(memory_space=pltpu.VMEM)
SMEM = pl.BlockSpec(memory_space=pltpu.SMEM)


def exchange(value, axes):
    return lax.all_to_all(value, axes, split_axis=0, concat_axis=0, tiled=True)


def dot(a, b):
    return jnp.dot(a, b, preferred_element_type=F32)


def mask_kernel(query_ref, key_ref, bias_ref):
    tiles, span, lanes = bias_ref.shape
    key = lax.broadcasted_iota(jnp.int32, (span, TILE), 0)
    offset = lax.broadcasted_iota(jnp.int32, (span, TILE), 1) + WINDOW - key
    reach = (offset >= 0) & (offset < WINDOW)
    for tile in range(tiles):
        start = tile * TILE
        same = query_ref[:, start : start + TILE] == key_ref[start : start + span, :]
        bias = jnp.where(reach & same, 0.0, -1e30).astype(F32)
        bias_ref[tile] = jnp.concatenate([bias] * (lanes // TILE), axis=1)


def sort_kernel(wanted_ref, x_ref, mine_ref, theirs_ref, chosen_ref):
    half = wanted_ref.shape[1]
    source = lax.broadcasted_iota(jnp.int32, (half, half), 0)
    chosen_ref[...] = jnp.where(source == wanted_ref[...], 1.0, 0.0).astype(BF16)
    split(chosen_ref, x_ref, mine_ref, theirs_ref)


def resort_kernel(chosen_ref, x_ref, mine_ref, theirs_ref):
    split(chosen_ref, x_ref, mine_ref, theirs_ref)


def split(chosen_ref, x_ref, mine_ref, theirs_ref):
    half = chosen_ref.shape[1]
    for part in range(x_ref.shape[1] // half):
        both = dot(x_ref[:, part * half : (part + 1) * half], chosen_ref[...]).astype(BF16)
        columns = slice(part * half // 2, (part + 1) * half // 2)
        mine_ref[:, columns] = both[:, : half // 2]
        theirs_ref[:, columns] = both[:, half // 2 :]


def flip_kernel(
    core_ref, mine_ref, theirs_ref, halo_ref, other_ref, out_ref, mine_t_ref, theirs_t_ref, halo_t_ref
):
    @pl.when(core_ref[0] == 0)
    def _():
        out_ref[...] = halo_ref[...]

    @pl.when(core_ref[0] != 0)
    def _():
        out_ref[...] = other_ref[...]

    mine_t_ref[...] = jnp.transpose(mine_ref[...])
    theirs_t_ref[...] = jnp.transpose(theirs_ref[...])
    halo_t_ref[...] = jnp.transpose(out_ref[...])


def project_kernel(core_ref, mine_ref, theirs_ref, halo_ref, w_ref, keep_ref, send_ref):
    tokens, wide = send_ref.shape
    columns = wide - 128
    first = core_ref[0] == 0
    theirs = dot(theirs_ref[...], w_ref[...])
    mine_kv = dot(mine_ref[...], w_ref[:, columns - 128 :])
    halo_kv = dot(halo_ref[...], w_ref[:, columns - 128 :])
    send_ref[:, :columns] = theirs
    send_ref[: tokens - WINDOW, columns:] = mine_kv[: tokens - WINDOW]
    send_ref[tokens - WINDOW :, columns:] = jnp.where(first, mine_kv[tokens - WINDOW :], halo_kv)
    keep_ref[...] = jnp.where(first, halo_kv, theirs[tokens - WINDOW :, columns - 128 :])


def attend_kernel(
    mine_ref, w_ref, got_ref, keep_ref, up_ref, bias_ref, sinks_ref, att_ref, pack_ref, acc_ref
):
    tokens, wide = up_ref.shape
    columns = w_ref.shape[1]
    heads = wide // 64
    proj = dot(mine_ref[...], w_ref[...]) + got_ref[:, :columns]
    halo = keep_ref[...] + got_ref[tokens - WINDOW :, columns:]
    query = (proj[:, :wide].astype(BF16).astype(F32) * 0.125).astype(BF16)
    keyval = jnp.concatenate([halo, proj[:, wide:]], axis=0)
    flipped = jnp.transpose(keyval).astype(BF16)
    keyval = keyval.astype(BF16)
    upstream = up_ref[...]
    sinks = sinks_ref[...]
    acc_ref[...] = jnp.zeros_like(acc_ref)

    def stack(value, start):
        return jnp.concatenate(
            [value[start : start + TILE, 64 * h : 64 * h + 64] for h in range(heads)], axis=0
        )

    for tile in range(tokens // TILE):
        start = tile * TILE
        span = TILE + WINDOW
        qs, us = stack(query, start), stack(upstream, start)
        block = keyval[start : start + span]
        keys, values = block[:, :64], block[:, 64:]
        contract = (((1,), (1,)), ((), ()))
        score = lax.dot_general(keys, qs, contract, preferred_element_type=F32) + bias_ref[tile]
        top = jnp.maximum(jnp.max(score, axis=0, keepdims=True), sinks)
        expo = jnp.exp(score - top)
        total = jnp.sum(expo, axis=0, keepdims=True) + jnp.exp(sinks - top)
        probs = expo * (1.0 / total)
        probs_b = probs.astype(BF16)
        dprob = lax.dot_general(values, us, contract, preferred_element_type=F32)
        delta = jnp.sum(probs * dprob, axis=0, keepdims=True)
        dscore = (probs * (dprob - delta)).astype(BF16)
        part = flipped[:, start : start + span]
        att_t = dot(part[64:], probs_b)
        dq_t = dot(part[:64], dscore) * 0.125
        both = jnp.transpose(jnp.concatenate([att_t, dq_t], axis=0)).astype(BF16)
        for h in range(heads):
            rows = both[h * TILE : (h + 1) * TILE]
            att_ref[start : start + TILE, 64 * h : 64 * h + 64] = rows[:, :64]
            pack_ref[start : start + TILE, 64 * h : 64 * h + 64] = rows[:, 64:]
        grads = jnp.concatenate([dot(dscore, qs), dot(probs_b, us)], axis=1)
        acc_ref[start : start + span] += grads
    pack_ref[:, wide:columns] = acc_ref[WINDOW:].astype(BF16)
    pack_ref[: tokens - WINDOW, columns:] = jnp.zeros((tokens - WINDOW, 128), BF16)
    pack_ref[tokens - WINDOW :, columns:] = acc_ref[:WINDOW].astype(BF16)


def weight_grad_kernel(core_ref, mine_ref, theirs_ref, halo_ref, pack_ref, got_ref, out_ref, own_ref):
    columns = out_ref.shape[1]
    tokens = pack_ref.shape[0]
    wide = columns - 128
    first = core_ref[0] == 0
    mine_owed, theirs_owed = pack_ref[:, columns:], got_ref[:, columns:]
    none = jnp.zeros((tokens, 128), F32)
    mine_kv = pack_ref[:, wide:columns].astype(F32) + jnp.where(first, theirs_owed.astype(F32), none)
    theirs_kv = got_ref[:, wide:columns].astype(F32) + jnp.where(first, none, mine_owed.astype(F32))
    mine_kv = mine_kv.astype(BF16)
    own_ref[...] = mine_kv
    owed = jnp.where(first, mine_owed.astype(F32), theirs_owed.astype(F32)).astype(BF16)
    out_ref[:, :wide] = (
        dot(mine_ref[...], pack_ref[:, :wide]) + dot(theirs_ref[...], got_ref[:, :wide])
    ).astype(BF16)
    out_ref[:, wide:] = (
        dot(mine_ref[...], mine_kv)
        + dot(theirs_ref[...], theirs_kv.astype(BF16))
        + dot(halo_ref[...], owed[tokens - WINDOW :])
    ).astype(BF16)


def input_grad_kernel(place_ref, pack_ref, own_ref, late_ref, w_ref, other_ref, term_ref, whole_ref):
    tokens = pack_ref.shape[0]
    wide = whole_ref.shape[1] - 128
    across, deep = term_ref.shape[0], term_ref.shape[2] // 128
    here = place_ref[1]
    rows = 24

    def interleave(first_ref, second_ref):
        for start in range(0, w_ref.shape[0], rows):
            whole_ref[2 * start : 2 * start + rows] = first_ref[start : start + rows]
            whole_ref[2 * start + rows : 2 * start + 2 * rows] = second_ref[start : start + rows]

    pl.when(place_ref[0] == 0)(lambda: interleave(w_ref, other_ref))
    pl.when(place_ref[0] != 0)(lambda: interleave(other_ref, w_ref))
    tail = own_ref[tokens - WINDOW :].astype(F32) + late_ref[...].astype(F32)
    keyval = jnp.concatenate([own_ref[: tokens - WINDOW], tail.astype(BF16)], axis=0)
    mine = jnp.concatenate([pack_ref[:, :wide], keyval], axis=1)
    for x in range(across):
        slot = (x + across - here) % across
        for z in range(deep):
            rows = whole_ref[128 * (z * across + x) : 128 * (z * across + x + 1), :]
            block = lax.dot_general(
                mine, rows, (((1,), (1,)), ((), ())), preferred_element_type=F32
            )
            term_ref[slot, :, 128 * z : 128 * z + 128] = block.astype(BF16)


def near_sum_kernel(depth_ref, blocks_ref, *refs):
    *got_refs, out_ref = refs
    total = blocks_ref[0].astype(F32)
    for got in got_refs:
        total += got[...].astype(F32)
    deep = out_ref.shape[0]
    for z in range(deep):
        slot = (z + deep - depth_ref[0]) % deep
        out_ref[slot] = total[:, 128 * z : 128 * z + 128].astype(BF16)


def last_sum_kernel(grads_ref, sums_ref, *refs):
    *got_refs, inputs_ref, query_ref, keyval_ref = refs
    total = sums_ref[0].astype(F32)
    for got in got_refs:
        total += got[...].astype(F32)
    inputs_ref[...] = total
    grads = grads_ref[0].astype(F32)
    for index in range(1, grads_ref.shape[0]):
        grads += grads_ref[index].astype(F32)
    wide = query_ref.shape[1]
    query_ref[...] = grads[:, :wide]
    keyval_ref[...] = grads[:, wide:]


def call(kernel, specs, shapes, *args, scratch=()):
    placed = [
        a if s is SMEM else pltpu.with_memory_space_constraint(a, pltpu.VMEM)
        for a, s in zip(args, specs)
    ]
    return pl.pallas_call(
        kernel,
        in_specs=specs,
        out_specs=[VMEM] * len(shapes),
        out_shape=[pltpu.VMEM(*s) for s in shapes],
        scratch_shapes=scratch,
        compiler_params=pltpu.CompilerParams(vmem_limit_bytes=16 << 20),
    )(*placed)


def body(inputs, w_query, w_keyval, sinks, segments, upstream):
    tokens, width = inputs.shape
    heads = sinks.shape[0]
    split_at = w_query.shape[1]
    rows = w_query.shape[0]
    columns = split_at + w_keyval.shape[1]
    device = lax.axis_index(DP)
    core = lax.axis_index("core")
    flag = core.reshape(1).astype(jnp.int32)
    place = jnp.stack([core, lax.axis_index("x")]).astype(jnp.int32)
    depth = lax.axis_index("zl").reshape(1).astype(jnp.int32)
    count = lax.axis_size(DP)
    outer, near = lax.axis_size("y"), lax.axis_size("zh")
    deep, across = (lax.axis_size(axis) for axis in TENSOR)
    half = width // 2
    span = TILE + WINDOW

    shard = jnp.concatenate([w_query, w_keyval], axis=1)
    copies = lax.optimization_barrier(jnp.broadcast_to(shard[None], (near, rows, columns)))
    weights = exchange(copies, "zh")
    weights = weights.reshape(1, near * rows, columns)
    copies = lax.optimization_barrier(
        jnp.broadcast_to(weights, (outer, near * rows, columns))
    )
    weights = exchange(copies, "y").reshape(half, columns)

    target = jnp.arange(half, dtype=jnp.int32)
    part = jnp.where(target < half // 2, core, 1 - core)
    wanted = (target % (half // 2) // rows * 2 + part) * rows + target % rows
    halo = lax.ppermute(
        inputs[tokens - WINDOW :], DP, [(i - 1, i) for i in range(2, count, 2)]
    )
    mine_x, theirs_x, chosen = call(
        sort_kernel,
        [VMEM] * 2,
        [((tokens, half), BF16), ((tokens, half), BF16), ((half, half), BF16)],
        wanted[None, :],
        inputs,
    )
    theirs_x = lax.ppermute(theirs_x, "core", SWAP)
    halo, other_halo = call(
        resort_kernel,
        [VMEM] * 2,
        [((WINDOW, half), BF16), ((WINDOW, half), BF16)],
        chosen,
        halo,
    )
    other_halo = lax.ppermute(other_halo, "core", [(0, 1)])
    halo, mine_xt, theirs_xt, halo_t = call(
        flip_kernel,
        [SMEM] + [VMEM] * 4,
        [
            ((WINDOW, half), BF16),
            ((half, tokens), BF16),
            ((half, tokens), BF16),
            ((half, WINDOW), BF16),
        ],
        flag,
        mine_x,
        theirs_x,
        halo,
        other_halo,
    )

    seg_padded = jnp.concatenate([jnp.full((WINDOW,), -1, jnp.int32), segments], axis=0)
    query_seg = lax.dynamic_slice_in_dim(seg_padded, device * tokens + WINDOW, tokens, 0)
    key_seg = lax.dynamic_slice_in_dim(seg_padded, device * tokens, tokens + WINDOW, 0)
    (bias,) = call(
        mask_kernel,
        [VMEM] * 2,
        [((tokens // TILE, span, heads * TILE), F32)],
        query_seg[None, :],
        key_seg[:, None],
    )
    sink_row = jnp.repeat(sinks, TILE)[None, :]

    weights, mine_xt, theirs_xt, halo_t, bias, sink_row, upstream = lax.optimization_barrier(
        (weights, mine_xt, theirs_xt, halo_t, bias, sink_row, upstream)
    )
    keep, send = call(
        project_kernel,
        [SMEM] + [VMEM] * 4,
        [((WINDOW, 128), F32), ((tokens, columns + 128), F32)],
        flag,
        mine_x,
        theirs_x,
        halo,
        weights,
    )
    got = lax.ppermute(send, "core", SWAP)
    other = lax.ppermute(weights, "core", SWAP)
    attended, pack = call(
        attend_kernel,
        [VMEM] * 7,
        [((tokens, split_at), BF16), ((tokens, columns + 128), BF16)],
        mine_x,
        weights,
        got,
        keep,
        upstream,
        bias,
        sink_row,
        scratch=[pltpu.VMEM((WINDOW + tokens, 128), F32)],
    )
    got_pack = lax.ppermute(pack, "core", SWAP)
    late = lax.ppermute(
        pack[tokens - WINDOW :, columns:], DP, [(i, i - 1) for i in range(2, count, 2)]
    )

    term, own_kv = call(
        weight_grad_kernel,
        [SMEM] + [VMEM] * 5,
        [((half, columns), BF16), ((tokens, 128), BF16)],
        flag,
        mine_xt,
        theirs_xt,
        halo_t,
        pack,
        got_pack,
    )
    (blocks,) = call(
        input_grad_kernel,
        [SMEM] + [VMEM] * 5,
        [((across, tokens, width // across), BF16)],
        place,
        pack,
        own_kv,
        late,
        weights,
        other,
        scratch=[pltpu.VMEM((width, columns), BF16)],
    )
    term = exchange(term.reshape(outer, near * rows, columns), "y")
    term = jnp.sum(term.astype(F32), axis=0).astype(BF16)
    received = exchange(term.reshape(near, rows, columns), "zh")
    got_x = [
        lax.ppermute(blocks[s], "x", [(i, (i + s) % across) for i in range(across)])
        for s in range(1, across)
    ]
    (sums,) = call(
        near_sum_kernel,
        [SMEM] + [VMEM] * across,
        [((deep, tokens, 128), BF16)],
        depth,
        blocks,
        *got_x,
    )
    got_z = [
        lax.ppermute(sums[s], "zl", [(i, (i + s) % deep) for i in range(deep)])
        for s in range(1, deep)
    ]
    grad_inputs, grad_query, grad_keyval = pl.pallas_call(
        last_sum_kernel,
        in_specs=[VMEM] * (deep + 1),
        out_specs=[VMEM] * 3,
        out_shape=[
            jax.ShapeDtypeStruct((tokens, 128), F32),
            jax.ShapeDtypeStruct((rows, split_at), F32),
            jax.ShapeDtypeStruct((rows, columns - split_at), F32),
        ],
        compiler_params=pltpu.CompilerParams(vmem_limit_bytes=16 << 20),
    )(*(pltpu.with_memory_space_constraint(a, pltpu.VMEM) for a in (received, sums, *got_z)))
    return (attended, grad_inputs, grad_query, grad_keyval)


def solution(mesh):
    fine = Mesh(mesh.devices.reshape(8, 4, 2, 3, 4), (*DP, *TENSOR))

    return jax.shard_map(
        body,
        mesh=fine,
        in_specs=(
            P(DP, None),
            P(DP, TENSOR),
            P(DP, TENSOR),
            P(TENSOR),
            P(),
            P(DP, TENSOR),
        ),
        out_specs=(P(DP, TENSOR), P(DP, TENSOR), P(DP, TENSOR), P(DP, TENSOR)),
        check_vma=False,
    )
```

time: 124 us -> 121 us (0.976)
  the two profiles are of different devices: /device:TPU:70 before, /device:TPU:9 now
where the time goes in v5:
time: 121 us; the launch traced here: 120 us
  starting transfers between devices  54.3 us (45%)
  waiting for transfers between devices  27.4 us (23%)
  blocking collectives  23.5 us (19%)
  Pallas kernels  8.88 us (7%)
  local copies, waits for them, and re-layouts  3.74 us (3%)
  other arithmetic  1.63 us (1%)
    all_to_all x1, blocking collectives, exchange(): return lax.all_to_all(value, axes, split_axis=0, concat_axis=0, tiled=True)  23.5 us
    all_to_all x3, starting transfers between devices, exchange(): return lax.all_to_all(value, axes, split_axis=0, concat_axis=0, tiled=True)  19.1 us
    ppermute x1, waiting for transfers between devices, body(): other_halo = lax.ppermute(other_halo, 'core', [(0, 1)])  12.1 us
    ppermute x3, starting transfers between devices, body(): lax.ppermute(blocks[s], 'x', [(i, (i + s) % across) for i in range(across)])  10.5 us
    pallas_call x9, Pallas kernels, call(): pl.pallas_call(kernel, in_specs=specs, out_specs=[VMEM] * len(shapes), ou...  8.21 us
    ppermute x2, starting transfers between devices, body(): lax.ppermute(sums[s], 'zl', [(i, (i + s) % deep) for i in range(deep)])  8.15 us
    ppermute x1, waiting for transfers between devices, body(): lax.ppermute(pack[tokens - WINDOW:, columns:], DP, [(i, i - 1) for i in r...  5.95 us
    ppermute x1, starting transfers between devices, body(): lax.ppermute(inputs[tokens - WINDOW:], DP, [(i - 1, i) for i in range(2,...  5.25 us
  transfers between devices with their start and end apart: 15, of which 8 were waited for; matrix products, arithmetic and copies ran while one was open for 2% of the time, Pallas kernels for 4%

profile of v5, /device:TPU:9, one launch (start us, length us, event | category | flops | bytes accessed | tf_op | source)
XLA Modules:
  0.0 120.4 jit_solution(6037640343382260021)
XLA Ops:
  0.6 0.0 copy-start
  0.6 0.8 pad_maximum_fusion
  1.4 23.5 %all_to_all.20 = bf16[4,24,384]{2,1,0:T(8,128)(2,1)S(1)} all-to-all(bf16[4,24,384]{2,1,0:T(8,128)(2,1)S(1)} %broadcast_in_dim.34), channel_id=1, replica_groups=mesh['y'=8,'zh'=4,'core'=2,'zl'=3,'x'=4] {'zh'}, dimensions={0} | all-to-all | bytes 147456 | tf_op jit(solution)/shard_map/all_to_all | solution.py:21
  25.0 0.9 broadcast_in_dim.36
  25.8 7.0 %all-to-all-start.1 = ((bf16[8,96,384]{2,1,0:T(8,128)(2,1)}), bf16[8,96,384]{2,1,0:T(8,128)(2,1)S(1)}, u32[]{:S(2)}, u32[]{:S(2)}) async-start(bf16[8,96,384]{2,1,0:T(8,128)(2,1)} %broadcast_in_dim.36), calls=%async_computation.1 | async-start | bytes 1179648 | tf_op jit(solution)/shard_map/all_to_all | solution.py:21
  32.8 0.0 copy-done
  32.8 0.8 slice.21
  33.6 0.0 copy-start.4
  33.6 5.2 %collective-permute-start.1 = (bf16[128,1536]{1,0:T(8,128)(2,1)}, bf16[128,1536]{1,0:T(8,128)(2,1)S(1)}, u32[]{:S(2)}, u32[]{:S(2)}) collective-permute-start(bf16[128,1536]{1,0:T(8,128)(2,1)} %slice.21), channel_id=1, source_target_pairs={{12,24},{36,48},{60,72},{84,96},{108,120},{132,144},{156,168},{180... | collective-permute-start | bytes 1179656 | tf_op jit(solution)/shard_map/ppermute | solution.py:259
  38.9 0.0 copy-start.5
  38.9 1.4 %shard_map.93 = (bf16[192,768]{1,0:T(8,128)(2,1)S(1)}, bf16[192,768]{1,0:T(8,128)(2,1)}, bf16[768,768]{1,0:T(8,128)(2,1)S(1)}) custom-call(s32[1,768]{1,0:T(1,128)S(1)} %fusion.wanted_ref, bf16[192,1536]{1,0:T(8,128)(2,1)S(1)} %copy-done), custom_call_target="tpu_custom_call" | custom-call | tf_op jit(solution)/shard_map/pallas_call | solution.py:220
  40.3 1.9 %collective-permute-start = (bf16[192,768]{1,0:T(8,128)(2,1)}, bf16[192,768]{1,0:T(8,128)(2,1)S(1)}, u32[]{:S(2)}, u32[]{:S(2)}) collective-permute-start(bf16[192,768]{1,0:T(8,128)(2,1)} %get-tuple-element.30), channel_id=1, source_target_pairs={{0,12},{12,0},{1,13},{13,1},{2,14},{14,2},{3,15},{15,3},{4,16},{16... | collective-permute-start | bytes 884744 | tf_op jit(solution)/shard_map/ppermute | solution.py:269
  42.3 1.7 %collective-permute-done.1.x_ref = bf16[128,1536]{1,0:T(8,128)(2,1)S(1)} collective-permute-done((bf16[128,1536]{1,0:T(8,128)(2,1)}, bf16[128,1536]{1,0:T(8,128)(2,1)S(1)}, u32[]{:S(2)}, u32[]{:S(2)}) %collective-permute-start.1) | collective-permute-done | bytes 393248 | tf_op jit(solution)/shard_map/ppermute | solution.py:259
  44.0 1.2 shard_map.94
  45.1 0.0 copy-start.1
  45.1 1.3 %collective-permute-start.2 = (bf16[128,768]{1,0:T(8,128)(2,1)}, bf16[128,768]{1,0:T(8,128)(2,1)S(1)}, u32[]{:S(2)}, u32[]{:S(2)}) collective-permute-start(bf16[128,768]{1,0:T(8,128)(2,1)} %get-tuple-element.33), channel_id=1, source_target_pairs={{0,12},{1,13},{2,14},{3,15},{4,16},{5,17},{6,18},{7,19},{8,20},{9,... | collective-permute-start | bytes 589832 | tf_op jit(solution)/shard_map/ppermute | solution.py:277
  46.4 0.0 copy-done.4
  46.4 0.1 pad_dynamic-slice_fusion
  46.5 0.1 broadcast_in_dim.40.key_ref
  46.6 0.0 copy-done.5
  46.6 0.1 broadcast_in_dim.39
  46.7 0.1 broadcast_in_dim_reshape.3.sinks_ref
  46.8 0.1 pad_dynamic-slice_fusion.1
  46.9 0.0 copy-done.1
  46.9 0.4 shard_map.96.bias_ref
  47.2 0.0 collective-permute-done.theirs_ref
  47.3 12.1 %collective-permute-done.2.other_ref = bf16[128,768]{1,0:T(8,128)(2,1)S(1)} collective-permute-done((bf16[128,768]{1,0:T(8,128)(2,1)}, bf16[128,768]{1,0:T(8,128)(2,1)S(1)}, u32[]{:S(2)}, u32[]{:S(2)}) %collective-permute-start.2) | collective-permute-done | bytes 196640 | tf_op jit(solution)/shard_map/ppermute | solution.py:277
  59.4 0.0 copy-start.2
  59.4 0.9 copy-done.2
  60.3 0.0 copy-start.3
  60.3 0.3 shard_map.95
  60.6 0.0 all-to-all-done.1
  60.6 0.4 shard_map.97
  61.1 2.1 %collective-permute-start.3 = (f32[192,512]{1,0:T(8,128)S(1)}, f32[192,512]{1,0:T(8,128)S(1)}, u32[]{:S(2)}, u32[]{:S(2)}) collective-permute-start(f32[192,512]{1,0:T(8,128)S(1)} %get-tuple-element.39), channel_id=1, source_target_pairs={{0,12},{12,0},{1,13},{13,1},{2,14},{14,2},{3,15},{15,3},{4,16},{16... | collective-permute-start | bytes 1179656 | tf_op jit(solution)/shard_map/ppermute | solution.py:319
  63.1 1.6 %collective-permute-done.3.got_ref = f32[192,512]{1,0:T(8,128)S(1)} collective-permute-done((f32[192,512]{1,0:T(8,128)S(1)}, f32[192,512]{1,0:T(8,128)S(1)}, u32[]{:S(2)}, u32[]{:S(2)}) %collective-permute-start.3) | collective-permute-done | bytes 393248 | tf_op jit(solution)/shard_map/ppermute | solution.py:319
  64.7 0.0 copy-done.3
  64.7 1.7 %shard_map.98 = (bf16[192,256]{1,0:T(8,128)(2,1)S(1)}, bf16[192,512]{1,0:T(8,128)(2,1)S(1)}) custom-call(bf16[192,768]{1,0:T(8,128)(2,1)S(1)} %get-tuple-element.29.mine_ref, bf16[768,384]{1,0:T(8,128)(2,1)S(1)} %bitcast.19, f32[192,512]{1,0:T(8,128)S(1)} %collective-permute-done.3.got_ref, f32[128,128]{1,0:T(8,128)S(1)} %get-tuple-element.40.keep_ref, ...), custom_call_target="tpu_custom_call" | custom-call | tf_op jit(solution)/shard_map/pallas_call | solution.py:220
  66.3 2.0 %collective-permute-start.4 = (bf16[192,512]{1,0:T(8,128)(2,1)S(1)}, bf16[192,512]{1,0:T(8,128)(2,1)S(1)}, u32[]{:S(2)}, u32[]{:S(2)}) collective-permute-start(bf16[192,512]{1,0:T(8,128)(2,1)S(1)} %get-tuple-element.48.pack_ref), channel_id=1, source_target_pairs={{0,12},{12,0},{1,13},{13,1},{2,14},{14,2},{3,15},{15,3},{4,16},{16... | collective-permute-start | bytes 589832 | tf_op jit(solution)/shard_map/ppermute | solution.py:334
  68.4 1.3 %collective-permute-done.4.got_ref = bf16[192,512]{1,0:T(8,128)(2,1)S(1)} collective-permute-done((bf16[192,512]{1,0:T(8,128)(2,1)S(1)}, bf16[192,512]{1,0:T(8,128)(2,1)S(1)}, u32[]{:S(2)}, u32[]{:S(2)}) %collective-permute-start.4) | collective-permute-done | bytes 196640 | tf_op jit(solution)/shard_map/ppermute | solution.py:334
  69.7 1.4 %shard_map.99 = (bf16[768,384]{1,0:T(8,128)(2,1)}, bf16[192,128]{1,0:T(8,128)(2,1)S(1)}) custom-call(s32[1]{0:T(128)} %bitcast.2.core_ref, bf16[768,192]{1,0:T(8,128)(2,1)S(1)} %get-tuple-element.45.mine_ref, bf16[768,192]{1,0:T(8,128)(2,1)S(1)} %get-tuple-element.46.theirs_ref, bf16[768,128]{1,0:T(8,128)(2,1)S(1)} %get-tuple-element.47.halo_ref, ...), custom_call_target="tpu_custom_call" | custom-call | tf_op jit(solution)/shard_map/pallas_call | solution.py:220
  71.1 8.9 %all-to-all-start.2 = ((bf16[8,96,384]{2,1,0:T(8,128)(2,1)}), bf16[8,96,384]{2,1,0:T(8,128)(2,1)S(1)}, u32[]{:S(2)}, u32[]{:S(2)}) async-start(bf16[8,96,384]{2,1,0:T(8,128)(2,1)} %bitcast.4), calls=%async_computation.2 | async-start | bytes 1179648 | tf_op jit(solution)/shard_map/all_to_all | solution.py:21
  80.0 2.6 %collective-permute-start.6 = (bf16[768,384]{1,0:T(8,128)(2,1)S(1)}, bf16[768,384]{1,0:T(8,128)(2,1)S(1)}, u32[]{:S(2)}, u32[]{:S(2)}) collective-permute-start(bf16[768,384]{1,0:T(8,128)(2,1)S(1)} %bitcast.20), channel_id=1, source_target_pairs={{0,12},{12,0},{1,13},{13,1},{2,14},{14,2},{3,15},{15,3},{4,16},{16... | collective-permute-start | bytes 1769480 | tf_op jit(solution)/shard_map/ppermute | solution.py:320
  82.6 1.3 %collective-permute-start.5 = (bf16[128,128]{1,0:T(8,128)(2,1)S(1)}, bf16[128,128]{1,0:T(8,128)(2,1)S(1)}, u32[]{:S(2)}, u32[]{:S(2)}) collective-permute-start(bf16[128,128]{1,0:T(8,128)(2,1)S(1)} %slice.22), channel_id=1, source_target_pairs={{24,12},{48,36},{72,60},{96,84},{120,108},{144,132},{168,156},{192... | collective-permute-start | bytes 98312 | tf_op jit(solution)/shard_map/ppermute | solution.py:335
  83.9 0.1 pad_add_fusion.place_ref
  84.0 5.9 %collective-permute-done.5.late_ref = bf16[128,128]{1,0:T(8,128)(2,1)S(1)} collective-permute-done((bf16[128,128]{1,0:T(8,128)(2,1)S(1)}, bf16[128,128]{1,0:T(8,128)(2,1)S(1)}, u32[]{:S(2)}, u32[]{:S(2)}) %collective-permute-start.5) | collective-permute-done | bytes 32800 | tf_op jit(solution)/shard_map/ppermute | solution.py:335
  89.9 0.0 collective-permute-done.6.other_ref
  89.9 1.3 %shard_map.100.blocks_ref = bf16[4,192,384]{2,1,0:T(8,128)(2,1)S(1)} custom-call(s32[2]{0:T(128)S(1)} %pad_add_fusion.place_ref, bf16[192,512]{1,0:T(8,128)(2,1)S(1)} %get-tuple-element.48.pack_ref, bf16[192,128]{1,0:T(8,128)(2,1)S(1)} %get-tuple-element.50.own_ref, bf16[128,128]{1,0:T(8,128)(2,1)S(1)} %collective-permute-done.5.late_ref, ...), custom_call_target="tpu_custom_call" | custom-call | tf_op jit(solution)/shard_map/pallas_call | solution.py:220
  91.3 3.1 %collective-permute-start.7 = (bf16[192,384]{1,0:T(8,128)(2,1)S(1)}, bf16[192,384]{1,0:T(8,128)(2,1)S(1)}, u32[]{:S(2)}, u32[]{:S(2)}) collective-permute-start(bf16[192,384]{1,0:T(8,128)(2,1)S(1)} %get-tuple-element.56), channel_id=1, source_target_pairs={{0,1},{1,2},{2,3},{3,0},{4,5},{5,6},{6,7},{7,4},{8,9},{9,10},{10,1... | collective-permute-start | bytes 442376 | tf_op jit(solution)/shard_map/ppermute | solution.py:366
  94.5 4.4 %collective-permute-start.8 = (bf16[192,384]{1,0:T(8,128)(2,1)S(1)}, bf16[192,384]{1,0:T(8,128)(2,1)S(1)}, u32[]{:S(2)}, u32[]{:S(2)}) collective-permute-start(bf16[192,384]{1,0:T(8,128)(2,1)S(1)} %get-tuple-element.55), channel_id=1, source_target_pairs={{0,2},{1,3},{2,0},{3,1},{4,6},{5,7},{6,4},{7,5},{8,10},{9,11},{10,... | collective-permute-start | bytes 442376 | tf_op jit(solution)/shard_map/ppermute | solution.py:366
  98.8 3.1 %collective-permute-start.9 = (bf16[192,384]{1,0:T(8,128)(2,1)S(1)}, bf16[192,384]{1,0:T(8,128)(2,1)S(1)}, u32[]{:S(2)}, u32[]{:S(2)}) collective-permute-start(bf16[192,384]{1,0:T(8,128)(2,1)S(1)} %get-tuple-element.54), channel_id=1, source_target_pairs={{0,3},{1,0},{2,1},{3,2},{4,7},{5,4},{6,5},{7,6},{8,11},{9,8},{10,9... | collective-permute-start | bytes 442376 | tf_op jit(solution)/shard_map/ppermute | solution.py:366
  101.9 0.0 collective-permute-done.7.refs_0_
  101.9 0.0 collective-permute-done.8.refs_1_
  101.9 2.8 %collective-permute-done.9.refs_2_ = bf16[192,384]{1,0:T(8,128)(2,1)S(1)} collective-permute-done((bf16[192,384]{1,0:T(8,128)(2,1)S(1)}, bf16[192,384]{1,0:T(8,128)(2,1)S(1)}, u32[]{:S(2)}, u32[]{:S(2)}) %collective-permute-start.9) | collective-permute-done | bytes 147488 | tf_op jit(solution)/shard_map/ppermute | solution.py:366
  104.7 0.1 shard_map.101.sums_ref
  104.8 0.0 all-to-all-done.2
  104.8 0.7 reduce_sum.12
  105.5 3.3 %all-to-all-start.3 = ((bf16[4,24,384]{2,1,0:T(8,128)(2,1)}), bf16[4,24,384]{2,1,0:T(8,128)(2,1)S(1)}, u32[]{:S(2)}, u32[]{:S(2)}) async-start(bf16[4,24,384]{2,1,0:T(8,128)(2,1)} %bitcast.5), calls=%async_computation.3 | async-start | bytes 147456 | tf_op jit(solution)/shard_map/all_to_all | solution.py:21
  108.8 3.9 %collective-permute-start.10 = (bf16[192,128]{1,0:T(8,128)(2,1)S(1)}, bf16[192,128]{1,0:T(8,128)(2,1)S(1)}, u32[]{:S(2)}, u32[]{:S(2)}) collective-permute-start(bf16[192,128]{1,0:T(8,128)(2,1)S(1)} %get-tuple-element.58), channel_id=1, source_target_pairs={{0,4},{4,8},{8,0},{1,5},{5,9},{9,1},{2,6},{6,10},{10,2},{3,7},{7,1... | collective-permute-start | bytes 147464 | tf_op jit(solution)/shard_map/ppermute | solution.py:378
  112.7 4.3 %collective-permute-start.11 = (bf16[192,128]{1,0:T(8,128)(2,1)S(1)}, bf16[192,128]{1,0:T(8,128)(2,1)S(1)}, u32[]{:S(2)}, u32[]{:S(2)}) collective-permute-start(bf16[192,128]{1,0:T(8,128)(2,1)S(1)} %get-tuple-element.57), channel_id=1, source_target_pairs={{0,8},{4,0},{8,4},{1,9},{5,1},{9,5},{2,10},{6,2},{10,6},{3,11},{7,... | collective-permute-start | bytes 147464 | tf_op jit(solution)/shard_map/ppermute | solution.py:378
  117.0 0.6 copy.11
  117.6 0.1 collective-permute-done.10.refs_0_
  117.7 2.0 %collective-permute-done.11.refs_1_ = bf16[192,128]{1,0:T(8,128)(2,1)S(1)} collective-permute-done((bf16[192,128]{1,0:T(8,128)(2,1)S(1)}, bf16[192,128]{1,0:T(8,128)(2,1)S(1)}, u32[]{:S(2)}, u32[]{:S(2)}) %collective-permute-start.11) | collective-permute-done | bytes 49184 | tf_op jit(solution)/shard_map/ppermute | solution.py:378
  119.7 0.0 all-to-all-done.3.grads_ref
  119.7 0.7 shard_map.102
  (5 shorter events, 0.1 us)
Async XLA Ops:
  0.6 32.2 %copy-start = (bf16[192,1536]{1,0:T(8,128)(2,1)S(1)}, bf16[192,1536]{1,0:T(8,128)(2,1)}, u32[]{:S(2)}) copy-start(bf16[192,1536]{1,0:T(8,128)(2,1)} %x_ref.1) | copy-start | bytes 1769476
  25.8 34.8 %all-to-all-start.1 = ((bf16[8,96,384]{2,1,0:T(8,128)(2,1)}), bf16[8,96,384]{2,1,0:T(8,128)(2,1)S(1)}, u32[]{:S(2)}, u32[]{:S(2)}) async-start(bf16[8,96,384]{2,1,0:T(8,128)(2,1)} %broadcast_in_dim.36), calls=%async_computation.1 | async-start | bytes 1179648 | tf_op jit(solution)/shard_map/all_to_all | solution.py:21
  33.6 12.8 %copy-start.4 = (s32[12288]{0:T(1024)S(1)}, s32[12288]{0:T(1024)}, u32[]{:S(2)}) copy-start(s32[12288]{0:T(1024)} %param.10) | copy-start | bytes 147460
  33.6 10.3 %collective-permute-start.1 = (bf16[128,1536]{1,0:T(8,128)(2,1)}, bf16[128,1536]{1,0:T(8,128)(2,1)S(1)}, u32[]{:S(2)}, u32[]{:S(2)}) collective-permute-start(bf16[128,1536]{1,0:T(8,128)(2,1)} %slice.21), channel_id=1, source_target_pairs={{12,24},{36,48},{60,72},{84,96},{108,120},{132,144},{156,168},{180... | collective-permute-start | bytes 1179656 | tf_op jit(solution)/shard_map/ppermute | solution.py:259
  38.9 7.7 %copy-start.5 = (f32[4]{0:T(128)S(1)}, f32[4]{0:T(128)}, u32[]{:S(2)}) copy-start(f32[4]{0:T(128)} %param.9) | copy-start | bytes 52
  40.3 6.9 %collective-permute-start = (bf16[192,768]{1,0:T(8,128)(2,1)}, bf16[192,768]{1,0:T(8,128)(2,1)S(1)}, u32[]{:S(2)}, u32[]{:S(2)}) collective-permute-start(bf16[192,768]{1,0:T(8,128)(2,1)} %get-tuple-element.30), channel_id=1, source_target_pairs={{0,12},{12,0},{1,13},{13,1},{2,14},{14,2},{3,15},{15,3},{4,16},{16... | collective-permute-start | bytes 884744 | tf_op jit(solution)/shard_map/ppermute | solution.py:269
  45.1 1.7 %copy-start.1 = (bf16[128,768]{1,0:T(8,128)(2,1)}, bf16[128,768]{1,0:T(8,128)(2,1)S(1)}, u32[]{:S(2)}) copy-start(bf16[128,768]{1,0:T(8,128)(2,1)S(1)} %get-tuple-element.32.halo_ref) | copy-start | bytes 589828
  45.1 14.2 %collective-permute-start.2 = (bf16[128,768]{1,0:T(8,128)(2,1)}, bf16[128,768]{1,0:T(8,128)(2,1)S(1)}, u32[]{:S(2)}, u32[]{:S(2)}) collective-permute-start(bf16[128,768]{1,0:T(8,128)(2,1)} %get-tuple-element.33), channel_id=1, source_target_pairs={{0,12},{1,13},{2,14},{3,15},{4,16},{5,17},{6,18},{7,19},{8,20},{9,... | collective-permute-start | bytes 589832 | tf_op jit(solution)/shard_map/ppermute | solution.py:277
  59.4 0.9 copy-start.2
  60.3 4.4 %copy-start.3 = (bf16[192,256]{1,0:T(8,128)(2,1)S(1)}, bf16[192,256]{1,0:T(8,128)(2,1)}, u32[]{:S(2)}) copy-start(bf16[192,256]{1,0:T(8,128)(2,1)} %up_ref) | copy-start | bytes 294916
  61.1 3.6 %collective-permute-start.3 = (f32[192,512]{1,0:T(8,128)S(1)}, f32[192,512]{1,0:T(8,128)S(1)}, u32[]{:S(2)}, u32[]{:S(2)}) collective-permute-start(f32[192,512]{1,0:T(8,128)S(1)} %get-tuple-element.39), channel_id=1, source_target_pairs={{0,12},{12,0},{1,13},{13,1},{2,14},{14,2},{3,15},{15,3},{4,16},{16... | collective-permute-start | bytes 1179656 | tf_op jit(solution)/shard_map/ppermute | solution.py:319
  66.3 3.3 %collective-permute-start.4 = (bf16[192,512]{1,0:T(8,128)(2,1)S(1)}, bf16[192,512]{1,0:T(8,128)(2,1)S(1)}, u32[]{:S(2)}, u32[]{:S(2)}) collective-permute-start(bf16[192,512]{1,0:T(8,128)(2,1)S(1)} %get-tuple-element.48.pack_ref), channel_id=1, source_target_pairs={{0,12},{12,0},{1,13},{13,1},{2,14},{14,2},{3,15},{15,3},{4,16},{16... | collective-permute-start | bytes 589832 | tf_op jit(solution)/shard_map/ppermute | solution.py:334
  71.1 33.7 %all-to-all-start.2 = ((bf16[8,96,384]{2,1,0:T(8,128)(2,1)}), bf16[8,96,384]{2,1,0:T(8,128)(2,1)S(1)}, u32[]{:S(2)}, u32[]{:S(2)}) async-start(bf16[8,96,384]{2,1,0:T(8,128)(2,1)} %bitcast.4), calls=%async_computation.2 | async-start | bytes 1179648 | tf_op jit(solution)/shard_map/all_to_all | solution.py:21
  80.0 10.0 %collective-permute-start.6 = (bf16[768,384]{1,0:T(8,128)(2,1)S(1)}, bf16[768,384]{1,0:T(8,128)(2,1)S(1)}, u32[]{:S(2)}, u32[]{:S(2)}) collective-permute-start(bf16[768,384]{1,0:T(8,128)(2,1)S(1)} %bitcast.20), channel_id=1, source_target_pairs={{0,12},{12,0},{1,13},{13,1},{2,14},{14,2},{3,15},{15,3},{4,16},{16... | collective-permute-start | bytes 1769480 | tf_op jit(solution)/shard_map/ppermute | solution.py:320
  82.6 7.3 %collective-permute-start.5 = (bf16[128,128]{1,0:T(8,128)(2,1)S(1)}, bf16[128,128]{1,0:T(8,128)(2,1)S(1)}, u32[]{:S(2)}, u32[]{:S(2)}) collective-permute-start(bf16[128,128]{1,0:T(8,128)(2,1)S(1)} %slice.22), channel_id=1, source_target_pairs={{24,12},{48,36},{72,60},{96,84},{120,108},{144,132},{168,156},{192... | collective-permute-start | bytes 98312 | tf_op jit(solution)/shard_map/ppermute | solution.py:335
  91.3 10.6 %collective-permute-start.7 = (bf16[192,384]{1,0:T(8,128)(2,1)S(1)}, bf16[192,384]{1,0:T(8,128)(2,1)S(1)}, u32[]{:S(2)}, u32[]{:S(2)}) collective-permute-start(bf16[192,384]{1,0:T(8,128)(2,1)S(1)} %get-tuple-element.56), channel_id=1, source_target_pairs={{0,1},{1,2},{2,3},{3,0},{4,5},{5,6},{6,7},{7,4},{8,9},{9,10},{10,1... | collective-permute-start | bytes 442376 | tf_op jit(solution)/shard_map/ppermute | solution.py:366
  94.5 7.5 %collective-permute-start.8 = (bf16[192,384]{1,0:T(8,128)(2,1)S(1)}, bf16[192,384]{1,0:T(8,128)(2,1)S(1)}, u32[]{:S(2)}, u32[]{:S(2)}) collective-permute-start(bf16[192,384]{1,0:T(8,128)(2,1)S(1)} %get-tuple-element.55), channel_id=1, source_target_pairs={{0,2},{1,3},{2,0},{3,1},{4,6},{5,7},{6,4},{7,5},{8,10},{9,11},{10,... | collective-permute-start | bytes 442376 | tf_op jit(solution)/shard_map/ppermute | solution.py:366
  98.8 5.9 %collective-permute-start.9 = (bf16[192,384]{1,0:T(8,128)(2,1)S(1)}, bf16[192,384]{1,0:T(8,128)(2,1)S(1)}, u32[]{:S(2)}, u32[]{:S(2)}) collective-permute-start(bf16[192,384]{1,0:T(8,128)(2,1)S(1)} %get-tuple-element.54), channel_id=1, source_target_pairs={{0,3},{1,0},{2,1},{3,2},{4,7},{5,4},{6,5},{7,6},{8,11},{9,8},{10,9... | collective-permute-start | bytes 442376 | tf_op jit(solution)/shard_map/ppermute | solution.py:366
  105.5 14.2 %all-to-all-start.3 = ((bf16[4,24,384]{2,1,0:T(8,128)(2,1)}), bf16[4,24,384]{2,1,0:T(8,128)(2,1)S(1)}, u32[]{:S(2)}, u32[]{:S(2)}) async-start(bf16[4,24,384]{2,1,0:T(8,128)(2,1)} %bitcast.5), calls=%async_computation.3 | async-start | bytes 147456 | tf_op jit(solution)/shard_map/all_to_all | solution.py:21
  108.8 8.9 %collective-permute-start.10 = (bf16[192,128]{1,0:T(8,128)(2,1)S(1)}, bf16[192,128]{1,0:T(8,128)(2,1)S(1)}, u32[]{:S(2)}, u32[]{:S(2)}) collective-permute-start(bf16[192,128]{1,0:T(8,128)(2,1)S(1)} %get-tuple-element.58), channel_id=1, source_target_pairs={{0,4},{4,8},{8,0},{1,5},{5,9},{9,1},{2,6},{6,10},{10,2},{3,7},{7,1... | collective-permute-start | bytes 147464 | tf_op jit(solution)/shard_map/ppermute | solution.py:378
  112.7 7.0 %collective-permute-start.11 = (bf16[192,128]{1,0:T(8,128)(2,1)S(1)}, bf16[192,128]{1,0:T(8,128)(2,1)S(1)}, u32[]{:S(2)}, u32[]{:S(2)}) collective-permute-start(bf16[192,128]{1,0:T(8,128)(2,1)S(1)} %get-tuple-element.57), channel_id=1, source_target_pairs={{0,8},{4,0},{8,4},{1,9},{5,1},{9,5},{2,10},{6,2},{10,6},{3,11},{7,... | collective-permute-start | bytes 147464 | tf_op jit(solution)/shard_map/ppermute | solution.py:378

commit v6 on v5

--- a/solution.py
+++ b/solution.py
@@ -14,18 +14,36 @@
 F32 = jnp.float32
 BF16 = jnp.bfloat16
 VMEM = pl.BlockSpec(memory_space=pltpu.VMEM)
+FETCH = pl.BlockSpec(memory_space=pltpu.VMEM)
 SMEM = pl.BlockSpec(memory_space=pltpu.SMEM)
 
 
-def exchange(value, axes):
-    return lax.all_to_all(value, axes, split_axis=0, concat_axis=0, tiled=True)
+def groups_of(sizes, axis):
+    outer, near, cores = sizes
+    count = sizes[axis]
+    groups = []
+    for rest in range(outer * near // count):
+        for core in range(cores):
+            members = [(rank + core * count // 2) % count for rank in range(count)]
+            chips = [m * near + rest if axis == 0 else rest * near + m for m in members]
+            groups.append([chip * cores + core for chip in chips])
+    return groups
+
+
+def exchange(value, axis):
+    sizes = [lax.axis_size(name) for name in DP]
+    groups = groups_of(sizes, DP.index(axis))
+    return lax.all_to_all(
+        value, DP, split_axis=0, concat_axis=0, tiled=True, axis_index_groups=groups
+    )
 
 
 def dot(a, b):
     return jnp.dot(a, b, preferred_element_type=F32)
 
 
-def mask_kernel(query_ref, key_ref, bias_ref):
+def mask_kernel(query_ref, key_ref, up_ref, bias_ref, held_ref):
+    held_ref[...] = up_ref[...]
     tiles, span, lanes = bias_ref.shape
     key = lax.broadcasted_iota(jnp.int32, (span, TILE), 0)
     offset = lax.broadcasted_iota(jnp.int32, (span, TILE), 1) + WINDOW - key
@@ -37,24 +55,34 @@
         bias_ref[tile] = jnp.concatenate([bias] * (lanes // TILE), axis=1)
 
 
-def sort_kernel(wanted_ref, x_ref, mine_ref, theirs_ref, chosen_ref):
+def sort_kernel(core_ref, wanted_ref, x_ref, mine_ref, theirs_ref, chosen_ref):
     half = wanted_ref.shape[1]
     source = lax.broadcasted_iota(jnp.int32, (half, half), 0)
     chosen_ref[...] = jnp.where(source == wanted_ref[...], 1.0, 0.0).astype(BF16)
-    split(chosen_ref, x_ref, mine_ref, theirs_ref)
-
-
-def resort_kernel(chosen_ref, x_ref, mine_ref, theirs_ref):
-    split(chosen_ref, x_ref, mine_ref, theirs_ref)
-
-
-def split(chosen_ref, x_ref, mine_ref, theirs_ref):
+    split(core_ref, chosen_ref, x_ref, mine_ref, theirs_ref)
+
+
+def resort_kernel(core_ref, chosen_ref, x_ref, mine_ref, theirs_ref):
+    split(core_ref, chosen_ref, x_ref, mine_ref, theirs_ref)
+
+
+def split(core_ref, chosen_ref, x_ref, mine_ref, theirs_ref):
     half = chosen_ref.shape[1]
-    for part in range(x_ref.shape[1] // half):
+    wide = half // 2
+    for part in range(2):
         both = dot(x_ref[:, part * half : (part + 1) * half], chosen_ref[...]).astype(BF16)
-        columns = slice(part * half // 2, (part + 1) * half // 2)
-        mine_ref[:, columns] = both[:, : half // 2]
-        theirs_ref[:, columns] = both[:, half // 2 :]
+        plain = slice(part * wide, (part + 1) * wide)
+        turned = slice((1 - part) * wide, (2 - part) * wide)
+
+        @pl.when(core_ref[0] == 0)
+        def _():
+            mine_ref[:, plain] = both[:, :wide]
+            theirs_ref[:, turned] = both[:, wide:]
+
+        @pl.when(core_ref[0] != 0)
+        def _():
+            mine_ref[:, turned] = both[:, :wide]
+            theirs_ref[:, plain] = both[:, wide:]
 
 
 def flip_kernel(
@@ -168,9 +196,13 @@
     rows = 24
 
     def interleave(first_ref, second_ref):
-        for start in range(0, w_ref.shape[0], rows):
-            whole_ref[2 * start : 2 * start + rows] = first_ref[start : start + rows]
-            whole_ref[2 * start + rows : 2 * start + 2 * rows] = second_ref[start : start + rows]
+        blocks = w_ref.shape[0] // rows
+        for index in range(blocks):
+            into = 2 * index * rows
+            y, z = index // 4, index % 4
+            turned = (((y + blocks // 8) % (blocks // 4)) * 4 + (z + 2) % 4) * rows
+            whole_ref[into : into + rows] = first_ref[index * rows : (index + 1) * rows]
+            whole_ref[into + rows : into + 2 * rows] = second_ref[turned : turned + rows]
 
     pl.when(place_ref[0] == 0)(lambda: interleave(w_ref, other_ref))
     pl.when(place_ref[0] != 0)(lambda: interleave(other_ref, w_ref))
@@ -214,7 +246,7 @@
 
 def call(kernel, specs, shapes, *args, scratch=()):
     placed = [
-        a if s is SMEM else pltpu.with_memory_space_constraint(a, pltpu.VMEM)
+        pltpu.with_memory_space_constraint(a, pltpu.VMEM) if s is VMEM else a
         for a, s in zip(args, specs)
     ]
     return pl.pallas_call(
@@ -255,29 +287,33 @@
 
     target = jnp.arange(half, dtype=jnp.int32)
     part = jnp.where(target < half // 2, core, 1 - core)
-    wanted = (target % (half // 2) // rows * 2 + part) * rows + target % rows
+    block = target % (half // 2) // rows
+    block = block // near * near + (block % near + part * (near // 2)) % near
+    wanted = (block * 2 + part) * rows + target % rows
     halo = lax.ppermute(
         inputs[tokens - WINDOW :], DP, [(i - 1, i) for i in range(2, count, 2)]
     )
     mine_x, theirs_x, chosen = call(
         sort_kernel,
-        [VMEM] * 2,
+        [SMEM] + [VMEM] * 2,
         [((tokens, half), BF16), ((tokens, half), BF16), ((half, half), BF16)],
+        flag,
         wanted[None, :],
         inputs,
     )
     theirs_x = lax.ppermute(theirs_x, "core", SWAP)
     halo, other_halo = call(
         resort_kernel,
-        [VMEM] * 2,
+        [SMEM] + [VMEM] * 2,
         [((WINDOW, half), BF16), ((WINDOW, half), BF16)],
+        flag,
         chosen,
         halo,
     )
     other_halo = lax.ppermute(other_halo, "core", [(0, 1)])
     halo, mine_xt, theirs_xt, halo_t = call(
         flip_kernel,
-        [SMEM] + [VMEM] * 4,
+        [SMEM] + [VMEM] * 3 + [FETCH],
         [
             ((WINDOW, half), BF16),
             ((half, tokens), BF16),
@@ -294,12 +330,13 @@
     seg_padded = jnp.concatenate([jnp.full((WINDOW,), -1, jnp.int32), segments], axis=0)
     query_seg = lax.dynamic_slice_in_dim(seg_padded, device * tokens + WINDOW, tokens, 0)
     key_seg = lax.dynamic_slice_in_dim(seg_padded, device * tokens, tokens + WINDOW, 0)
-    (bias,) = call(
+    bias, upstream = call(
         mask_kernel,
-        [VMEM] * 2,
-        [((tokens // TILE, span, heads * TILE), F32)],
+        [VMEM] * 2 + [FETCH],
+        [((tokens // TILE, span, heads * TILE), F32), (upstream.shape, BF16)],
         query_seg[None, :],
         key_seg[:, None],
+        upstream,
     )
     sink_row = jnp.repeat(sinks, TILE)[None, :]
 

time: 121 us -> 126 us (1.041)
  the two profiles are of different devices: /device:TPU:9 before, /device:TPU:1 now
where the time goes in v6:
time: 126 us; the launch traced here: 125 us
  starting transfers between devices  75.8 us (60%)
  blocking collectives  20.4 us (16%)
  waiting for transfers between devices  13.8 us (11%)
  Pallas kernels  9.54 us (8%)
  local copies, waits for them, and re-layouts  2.76 us (2%)
  other arithmetic  1.66 us (1%)
    all_to_all x3, starting transfers between devices, exchange(): lax.all_to_all(value, DP, split_axis=0, concat_axis=0, tiled=True, axis_i...  34.7 us
    all_to_all x1, blocking collectives, exchange(): lax.all_to_all(value, DP, split_axis=0, concat_axis=0, tiled=True, axis_i...  20.4 us
    ppermute x3, starting transfers between devices, body(): lax.ppermute(blocks[s], 'x', [(i, (i + s) % across) for i in range(across)])  10.5 us
    pallas_call x9, Pallas kernels, call(): pl.pallas_call(kernel, in_specs=specs, out_specs=[VMEM] * len(shapes), ou...  8.87 us
    ppermute x1, starting transfers between devices, body(): got = lax.ppermute(send, 'core', SWAP)  8.25 us
    ppermute x2, starting transfers between devices, body(): lax.ppermute(sums[s], 'zl', [(i, (i + s) % deep) for i in range(deep)])  7.49 us
    ppermute x1, starting transfers between devices, body(): lax.ppermute(inputs[tokens - WINDOW:], DP, [(i - 1, i) for i in range(2,...  6.07 us
    ppermute x1, waiting for transfers between devices, body(): lax.ppermute(pack[tokens - WINDOW:, columns:], DP, [(i, i - 1) for i in r...  5.95 us
  transfers between devices with their start and end apart: 15, of which 7 were waited for; matrix products, arithmetic and copies ran while one was open for 2% of the time, Pallas kernels for 4%

profile of v6, /device:TPU:1, one launch (start us, length us, event | category | flops | bytes accessed | tf_op | source)
XLA Modules:
  0.0 124.9 jit_solution(17700757973543068339)
XLA Ops:
  0.6 0.0 copy-start
  0.6 0.8 pad_maximum_fusion
  1.4 20.4 %all_to_all.20 = bf16[4,24,384]{2,1,0:T(8,128)(2,1)S(1)} all-to-all(bf16[4,24,384]{2,1,0:T(8,128)(2,1)S(1)} %broadcast_in_dim.34), channel_id=1, replica_groups={{0,24,48,72},{60,84,12,36},{96,120,144,168},{156,180,108,132},{192,216,..., dimensions={0} | all-to-all | bytes 147456 | tf_op jit(solution)/shard_map/all_to_all | solution.py:36
  21.8 0.9 broadcast_in_dim.36
  22.7 9.0 %all-to-all-start.1 = ((bf16[8,96,384]{2,1,0:T(8,128)(2,1)}), bf16[8,96,384]{2,1,0:T(8,128)(2,1)S(1)}, u32[]{:S(2)}, u32[]{:S(2)}) async-start(bf16[8,96,384]{2,1,0:T(8,128)(2,1)} %broadcast_in_dim.36), calls=%async_computation.1 | async-start | bytes 1179648 | tf_op jit(solution)/shard_map/all_to_all | solution.py:36
  31.7 0.0 copy-done
  31.8 6.1 %collective-permute-start.1 = (bf16[128,1536]{1,0:T(8,128)(2,1)S(1)}, bf16[128,1536]{1,0:T(8,128)(2,1)S(1)}, u32[]{:S(2)}, u32[]{:S(2)}) collective-permute-start(bf16[128,1536]{1,0:T(8,128)(2,1)S(1)} %slice.21), channel_id=1, source_target_pairs={{12,24},{36,48},{60,72},{84,96},{108,120},{132,144},{156,168},{180... | collective-permute-start | bytes 1179656 | tf_op jit(solution)/shard_map/ppermute | solution.py:293
  37.8 0.1 fusion.2.wanted_ref
  37.9 0.0 copy-start.3
  37.9 0.0 copy-start.1
  38.0 1.7 %shard_map.93 = (bf16[192,768]{1,0:T(8,128)(2,1)S(1)}, bf16[192,768]{1,0:T(8,128)(2,1)}, bf16[768,768]{1,0:T(8,128)(2,1)S(1)}) custom-call(s32[1]{0:T(128)} %bitcast.core_ref, s32[1,768]{1,0:T(1,128)S(1)} %fusion.2.wanted_ref, bf16[192,1536]{1,0:T(8,128)(2,1)S(1)} %copy-done), custom_call_target="tpu_custom_call" | custom-call | tf_op jit(solution)/shard_map/pallas_call | solution.py:252
  39.7 0.0 copy-start.2
  39.7 2.0 %collective-permute-start = (bf16[192,768]{1,0:T(8,128)(2,1)}, bf16[192,768]{1,0:T(8,128)(2,1)S(1)}, u32[]{:S(2)}, u32[]{:S(2)}) collective-permute-start(bf16[192,768]{1,0:T(8,128)(2,1)} %get-tuple-element.32), channel_id=1, source_target_pairs={{0,12},{12,0},{1,13},{13,1},{2,14},{14,2},{3,15},{15,3},{4,16},{16... | collective-permute-start | bytes 884744 | tf_op jit(solution)/shard_map/ppermute | solution.py:304
  41.8 0.8 collective-permute-done.1.x_ref
  42.6 1.5 %shard_map.94 = (bf16[128,768]{1,0:T(8,128)(2,1)S(1)}, bf16[128,768]{1,0:T(8,128)(2,1)}) custom-call(s32[1]{0:T(128)} %bitcast.core_ref, bf16[768,768]{1,0:T(8,128)(2,1)S(1)} %get-tuple-element.33.chosen_ref, bf16[128,1536]{1,0:T(8,128)(2,1)S(1)} %collective-permute-done.1.x_ref), custom_call_target="tpu_custom_call" | custom-call | tf_op jit(solution)/shard_map/pallas_call | solution.py:252
  44.1 1.3 %collective-permute-start.2 = (bf16[128,768]{1,0:T(8,128)(2,1)}, bf16[128,768]{1,0:T(8,128)(2,1)S(1)}, u32[]{:S(2)}, u32[]{:S(2)}) collective-permute-start(bf16[128,768]{1,0:T(8,128)(2,1)} %get-tuple-element.35), channel_id=1, source_target_pairs={{0,12},{1,13},{2,14},{3,15},{4,16},{5,17},{6,18},{7,19},{8,20},{9,... | collective-permute-start | bytes 589832 | tf_op jit(solution)/shard_map/ppermute | solution.py:313
  45.4 0.8 pad_dynamic-slice_fusion
  46.2 0.1 broadcast_in_dim.40.key_ref
  46.3 0.0 copy-done.3
  46.3 0.1 broadcast_in_dim.39
  46.4 0.1 broadcast_in_dim_reshape.3.sinks_ref
  46.4 0.0 copy-done.2
  46.4 0.1 pad_dynamic-slice_fusion.1
  46.5 0.0 copy-done.1
  46.5 0.4 shard_map.96
  46.9 0.0 collective-permute-done.theirs_ref
  46.9 0.7 collective-permute-done.2.other_ref
  47.6 0.3 shard_map.95
  48.0 0.0 all-to-all-done.1
  48.0 0.4 shard_map.97
  48.4 8.3 %collective-permute-start.3 = (f32[192,512]{1,0:T(8,128)S(1)}, f32[192,512]{1,0:T(8,128)S(1)}, u32[]{:S(2)}, u32[]{:S(2)}) collective-permute-start(f32[192,512]{1,0:T(8,128)S(1)} %get-tuple-element.43), channel_id=1, source_target_pairs={{0,12},{12,0},{1,13},{13,1},{2,14},{14,2},{3,15},{15,3},{4,16},{16... | collective-permute-start | bytes 1179656 | tf_op jit(solution)/shard_map/ppermute | solution.py:356
  56.7 1.3 %collective-permute-done.3.got_ref = f32[192,512]{1,0:T(8,128)S(1)} collective-permute-done((f32[192,512]{1,0:T(8,128)S(1)}, f32[192,512]{1,0:T(8,128)S(1)}, u32[]{:S(2)}, u32[]{:S(2)}) %collective-permute-start.3) | collective-permute-done | bytes 393248 | tf_op jit(solution)/shard_map/ppermute | solution.py:356
  58.0 1.7 %shard_map.98 = (bf16[192,256]{1,0:T(8,128)(2,1)S(1)}, bf16[192,512]{1,0:T(8,128)(2,1)S(1)}) custom-call(bf16[192,768]{1,0:T(8,128)(2,1)S(1)} %get-tuple-element.31.mine_ref, bf16[768,384]{1,0:T(8,128)(2,1)S(1)} %bitcast.19, f32[192,512]{1,0:T(8,128)S(1)} %collective-permute-done.3.got_ref, f32[128,128]{1,0:T(8,128)S(1)} %get-tuple-element.44.keep_ref, ...), custom_call_target="tpu_custom_call" | custom-call | tf_op jit(solution)/shard_map/pallas_call | solution.py:252
  59.7 2.3 %collective-permute-start.4 = (bf16[192,512]{1,0:T(8,128)(2,1)S(1)}, bf16[192,512]{1,0:T(8,128)(2,1)S(1)}, u32[]{:S(2)}, u32[]{:S(2)}) collective-permute-start(bf16[192,512]{1,0:T(8,128)(2,1)S(1)} %get-tuple-element.52.pack_ref), channel_id=1, source_target_pairs={{0,12},{12,0},{1,13},{13,1},{2,14},{14,2},{3,15},{15,3},{4,16},{16... | collective-permute-start | bytes 589832 | tf_op jit(solution)/shard_map/ppermute | solution.py:371
  61.9 1.1 collective-permute-done.4.got_ref
  63.0 1.4 %shard_map.99 = (bf16[768,384]{1,0:T(8,128)(2,1)}, bf16[192,128]{1,0:T(8,128)(2,1)S(1)}) custom-call(s32[1]{0:T(128)} %bitcast.core_ref, bf16[768,192]{1,0:T(8,128)(2,1)S(1)} %get-tuple-element.49.mine_ref, bf16[768,192]{1,0:T(8,128)(2,1)S(1)} %get-tuple-element.50.theirs_ref, bf16[768,128]{1,0:T(8,128)(2,1)S(1)} %get-tuple-element.51.halo_ref, ...), custom_call_target="tpu_custom_call" | custom-call | tf_op jit(solution)/shard_map/pallas_call | solution.py:252
  64.4 16.6 %all-to-all-start.2 = ((bf16[8,96,384]{2,1,0:T(8,128)(2,1)}), bf16[8,96,384]{2,1,0:T(8,128)(2,1)S(1)}, u32[]{:S(2)}, u32[]{:S(2)}) async-start(bf16[8,96,384]{2,1,0:T(8,128)(2,1)} %bitcast.4), calls=%async_computation.2 | async-start | bytes 1179648 | tf_op jit(solution)/shard_map/all_to_all | solution.py:36
  81.1 1.9 %collective-permute-start.6 = (bf16[768,384]{1,0:T(8,128)(2,1)S(1)}, bf16[768,384]{1,0:T(8,128)(2,1)S(1)}, u32[]{:S(2)}, u32[]{:S(2)}) collective-permute-start(bf16[768,384]{1,0:T(8,128)(2,1)S(1)} %bitcast.20), channel_id=1, source_target_pairs={{0,12},{12,0},{1,13},{13,1},{2,14},{14,2},{3,15},{15,3},{4,16},{16... | collective-permute-start | bytes 1769480 | tf_op jit(solution)/shard_map/ppermute | solution.py:357
  83.0 1.3 %collective-permute-start.5 = (bf16[128,128]{1,0:T(8,128)(2,1)S(1)}, bf16[128,128]{1,0:T(8,128)(2,1)S(1)}, u32[]{:S(2)}, u32[]{:S(2)}) collective-permute-start(bf16[128,128]{1,0:T(8,128)(2,1)S(1)} %slice.22), channel_id=1, source_target_pairs={{24,12},{48,36},{72,60},{96,84},{120,108},{144,132},{168,156},{192... | collective-permute-start | bytes 98312 | tf_op jit(solution)/shard_map/ppermute | solution.py:372
  84.3 0.1 pad_add_fusion.place_ref
  84.4 5.9 %collective-permute-done.5.late_ref = bf16[128,128]{1,0:T(8,128)(2,1)S(1)} collective-permute-done((bf16[128,128]{1,0:T(8,128)(2,1)S(1)}, bf16[128,128]{1,0:T(8,128)(2,1)S(1)}, u32[]{:S(2)}, u32[]{:S(2)}) %collective-permute-start.5) | collective-permute-done | bytes 32800 | tf_op jit(solution)/shard_map/ppermute | solution.py:372
  90.3 0.0 collective-permute-done.6.other_ref
  90.3 1.3 %shard_map.100.blocks_ref = bf16[4,192,384]{2,1,0:T(8,128)(2,1)S(1)} custom-call(s32[2]{0:T(128)S(1)} %pad_add_fusion.place_ref, bf16[192,512]{1,0:T(8,128)(2,1)S(1)} %get-tuple-element.52.pack_ref, bf16[192,128]{1,0:T(8,128)(2,1)S(1)} %get-tuple-element.54.own_ref, bf16[128,128]{1,0:T(8,128)(2,1)S(1)} %collective-permute-done.5.late_ref, ...), custom_call_target="tpu_custom_call" | custom-call | tf_op jit(solution)/shard_map/pallas_call | solution.py:252
  91.7 3.1 %collective-permute-start.7 = (bf16[192,384]{1,0:T(8,128)(2,1)S(1)}, bf16[192,384]{1,0:T(8,128)(2,1)S(1)}, u32[]{:S(2)}, u32[]{:S(2)}) collective-permute-start(bf16[192,384]{1,0:T(8,128)(2,1)S(1)} %get-tuple-element.60), channel_id=1, source_target_pairs={{0,1},{1,2},{2,3},{3,0},{4,5},{5,6},{6,7},{7,4},{8,9},{9,10},{10,1... | collective-permute-start | bytes 442376 | tf_op jit(solution)/shard_map/ppermute | solution.py:403
  94.9 4.4 %collective-permute-start.8 = (bf16[192,384]{1,0:T(8,128)(2,1)S(1)}, bf16[192,384]{1,0:T(8,128)(2,1)S(1)}, u32[]{:S(2)}, u32[]{:S(2)}) collective-permute-start(bf16[192,384]{1,0:T(8,128)(2,1)S(1)} %get-tuple-element.59), channel_id=1, source_target_pairs={{0,2},{1,3},{2,0},{3,1},{4,6},{5,7},{6,4},{7,5},{8,10},{9,11},{10,... | collective-permute-start | bytes 442376 | tf_op jit(solution)/shard_map/ppermute | solution.py:403
  99.2 3.1 %collective-permute-start.9 = (bf16[192,384]{1,0:T(8,128)(2,1)S(1)}, bf16[192,384]{1,0:T(8,128)(2,1)S(1)}, u32[]{:S(2)}, u32[]{:S(2)}) collective-permute-start(bf16[192,384]{1,0:T(8,128)(2,1)S(1)} %get-tuple-element.58), channel_id=1, source_target_pairs={{0,3},{1,0},{2,1},{3,2},{4,7},{5,4},{6,5},{7,6},{8,11},{9,8},{10,9... | collective-permute-start | bytes 442376 | tf_op jit(solution)/shard_map/ppermute | solution.py:403
  102.3 0.0 collective-permute-done.7.refs_0_
  102.3 0.0 collective-permute-done.8.refs_1_
  102.3 2.8 %collective-permute-done.9.refs_2_ = bf16[192,384]{1,0:T(8,128)(2,1)S(1)} collective-permute-done((bf16[192,384]{1,0:T(8,128)(2,1)S(1)}, bf16[192,384]{1,0:T(8,128)(2,1)S(1)}, u32[]{:S(2)}, u32[]{:S(2)}) %collective-permute-start.9) | collective-permute-done | bytes 147488 | tf_op jit(solution)/shard_map/ppermute | solution.py:403
  105.1 0.1 shard_map.101.sums_ref
  105.2 0.0 all-to-all-done.2
  105.2 0.7 reduce_sum.12
  105.9 9.0 %all-to-all-start.3 = ((bf16[4,24,384]{2,1,0:T(8,128)(2,1)}), bf16[4,24,384]{2,1,0:T(8,128)(2,1)S(1)}, u32[]{:S(2)}, u32[]{:S(2)}) async-start(bf16[4,24,384]{2,1,0:T(8,128)(2,1)} %bitcast.5), calls=%async_computation.3 | async-start | bytes 147456 | tf_op jit(solution)/shard_map/all_to_all | solution.py:36
  115.0 3.5 %collective-permute-start.10 = (bf16[192,128]{1,0:T(8,128)(2,1)S(1)}, bf16[192,128]{1,0:T(8,128)(2,1)S(1)}, u32[]{:S(2)}, u32[]{:S(2)}) collective-permute-start(bf16[192,128]{1,0:T(8,128)(2,1)S(1)} %get-tuple-element.62), channel_id=1, source_target_pairs={{0,4},{4,8},{8,0},{1,5},{5,9},{9,1},{2,6},{6,10},{10,2},{3,7},{7,1... | collective-permute-start | bytes 147464 | tf_op jit(solution)/shard_map/ppermute | solution.py:415
  118.4 4.0 %collective-permute-start.11 = (bf16[192,128]{1,0:T(8,128)(2,1)S(1)}, bf16[192,128]{1,0:T(8,128)(2,1)S(1)}, u32[]{:S(2)}, u32[]{:S(2)}) collective-permute-start(bf16[192,128]{1,0:T(8,128)(2,1)S(1)} %get-tuple-element.61), channel_id=1, source_target_pairs={{0,8},{4,0},{8,4},{1,9},{5,1},{9,5},{2,10},{6,2},{10,6},{3,11},{7,... | collective-permute-start | bytes 147464 | tf_op jit(solution)/shard_map/ppermute | solution.py:415
  122.5 0.6 copy.11
  123.1 0.0 collective-permute-done.10.refs_0_
  123.1 1.1 collective-permute-done.11.refs_1_
  124.2 0.0 all-to-all-done.3.grads_ref
  124.2 0.7 shard_map.102
  (5 shorter events, 0.1 us)
Async XLA Ops:
  0.6 31.1 %copy-start = (bf16[192,1536]{1,0:T(8,128)(2,1)S(1)}, bf16[192,1536]{1,0:T(8,128)(2,1)}, u32[]{:S(2)}) copy-start(bf16[192,1536]{1,0:T(8,128)(2,1)} %x_ref.1) | copy-start | bytes 1769476
  22.7 25.2 %all-to-all-start.1 = ((bf16[8,96,384]{2,1,0:T(8,128)(2,1)}), bf16[8,96,384]{2,1,0:T(8,128)(2,1)S(1)}, u32[]{:S(2)}, u32[]{:S(2)}) async-start(bf16[8,96,384]{2,1,0:T(8,128)(2,1)} %broadcast_in_dim.36), calls=%async_computation.1 | async-start | bytes 1179648 | tf_op jit(solution)/shard_map/all_to_all | solution.py:36
  31.8 10.8 %collective-permute-start.1 = (bf16[128,1536]{1,0:T(8,128)(2,1)S(1)}, bf16[128,1536]{1,0:T(8,128)(2,1)S(1)}, u32[]{:S(2)}, u32[]{:S(2)}) collective-permute-start(bf16[128,1536]{1,0:T(8,128)(2,1)S(1)} %slice.21), channel_id=1, source_target_pairs={{12,24},{36,48},{60,72},{84,96},{108,120},{132,144},{156,168},{180... | collective-permute-start | bytes 1179656 | tf_op jit(solution)/shard_map/ppermute | solution.py:293
  37.9 8.3 %copy-start.3 = (f32[4]{0:T(128)S(1)}, f32[4]{0:T(128)}, u32[]{:S(2)}) copy-start(f32[4]{0:T(128)} %param.9) | copy-start | bytes 52
  37.9 8.6 %copy-start.1 = (bf16[192,256]{1,0:T(8,128)(2,1)S(1)}, bf16[192,256]{1,0:T(8,128)(2,1)}, u32[]{:S(2)}) copy-start(bf16[192,256]{1,0:T(8,128)(2,1)} %up_ref.1) | copy-start | bytes 294916
  39.7 6.7 %copy-start.2 = (s32[12288]{0:T(1024)S(1)}, s32[12288]{0:T(1024)}, u32[]{:S(2)}) copy-start(s32[12288]{0:T(1024)} %param.10) | copy-start | bytes 147460
  39.7 7.2 %collective-permute-start = (bf16[192,768]{1,0:T(8,128)(2,1)}, bf16[192,768]{1,0:T(8,128)(2,1)S(1)}, u32[]{:S(2)}, u32[]{:S(2)}) collective-permute-start(bf16[192,768]{1,0:T(8,128)(2,1)} %get-tuple-element.32), channel_id=1, source_target_pairs={{0,12},{12,0},{1,13},{13,1},{2,14},{14,2},{3,15},{15,3},{4,16},{16... | collective-permute-start | bytes 884744 | tf_op jit(solution)/shard_map/ppermute | solution.py:304
  44.1 3.5 %collective-permute-start.2 = (bf16[128,768]{1,0:T(8,128)(2,1)}, bf16[128,768]{1,0:T(8,128)(2,1)S(1)}, u32[]{:S(2)}, u32[]{:S(2)}) collective-permute-start(bf16[128,768]{1,0:T(8,128)(2,1)} %get-tuple-element.35), channel_id=1, source_target_pairs={{0,12},{1,13},{2,14},{3,15},{4,16},{5,17},{6,18},{7,19},{8,20},{9,... | collective-permute-start | bytes 589832 | tf_op jit(solution)/shard_map/ppermute | solution.py:313
  48.4 9.6 %collective-permute-start.3 = (f32[192,512]{1,0:T(8,128)S(1)}, f32[192,512]{1,0:T(8,128)S(1)}, u32[]{:S(2)}, u32[]{:S(2)}) collective-permute-start(f32[192,512]{1,0:T(8,128)S(1)} %get-tuple-element.43), channel_id=1, source_target_pairs={{0,12},{12,0},{1,13},{13,1},{2,14},{14,2},{3,15},{15,3},{4,16},{16... | collective-permute-start | bytes 1179656 | tf_op jit(solution)/shard_map/ppermute | solution.py:356
  59.7 3.3 %collective-permute-start.4 = (bf16[192,512]{1,0:T(8,128)(2,1)S(1)}, bf16[192,512]{1,0:T(8,128)(2,1)S(1)}, u32[]{:S(2)}, u32[]{:S(2)}) collective-permute-start(bf16[192,512]{1,0:T(8,128)(2,1)S(1)} %get-tuple-element.52.pack_ref), channel_id=1, source_target_pairs={{0,12},{12,0},{1,13},{13,1},{2,14},{14,2},{3,15},{15,3},{4,16},{16... | collective-permute-start | bytes 589832 | tf_op jit(solution)/shard_map/ppermute | solution.py:371
  64.4 40.8 %all-to-all-start.2 = ((bf16[8,96,384]{2,1,0:T(8,128)(2,1)}), bf16[8,96,384]{2,1,0:T(8,128)(2,1)S(1)}, u32[]{:S(2)}, u32[]{:S(2)}) async-start(bf16[8,96,384]{2,1,0:T(8,128)(2,1)} %bitcast.4), calls=%async_computation.2 | async-start | bytes 1179648 | tf_op jit(solution)/shard_map/all_to_all | solution.py:36
  81.1 9.3 %collective-permute-start.6 = (bf16[768,384]{1,0:T(8,128)(2,1)S(1)}, bf16[768,384]{1,0:T(8,128)(2,1)S(1)}, u32[]{:S(2)}, u32[]{:S(2)}) collective-permute-start(bf16[768,384]{1,0:T(8,128)(2,1)S(1)} %bitcast.20), channel_id=1, source_target_pairs={{0,12},{12,0},{1,13},{13,1},{2,14},{14,2},{3,15},{15,3},{4,16},{16... | collective-permute-start | bytes 1769480 | tf_op jit(solution)/shard_map/ppermute | solution.py:357
  83.0 7.3 %collective-permute-start.5 = (bf16[128,128]{1,0:T(8,128)(2,1)S(1)}, bf16[128,128]{1,0:T(8,128)(2,1)S(1)}, u32[]{:S(2)}, u32[]{:S(2)}) collective-permute-start(bf16[128,128]{1,0:T(8,128)(2,1)S(1)} %slice.22), channel_id=1, source_target_pairs={{24,12},{48,36},{72,60},{96,84},{120,108},{144,132},{168,156},{192... | collective-permute-start | bytes 98312 | tf_op jit(solution)/shard_map/ppermute | solution.py:372
  91.7 10.6 %collective-permute-start.7 = (bf16[192,384]{1,0:T(8,128)(2,1)S(1)}, bf16[192,384]{1,0:T(8,128)(2,1)S(1)}, u32[]{:S(2)}, u32[]{:S(2)}) collective-permute-start(bf16[192,384]{1,0:T(8,128)(2,1)S(1)} %get-tuple-element.60), channel_id=1, source_target_pairs={{0,1},{1,2},{2,3},{3,0},{4,5},{5,6},{6,7},{7,4},{8,9},{9,10},{10,1... | collective-permute-start | bytes 442376 | tf_op jit(solution)/shard_map/ppermute | solution.py:403
  94.9 7.5 %collective-permute-start.8 = (bf16[192,384]{1,0:T(8,128)(2,1)S(1)}, bf16[192,384]{1,0:T(8,128)(2,1)S(1)}, u32[]{:S(2)}, u32[]{:S(2)}) collective-permute-start(bf16[192,384]{1,0:T(8,128)(2,1)S(1)} %get-tuple-element.59), channel_id=1, source_target_pairs={{0,2},{1,3},{2,0},{3,1},{4,6},{5,7},{6,4},{7,5},{8,10},{9,11},{10,... | collective-permute-start | bytes 442376 | tf_op jit(solution)/shard_map/ppermute | solution.py:403
  99.2 5.9 %collective-permute-start.9 = (bf16[192,384]{1,0:T(8,128)(2,1)S(1)}, bf16[192,384]{1,0:T(8,128)(2,1)S(1)}, u32[]{:S(2)}, u32[]{:S(2)}) collective-permute-start(bf16[192,384]{1,0:T(8,128)(2,1)S(1)} %get-tuple-element.58), channel_id=1, source_target_pairs={{0,3},{1,0},{2,1},{3,2},{4,7},{5,4},{6,5},{7,6},{8,11},{9,8},{10,9... | collective-permute-start | bytes 442376 | tf_op jit(solution)/shard_map/ppermute | solution.py:403
  105.9 18.3 %all-to-all-start.3 = ((bf16[4,24,384]{2,1,0:T(8,128)(2,1)}), bf16[4,24,384]{2,1,0:T(8,128)(2,1)S(1)}, u32[]{:S(2)}, u32[]{:S(2)}) async-start(bf16[4,24,384]{2,1,0:T(8,128)(2,1)} %bitcast.5), calls=%async_computation.3 | async-start | bytes 147456 | tf_op jit(solution)/shard_map/all_to_all | solution.py:36
  115.0 8.2 %collective-permute-start.10 = (bf16[192,128]{1,0:T(8,128)(2,1)S(1)}, bf16[192,128]{1,0:T(8,128)(2,1)S(1)}, u32[]{:S(2)}, u32[]{:S(2)}) collective-permute-start(bf16[192,128]{1,0:T(8,128)(2,1)S(1)} %get-tuple-element.62), channel_id=1, source_target_pairs={{0,4},{4,8},{8,0},{1,5},{5,9},{9,1},{2,6},{6,10},{10,2},{3,7},{7,1... | collective-permute-start | bytes 147464 | tf_op jit(solution)/shard_map/ppermute | solution.py:415
  118.4 5.8 %collective-permute-start.11 = (bf16[192,128]{1,0:T(8,128)(2,1)S(1)}, bf16[192,128]{1,0:T(8,128)(2,1)S(1)}, u32[]{:S(2)}, u32[]{:S(2)}) collective-permute-start(bf16[192,128]{1,0:T(8,128)(2,1)S(1)} %get-tuple-element.61), channel_id=1, source_target_pairs={{0,8},{4,0},{8,4},{1,9},{5,1},{9,5},{2,10},{6,2},{10,6},{3,11},{7,... | collective-permute-start | bytes 147464 | tf_op jit(solution)/shard_map/ppermute | solution.py:415
